TPU v7x, 32 devices: a whole 2x2x4 slice. The times are simulated.
32 devices in a mesh: dp: 8 (over z, y), head: 4 (over x, core).
Axes of the slice: x: 2, y: 2, z: 4, core: 2. Of those that a mesh axis runs over, the one named last changes fastest.
Arguments:
- layer_input: bfloat16 [2, 16384, 768], P(None, ('dp', 'head')), may hold values from -6 to 6
- output_grad: bfloat16 [2, 16384, 768], P(None, ('dp', 'head')), may hold values from -6 to 6
- lengths: int32 [2, 32], P(None, 'dp'), may hold values from 64 to 512, as said below
- w_qkv: bfloat16 [3, 768, 768], P(None, 'dp', 'head'), may hold values from -0.21875 to 0.21875
- w_out: bfloat16 [768, 768], P('head', 'dp'), may hold values from -4 to 4
- w_up: bfloat16 [768, 3072], P('dp', 'head'), may hold values from -0.21875 to 0.21875
- w_down: bfloat16 [3072, 768], P('head', 'dp'), may hold values from -0.109375 to 0.109375
- norm_gains: float32 [2, 768], replicated, may hold values from 0.5 to 1.5
- norm_biases: float32 [2, 768], replicated, may hold values from -3 to 3
- mask_logits: float32 [12, 512, 512], P('head', 'dp'), may hold values from -9 to 9
- mask_noise: float32 [12, 512, 512], P('head', 'dp'), may hold values from -6 to 6
Outputs:
- layer_output: bfloat16 [2, 16384, 768], P(None, ('dp', 'head'))
- input_grad: float32 [2, 16384, 768], P(None, ('dp', 'head'))
- w_qkv_grad: float32 [3, 768, 768], P(None, 'dp', 'head')
- w_out_grad: float32 [768, 768], P('head', 'dp')
- w_up_grad: float32 [768, 3072], P('dp', 'head')
- w_down_grad: float32 [3072, 768], P('head', 'dp')
- gains_grad: float32 [2, 768], replicated
- biases_grad: float32 [2, 768], replicated
- logits_grad: float32 [12, 512, 512], P('head', 'dp')
Inputs may be any that keep to these rules, and one draw needn't show every extreme that they name: `lengths`: each sequence's number of valid tokens; in each micro-batch the first sequence of each index of dp has 512.
All inputs are finite; a program needn't handle non-finite values.
Results may differ from a plain program's by a relative error of at most 0.013.
The roundings to bfloat16 on the way count: a program that leaves them out, or rounds other values in their place, can miss the bound.
Values may be sent and summed in bfloat16 or wider, within the bound.
No kernel may reach another device: no remote copies, remote signals or barrier semaphores. Data moves between devices by JAX's collectives and lax.ppermute only.
A program may use at most 192 MiB of HBM per device.

v0:
```python
import functools, math
import jax, jax.numpy as jnp
from jax import lax
from jax.experimental import pallas as pl
from jax.experimental.pallas import tpu as pltpu
from jax.sharding import PartitionSpec as P

HEAD_DIM = 64
EPS = 1e-05
F32 = jnp.float32
BF16 = jnp.bfloat16
GP = jnp.float32
SCALE = 1.0 / math.sqrt(HEAD_DIM)
LOG2E = math.log2(math.e)
NEG = -1e30
INV_SQRT2 = 1.0 / math.sqrt(2.0)
INV_SQRT2PI = 1.0 / math.sqrt(2.0 * math.pi)


def dot_nn(a, b):
    return lax.dot_general(a, b, (((1,), (0,)), ((), ())), preferred_element_type=F32)


def dot_nt(a, b):
    return lax.dot_general(a, b, (((1,), (1,)), ((), ())), preferred_element_type=F32)


def dot_tn(a, b):
    return lax.dot_general(a, b, (((0,), (0,)), ((), ())), preferred_element_type=F32)


def piece(ref, bits, d, flip):
    y = bits[0] ^ (d & 1)
    z1 = bits[1] ^ ((d >> 1) & 1)
    z2 = bits[2] ^ ((d >> 2) & 1)
    if flip:
        return ref.at[y, 0, z1, z2]
    return ref.at[0, y, z1, z2]


def assemble(dst, ref, bits, flip, cols=None):
    rows = ref.shape[-2]
    cols = pl.ds(0, ref.shape[-1]) if cols is None else cols
    for d in range(8):
        dst[pl.ds(d * rows, rows), cols] = piece(ref, bits, d, flip)[...]


def scatter(ref, src, bits, flip):
    rows = ref.shape[-2]
    for d in range(8):
        piece(ref, bits, d, flip)[...] = src[pl.ds(d * rows, rows), :]


def own(bits, y, z1, z2):
    return (bits[0] ^ y) + 2 * (bits[1] ^ z1) + 4 * (bits[2] ^ z2)


RELATIVE = [(y, z1, z2) for y in range(2) for z1 in range(2) for z2 in range(2)]


def spec_a(tail, pick):
    zeros = (0,) * len(tail)
    return pl.BlockSpec((1, 2, 2, 2) + tail, lambda k, *_: (pick(k), 0, 0, 0) + zeros)


def spec_b(tail, pick):
    zeros = (0,) * len(tail)
    return pl.BlockSpec((2, 1, 2, 2) + tail, lambda k, *_: (0, pick(k), 0, 0) + zeros)


def whole(shape):
    zeros = (0,) * len(shape)
    return pl.BlockSpec(shape, lambda *_: zeros)


def low_pick(k):
    return jnp.minimum(k, 1)


def high_pick(k):
    return jnp.maximum(k - 2, 0)


def norm_stats(z):
    mean = jnp.mean(z, axis=1, keepdims=True)
    centered = z - mean
    inverse = lax.rsqrt(jnp.mean(centered * centered, axis=1, keepdims=True) + EPS)
    return centered * inverse, inverse


def norm_back(du, unit, inverse):
    return inverse * (
        du
        - jnp.mean(du, axis=1, keepdims=True)
        - unit * jnp.mean(du * unit, axis=1, keepdims=True)
    )


def gelu_pair(up):
    cdf = 0.5 + 0.5 * lax.erf(up * INV_SQRT2)
    pdf = INV_SQRT2PI * jnp.exp(-0.5 * (up * up))
    return up * cdf, cdf + up * pdf


SHARE = 200


def cost(flops, moved):
    return pl.CostEstimate(flops=flops // SHARE, bytes_accessed=moved // SHARE, transcendentals=0)


def params(mib=56, n=1):
    return pltpu.CompilerParams(
        dimension_semantics=("arbitrary",) * n, vmem_limit_bytes=mib * 1024 * 1024
    )


def load_pair(k, bits, wu, wd, ua0, ua1, db0, db1):
    @pl.when(k < 2)
    def _():
        assemble(wu, ua0, bits, False)
        assemble(wd, db0, bits, True)

    @pl.when(k >= 2)
    def _():
        assemble(wu, ua1, bits, False)
        assemble(wd, db1, bits, True)


def ffn_units(chunk, hid, wu, wd, act_o, gp_o, acc):
    rows = hid.shape[0]
    ats = [pl.ds(r * chunk, chunk) for r in range(rows // chunk)]
    ahead = dot_nn(hid[ats[0], :], wu[...])
    for r, at in enumerate(ats):
        act, gp = gelu_pair(ahead)
        if r + 1 < len(ats):
            ahead = dot_nn(hid[ats[r + 1], :], wu[...])
        act = act.astype(BF16)
        act_o[0, at, :] = act
        gp_o[0, at, :] = gp.astype(gp_o.dtype)
        acc[at, :] += dot_nt(act, wd[...])


def ffn_part_kernel(chunk, bits, hid, ua0, ua1, db0, db1, act_o, gp_o, acc, wu, wd):
    k = pl.program_id(0)
    load_pair(k, bits, wu, wd, ua0, ua1, db0, db1)

    @pl.when(k == 0)
    def _():
        acc[...] = hid[...].astype(F32)

    ffn_units(chunk, hid, wu, wd, act_o, gp_o, acc)


def ffn_part(bits, hid, ua0, ua1, db0, db1, units, chunk=512):
    rows, width = hid.shape
    p, n = ua0.shape[-2:]
    sds = jax.ShapeDtypeStruct
    col = pl.BlockSpec((1, rows, n), lambda k, *_: (k, 0, 0))
    return pl.pallas_call(
        functools.partial(ffn_part_kernel, chunk),
        out_shape=(sds((4, rows, units), BF16), sds((4, rows, units), GP), sds((rows, width), F32)),
        grid_spec=pltpu.PrefetchScalarGridSpec(
            num_scalar_prefetch=1, grid=(4,),
            in_specs=[whole((rows, width)), spec_a((p, n), low_pick), spec_a((p, n), high_pick),
                      spec_b((p, n), low_pick), spec_b((p, n), high_pick)],
            out_specs=[col, col, whole((rows, width))],
            scratch_shapes=[pltpu.VMEM((width, n), BF16), pltpu.VMEM((width, n), BF16)],
        ),
        compiler_params=params(48),
        cost_estimate=cost(4 * rows * width * 4 * n, 16 * rows * width),
    )(bits, hid, ua0, ua1, db0, db1)


def ffn_rest_kernel(chunk, bits, lens, hid, ua0, ua1, db0, db1, part, gain, bias, dout, act_i, gp_i,
                    act_o, gp_o, out, dsec, dffn, dffnt, dgain, dbias, wu, wd, acc):
    k = pl.program_id(0)
    rows = hid.shape[0]
    load_pair(k, bits, wu, wd, ua0, ua1, db0, db1)

    @pl.when(k == 0)
    def _():
        acc[...] = part[...]

    ffn_units(chunk, hid, wu, wd, act_o, gp_o, acc)

    @pl.when(k == 3)
    def _():
        length = rows // lens.shape[0]
        small = 256
        g = gain[...]
        b = bias[...]
        dg = jnp.zeros_like(g)
        db = jnp.zeros_like(g)
        for r in range(rows // small):
            at = pl.ds(r * small, small)
            size = lens[r * small // length]
            pos = (r * small % length) + lax.broadcasted_iota(jnp.int32, (small, 1), 0)
            valid = pos < size
            unit, inverse = norm_stats(acc[at, :])
            out[at, :] = jnp.where(valid, unit * g + b, 0.0).astype(BF16)
            dy = jnp.where(valid, dout[at, :].astype(F32), 0.0)
            dg += jnp.sum(dy * unit, axis=0, keepdims=True)
            db += jnp.sum(dy, axis=0, keepdims=True)
            dz = norm_back(dy * g, unit, inverse)
            dsec[at, :] = dz
            low = dz.astype(BF16)
            dffn[at, :] = low
            dffnt[:, at] = low.T
        dgain[...] = dg
        dbias[...] = db


def ffn_rest(bits, lens, hid, ua0, ua1, db0, db1, part, gain, bias, dout, act, gp, chunk=512):
    rows, width = hid.shape
    p, n = ua0.shape[-2:]
    last = act.shape[2] // n - 1
    sds = jax.ShapeDtypeStruct
    full = whole((rows, width))
    line = whole((1, width))
    col = pl.BlockSpec((1, rows, n), lambda k, *_: (k, 0, last))
    anywhere = pl.BlockSpec(memory_space=pl.ANY)
    return pl.pallas_call(
        functools.partial(ffn_rest_kernel, chunk),
        out_shape=(sds(act.shape, act.dtype), sds(gp.shape, gp.dtype), sds((rows, width), BF16), sds((rows, width), F32),
                   sds((rows, width), BF16), sds((width, rows), BF16), sds((1, width), F32), sds((1, width), F32)),
        grid_spec=pltpu.PrefetchScalarGridSpec(
            num_scalar_prefetch=2, grid=(4,),
            in_specs=[full, spec_a((p, n), low_pick), spec_a((p, n), high_pick),
                      spec_b((p, n), low_pick), spec_b((p, n), high_pick), full, line, line, full, anywhere, anywhere],
            out_specs=[col, col, full, full, full, whole((width, rows)), line, line],
            scratch_shapes=[pltpu.VMEM((width, n), BF16), pltpu.VMEM((width, n), BF16), pltpu.VMEM((rows, width), F32)],
        ),
        input_output_aliases={11: 0, 12: 1},
        compiler_params=params(48),
        cost_estimate=cost(4 * rows * width * 4 * n, 20 * rows * width),
    )(bits, lens, hid, ua0, ua1, db0, db1, part, gain, bias, dout, act, gp)


def down_grad_kernel(bits, dt, act, keep, send):
    k = pl.program_id(0)
    grad = dot_nn(dt[...], act[0]).astype(BF16)
    rows = keep.shape[-2]

    def put(ref):
        for d in range(8):
            piece(ref, bits, d, True)[...] = grad[d * rows : (d + 1) * rows]

    @pl.when(k < 2)
    def _():
        put(keep)

    @pl.when(k >= 2)
    def _():
        put(send)


def down_grads(bits, dt, act):
    width, rows = dt.shape
    n = act.shape[2]
    p = width // 8
    sds = jax.ShapeDtypeStruct
    return pl.pallas_call(
        down_grad_kernel,
        out_shape=(sds((2, 2, 2, 2, p, n), BF16), sds((2, 2, 2, 2, p, n), BF16)),
        grid_spec=pltpu.PrefetchScalarGridSpec(
            num_scalar_prefetch=1, grid=(4,),
            in_specs=[whole((width, rows)), pl.BlockSpec((1, rows, n), lambda k, *_: (k, 0, 0))],
            out_specs=[spec_b((p, n), low_pick), spec_b((p, n), high_pick)],
        ),
        compiler_params=params(40),
        cost_estimate=cost(2 * rows * width * 4 * n, 14 * rows * width),
    )(bits, dt, act)


def ffn_bwd_kernel(chunk, last, bits, ht, dffn, uap, uaq, dbp, dbq, gp, *rest):
    if last:
        dsec, part, unit, inverse, gain, gu, dfirst, dattn, dattnt, dgain, dbias, wu, wd, dup_s, acc = rest
    else:
        gu, acc, wu, wd, dup_s = rest
    k = pl.program_id(0)
    rows, width = dffn.shape
    np = uap.shape[-1]
    left, right = pl.ds(0, np), pl.ds(np, uaq.shape[-1])

    assemble(wu, uap, bits, False, left)
    assemble(wu, uaq, bits, False, right)
    assemble(wd, dbp, bits, True, left)
    assemble(wd, dbq, bits, True, right)

    @pl.when(k == 0)
    def _():
        if last:
            acc[...] = part[...] + dsec[...]
        else:
            acc[...] = jnp.zeros_like(acc)

    ats = [pl.ds(r * chunk, chunk) for r in range(rows // chunk)]
    ahead = dot_nn(dffn[ats[0], :], wd[...])
    for r, at in enumerate(ats):
        dup = (ahead * gp[0, at, :].astype(F32)).astype(BF16)
        if r + 1 < len(ats):
            ahead = dot_nn(dffn[ats[r + 1], :], wd[...])
        dup_s[at, :] = dup
        acc[at, :] += dot_nt(dup, wu[...])

    grad = dot_nn(ht[...], dup_s[...]).astype(BF16)
    p = gu.shape[-2]
    for d in range(8):
        piece(gu, bits, d, False)[...] = grad[d * p : (d + 1) * p]

    if last:

        @pl.when(k == 1)
        def _():
            small = 256
            g = gain[...]
            dg = jnp.zeros_like(g)
            db = jnp.zeros_like(g)
            for r in range(rows // small):
                at = pl.ds(r * small, small)
                dh = acc[at, :]
                u = unit[at, :]
                dg += jnp.sum(dh * u, axis=0, keepdims=True)
                db += jnp.sum(dh, axis=0, keepdims=True)
                dz = norm_back(dh * g, u, inverse[at, :])
                dfirst[at, :] = dz
                low = dz.astype(BF16)
                dattn[at, :] = low
                dattnt[:, at] = low.T
            dgain[...] = dg
            dbias[...] = db


def ffn_backward(last, bits, ht, dffn, uap, uaq, dbp, dbq, gp, extra=(), chunk=512):
    rows, width = dffn.shape
    p, np = uap.shape[-2:]
    nq = uaq.shape[-1]
    n = np + nq
    sds = jax.ShapeDtypeStruct
    off = 0 if last else 2
    pick = lambda k: k
    full = whole((rows, width))
    line = whole((1, width))
    out_shape = [sds((2, 2, 2, 2, p, n), BF16)]
    out_specs = [spec_a((p, n), pick)]
    in_specs = [
        whole((width, rows)), full,
        spec_a((p, np), pick), spec_a((p, nq), pick), spec_b((p, np), pick), spec_b((p, nq), pick),
        pl.BlockSpec((1, rows, n), lambda k, *_: (k + off, 0, 0)),
    ]
    scratch = [pltpu.VMEM((width, n), BF16), pltpu.VMEM((width, n), BF16), pltpu.VMEM((rows, n), BF16)]
    if last:
        in_specs += [full] * 3 + [whole((rows, 1)), line]
        out_shape += [sds((rows, width), F32), sds((rows, width), BF16), sds((width, rows), BF16), sds((1, width), F32), sds((1, width), F32)]
        out_specs += [full, full, whole((width, rows)), line, line]
        scratch += [pltpu.VMEM((rows, width), F32)]
    else:
        out_shape += [sds((rows, width), F32)]
        out_specs += [full]
    return pl.pallas_call(
        functools.partial(ffn_bwd_kernel, chunk, last),
        out_shape=out_shape,
        grid_spec=pltpu.PrefetchScalarGridSpec(
            num_scalar_prefetch=1, grid=(2,), in_specs=in_specs, out_specs=out_specs, scratch_shapes=scratch,
        ),
        compiler_params=params(56),
        cost_estimate=cost(6 * rows * width * 2 * n, 30 * rows * width),
    )(bits, ht, dffn, uap, uaq, dbp, dbq, gp, *extra)


def key_bias(size, length):
    pos = lax.broadcasted_iota(jnp.int32, (1, length), 1)
    return jnp.where(pos < size, 0.0, NEG).astype(F32)


def gate_rows(ga, gb, bits, i, d0, count):
    parts = []
    for j in range(count):
        d = d0 + j
        y = bits[0] ^ (d & 1)
        z1 = bits[1] ^ ((d >> 1) & 1)
        z2 = bits[2] ^ ((d >> 2) & 1)
        parts.append(ga[0, y, z1, z2, i])
        parts.append(gb[y, 0, z1, z2, i])
    return jnp.concatenate(parts, axis=0).astype(F32)


def att_fwd_kernel(bits, lens, qk, v, ga, gb, mixed, lse):
    length = qk.shape[1]
    heads = v.shape[2] // HEAD_DIM
    bias = key_bias(lens[pl.program_id(1)], length)
    count = length // (2 * ga.shape[-2])
    cols = [pl.ds(i * HEAD_DIM, HEAD_DIM) for i in range(2 * heads)]

    def score(i):
        return dot_nt(qk[0, :, cols[i]], qk[0, :, cols[heads + i]])

    ahead = score(0)
    outs = []
    stats = []
    for i in range(heads):
        s = ahead * (SCALE * LOG2E) + bias
        if i + 1 < heads:
            ahead = score(i + 1)
        top = jnp.max(s, axis=1, keepdims=True)
        e = jnp.exp2(s - top)
        total = jnp.sum(e, axis=1, keepdims=True)
        w = (e * gate_rows(ga, gb, bits, i, 0, count)).astype(BF16)
        outs.append(dot_nn(w, v[0, :, cols[i]]) * (1.0 / total))
        stats.append(top + jnp.log2(total))
    mixed[0] = jnp.concatenate(outs, axis=1).astype(BF16)
    lse[0] = jnp.concatenate(stats, axis=1)


def attention_forward(bits, lens, qk, v, ga, gb):
    _, rows, w2 = qk.shape
    w1 = v.shape[2]
    count = lens.shape[0]
    length = rows // count
    heads, sub, keys = ga.shape[-3:]
    sds = jax.ShapeDtypeStruct
    return pl.pallas_call(
        att_fwd_kernel,
        out_shape=(sds((2, rows, w1), BF16), sds((2, rows, heads), F32)),
        grid_spec=pltpu.PrefetchScalarGridSpec(
            num_scalar_prefetch=2, grid=(2, count),
            in_specs=[
                pl.BlockSpec((1, length, w2), lambda k, s, *_: (k, s, 0)),
                pl.BlockSpec((1, length, w1), lambda k, s, *_: (k, s, 0)),
                spec_a((heads, sub, keys), lambda k: k), spec_b((heads, sub, keys), lambda k: k),
            ],
            out_specs=[
                pl.BlockSpec((1, length, w1), lambda k, s, *_: (k, s, 0)),
                pl.BlockSpec((1, length, heads), lambda k, s, *_: (k, s, 0)),
            ],
        ),
        compiler_params=params(n=2),
        cost_estimate=cost(16 * 2 * rows * length * w1, 16 * rows * w1),
    )(bits, lens, qk, v, ga, gb)


def att_bwd_kernel(last, bits, lens, qk, v, ga, gb, lse, dattn, wo, *rest):
    if last:
        ra, rb, dqk, dv, a_keep, a_send, b_keep, b_send, dm_s, dmt, qt, acc = rest
    else:
        dqk, dv, oga, ogb, dm_s, dmt, qt, acc = rest
    length = qk.shape[1]
    heads = v.shape[2] // HEAD_DIM
    hw = heads * HEAD_DIM
    k = pl.program_id(0)
    seq = pl.program_id(1)
    bias = key_bias(lens[seq], length)
    sub = ga.shape[-2]
    count = length // (2 * sub)
    cols = [pl.ds(i * HEAD_DIM, HEAD_DIM) for i in range(2 * heads)]

    dm = dot_nn(dattn[...], wo[0]).astype(BF16)
    dm_s[...] = dm
    dmt[...] = dm.T
    qt[...] = qk[0, :, pl.ds(0, hw)].T

    def products(i):
        return (
            dot_nt(qk[0, :, cols[i]], qk[0, :, cols[heads + i]]),
            dot_nt(dm_s[:, cols[i]], v[0, :, cols[i]]),
        )

    ahead = products(0)
    dqs, dks, dvs = [], [], []
    for i in range(heads):
        s, dw = ahead
        p = jnp.exp2(s * (SCALE * LOG2E) + bias - lse[0, :, pl.ds(i, 1)])
        if i + 1 < heads:
            ahead = products(i + 1)
        g = gate_rows(ga, gb, bits, i, 0, count)
        w = (p * g).astype(BF16)
        t = dw * p
        acc[i] = t + jnp.where(seq == 0, 0.0, acc[i])
        u = t * g
        ds = (u - p * jnp.sum(u, axis=1, keepdims=True)).astype(BF16)
        dqs.append(dot_nn(ds, qk[0, :, cols[heads + i]]) * SCALE)
        dvs.append(dot_nn(dmt[cols[i], :], w).astype(BF16).T)
        dks.append((dot_nn(qt[cols[i], :], ds) * SCALE).astype(BF16).T)
    dqk[0] = jnp.concatenate([d.astype(BF16) for d in dqs] + dks, axis=1)
    dv[0] = jnp.concatenate(dvs, axis=1)

    def first_rows(y, z1, z2):
        return pl.ds(pl.multiple_of(own(bits, y, z1, z2) * 2 * sub, sub), sub)

    def second_rows(y, z1, z2):
        return pl.ds(pl.multiple_of(own(bits, y, z1, z2) * 2 * sub + sub, sub), sub)

    @pl.when(seq == pl.num_programs(1) - 1)
    def _():
        if not last:
            for r in RELATIVE:
                for i in range(heads):
                    oga[(0,) + r + (i,)] = acc[i, first_rows(*r), :].astype(BF16)
                    ogb[(r[0], 0) + r[1:] + (i,)] = acc[i, second_rows(*r), :].astype(BF16)
            return

        def put_a(ref):
            for r in RELATIVE:
                for i in range(heads):
                    ref[r + (i,)] = (acc[i, first_rows(*r), :] + ra[(0,) + r + (i,)].astype(F32)).astype(BF16)

        @pl.when(k == 0)
        def _():
            put_a(a_keep)

        @pl.when(k == 1)
        def _():
            put_a(a_send)

        for r in RELATIVE:
            ref = b_send if r[0] else b_keep
            for i in range(heads):
                ref[(0,) + r[1:] + (i,)] = (
                    acc[i, second_rows(*r), :] + rb[(r[0], 0) + r[1:] + (i,)].astype(F32)
                ).astype(BF16)


def attention_backward(last, bits, lens, qk, v, ga, gb, lse, dattn, wo, got=()):
    _, rows, w2 = qk.shape
    w1 = v.shape[2]
    width = dattn.shape[1]
    count = lens.shape[0]
    length = rows // count
    tail = ga.shape[-3:]
    heads, sub, keys = tail
    sds = jax.ShapeDtypeStruct
    pick = lambda k: k
    in_specs = [
        pl.BlockSpec((1, length, w2), lambda k, s, *_: (k, s, 0)),
        pl.BlockSpec((1, length, w1), lambda k, s, *_: (k, s, 0)),
        spec_a(tail, pick), spec_b(tail, pick),
        pl.BlockSpec((1, length, heads), lambda k, s, *_: (k, s, 0)),
        pl.BlockSpec((length, width), lambda k, s, *_: (s, 0)),
        pl.BlockSpec((1, width, w1), lambda k, s, *_: (k, 0, 0)),
    ]
    out_shape = [sds((2, rows, w2), BF16), sds((2, rows, w1), BF16)]
    out_specs = [
        pl.BlockSpec((1, length, w2), lambda k, s, *_: (k, s, 0)),
        pl.BlockSpec((1, length, w1), lambda k, s, *_: (k, s, 0)),
    ]
    if last:
        in_specs += [spec_a(tail, pick), spec_b(tail, pick)]
        out_shape += [sds((2, 2, 2) + tail, BF16)] * 4
        out_specs += [whole((2, 2, 2) + tail)] * 2 + [
            pl.BlockSpec((1, 2, 2) + tail, lambda k, *_: (k, 0, 0, 0, 0, 0))
        ] * 2
    else:
        out_shape += [sds((2, 2, 2, 2) + tail, BF16)] * 2
        out_specs += [spec_a(tail, pick), spec_b(tail, pick)]
    return pl.pallas_call(
        functools.partial(att_bwd_kernel, last),
        out_shape=out_shape,
        grid_spec=pltpu.PrefetchScalarGridSpec(
            num_scalar_prefetch=2, grid=(2, count), in_specs=in_specs, out_specs=out_specs,
            scratch_shapes=[
                pltpu.VMEM((length, w1), BF16), pltpu.VMEM((w1, length), BF16),
                pltpu.VMEM((w1, length), BF16), pltpu.VMEM((heads, length, keys), F32),
            ],
        ),
        compiler_params=params(n=2),
        cost_estimate=cost(40 * 2 * rows * length * w1, 30 * rows * w1),
    )(bits, lens, qk, v, ga, gb, lse, dattn, wo, *got)


def qkv_kernel(first, bits, x, wa, wb, qk, v, wqk, wv, wo, *rest):
    w1 = v.shape[2]
    wb_s = rest[-1]
    assemble(wqk.at[0], wa, bits, False)
    assemble(wb_s, wb, bits, True)

    if first:

        @pl.when(pl.program_id(0) == 0)
        def _():
            rest[0][...] = x[...].T

    wv[0] = wb_s[:, pl.ds(0, w1)]
    wo[0] = wb_s[:, pl.ds(w1, w1)]
    qk[0] = dot_nn(x[...], wqk[0]).astype(BF16)
    v[0] = dot_nn(x[...], wv[0]).astype(BF16)


def project(first, bits, x, wa, wb):
    rows, width = x.shape
    p, w2 = wa.shape[-2:]
    w1 = w2 // 2
    sds = jax.ShapeDtypeStruct
    pick = lambda k: k
    head = lambda s: pl.BlockSpec((1,) + s, lambda k, *_: (k, 0, 0))
    return pl.pallas_call(
        functools.partial(qkv_kernel, first),
        out_shape=[sds((2, rows, w2), BF16), sds((2, rows, w1), BF16), sds((2, width, w2), BF16),
                   sds((2, width, w1), BF16), sds((2, width, w1), BF16)]
        + ([sds((width, rows), BF16)] if first else []),
        grid_spec=pltpu.PrefetchScalarGridSpec(
            num_scalar_prefetch=1, grid=(2,),
            in_specs=[whole((rows, width)), spec_a((p, w2), pick), spec_b((p, w2), pick)],
            out_specs=[head((rows, w2)), head((rows, w1)), head((width, w2)), head((width, w1)), head((width, w1))]
            + ([whole((width, rows))] if first else []),
            scratch_shapes=[pltpu.VMEM((width, w2), BF16)],
        ),
        compiler_params=params(),
        cost_estimate=cost(2 * rows * width * 2 * (w1 + w2), 8 * rows * width),
    )(bits, x, wa, wb)


def out_kernel(x, m0, m1, wo0, wo1, gain, bias, hid, unit, inverse, hidt):
    attn = dot_nt(m0[0], wo0[0]) + dot_nt(m0[1], wo0[1]) + dot_nt(m1[0], wo1[0]) + dot_nt(m1[1], wo1[1])
    u, inv = norm_stats(x[...].astype(F32) + attn)
    h = (u * gain[...] + bias[...]).astype(BF16)
    hid[...] = h
    hidt[...] = h.T
    unit[...] = u
    inverse[...] = inv


def out_forward(x, m0, m1, wo0, wo1, gain, bias, block=256):
    rows, width = x.shape
    w1 = wo0.shape[2]
    sds = jax.ShapeDtypeStruct
    row = lambda w: pl.BlockSpec((block, w), lambda r: (r, 0))
    mix = pl.BlockSpec((2, block, w1), lambda r: (0, r, 0))
    return pl.pallas_call(
        out_kernel,
        grid=(rows // block,),
        out_shape=(sds((rows, width), BF16), sds((rows, width), F32), sds((rows, 1), F32), sds((width, rows), BF16)),
        in_specs=[row(width), mix, mix, whole((2, width, w1)), whole((2, width, w1)), whole((1, width)), whole((1, width))],
        out_specs=[row(width), row(width), row(1), pl.BlockSpec((width, block), lambda r: (0, r))],
        compiler_params=params(),
        cost_estimate=cost(2 * rows * width * 4 * w1, 12 * rows * width),
    )(x, m0, m1, wo0, wo1, gain, bias)


def qkv_grad_kernel(last, bits, xt, dat, dqk, dv, mixed, *rest):
    if last:
        ra, rb, a_keep, a_send, b_keep, b_send, ta, tb = rest
    else:
        ga, gb, ta, tb = rest
    w1 = dv.shape[2]
    k = pl.program_id(0)
    ta[...] = dot_nn(xt[...], dqk[0]).astype(ta.dtype)
    tb[:, pl.ds(0, w1)] = dot_nn(xt[...], dv[0]).astype(tb.dtype)
    tb[:, pl.ds(w1, w1)] = dot_nn(dat[...], mixed[0]).astype(tb.dtype)
    if not last:
        scatter(ga, ta, bits, False)
        scatter(gb, tb, bits, True)
        return
    p = ra.shape[-2]

    def rows(r):
        return pl.ds(pl.multiple_of(own(bits, *r) * p, 16), p)

    def put_a(ref):
        for r in RELATIVE:
            ref[r] = (ta[rows(r), :] + ra[(0,) + r].astype(F32)).astype(BF16)

    @pl.when(k == 0)
    def _():
        put_a(a_keep)

    @pl.when(k == 1)
    def _():
        put_a(a_send)

    for r in RELATIVE:
        ref = b_send if r[0] else b_keep
        ref[(0,) + r[1:]] = (tb[rows(r), :] + rb[(r[0], 0) + r[1:]].astype(F32)).astype(BF16)


def qkv_grads(last, bits, xt, dat, dqk, dv, mixed, got=()):
    width, rows = xt.shape
    w2 = dqk.shape[2]
    w1 = dv.shape[2]
    per = width // 8
    sds = jax.ShapeDtypeStruct
    pick = lambda k: k
    head = lambda w: pl.BlockSpec((1, rows, w), lambda k, *_: (k, 0, 0))
    in_specs = [whole((width, rows)), whole((width, rows)), head(w2), head(w1), head(w1)]
    if last:
        in_specs += [spec_a((per, w2), pick), spec_b((per, w2), pick)]
        out_shape = [sds((2, 2, 2, per, w2), BF16)] * 4
        out_specs = [whole((2, 2, 2, per, w2))] * 2 + [
            pl.BlockSpec((1, 2, 2, per, w2), lambda k, *_: (k, 0, 0, 0, 0))
        ] * 2
    else:
        out_shape = [sds((2, 2, 2, 2, per, w2), BF16)] * 2
        out_specs = [spec_a((per, w2), pick), spec_b((per, w2), pick)]
    kind = F32 if last else BF16
    return pl.pallas_call(
        functools.partial(qkv_grad_kernel, last),
        out_shape=out_shape,
        grid_spec=pltpu.PrefetchScalarGridSpec(
            num_scalar_prefetch=1, grid=(2,), in_specs=in_specs, out_specs=out_specs,
            scratch_shapes=[pltpu.VMEM((width, w2), kind), pltpu.VMEM((width, w2), kind)],
        ),
        compiler_params=params(40),
        cost_estimate=cost(2 * rows * width * 2 * 2 * w2, 8 * rows * width),
    )(bits, xt, dat, dqk, dv, mixed, *got)


def dinput_kernel(dfirst, dqk0, dqk1, dv0, dv1, wqk0, wqk1, wv0, wv1, out):
    total = dfirst[...]
    for a, b, wa, wb in ((dqk0, dv0, wqk0, wv0), (dqk1, dv1, wqk1, wv1)):
        for k in range(2):
            total = total + dot_nt(a[k], wa[k]) + dot_nt(b[k], wb[k])
    out[...] = total


def input_backward(dfirst, dqk0, dqk1, dv0, dv1, wqk0, wqk1, wv0, wv1, block=256):
    rows, width = dfirst.shape
    w2 = wqk0.shape[2]
    w1 = wv0.shape[2]
    row = pl.BlockSpec((block, width), lambda r: (r, 0))
    part = lambda w: pl.BlockSpec((2, block, w), lambda r: (0, r, 0))
    return pl.pallas_call(
        dinput_kernel,
        grid=(rows // block,),
        out_shape=jax.ShapeDtypeStruct((rows, width), F32),
        in_specs=[row, part(w2), part(w2), part(w1), part(w1)]
        + [whole((2, width, w2))] * 2 + [whole((2, width, w1))] * 2,
        out_specs=row,
        compiler_params=params(),
        cost_estimate=cost(2 * rows * width * 4 * (w1 + w2), 14 * rows * width),
    )(dfirst, dqk0, dqk1, dv0, dv1, wqk0, wqk1, wv0, wv1)


GROUPS = 8


def partner_dp(value, bit):
    size = lax.axis_size("dp")
    step = (1 << bit) * (size // GROUPS)
    return lax.ppermute(value, "dp", [(i, i ^ step) for i in range(size)])


def partner_head(value, bit):
    size = lax.axis_size("head")
    return lax.ppermute(value, "head", [(i, i ^ (1 << bit)) for i in range(size)])


def over_y(value):
    return partner_dp(value, 0)


def over_near(value):
    return partner_dp(value, 1)


def over_far(value):
    return partner_dp(value, 2)


def over_pair(value):
    return partner_head(value, 0)


def over_x(value):
    return partner_head(value, 1)


def inner_groups():
    inner = lax.axis_size("dp") // GROUPS
    return inner, [[g * inner + i for i in range(inner)] for g in range(GROUPS)]


def inner_gather(value, axis):
    inner, groups = inner_groups()
    if inner == 1:
        return value
    return lax.all_gather(value, "dp", axis_index_groups=groups, axis=axis, tiled=True)


def inner_scatter(value, axis):
    inner, groups = inner_groups()
    if inner == 1:
        return value
    return lax.psum_scatter(value, "dp", axis_index_groups=groups, scatter_dimension=axis, tiled=True)


def after(values, *waits):
    return lax.optimization_barrier((tuple(values), waits))[0]


def wide(value):
    return value.astype(F32)


def first_sum(keep, got):
    return (wide(keep[1]) + wide(got[1])).astype(BF16)


def second_sum(keep, got, more):
    return (wide(keep[0, 1]) + wide(got[0, 1]) + wide(more[1])).astype(BF16)


def third_sum(keep, got, more, last):
    return wide(keep[0, 0]) + wide(got[0, 0]) + wide(more[0]) + wide(last)


def low_sum(keep, got):
    return (wide(keep[1]) + wide(got[1])).astype(BF16)


def high_sum(keep, got, more):
    return wide(keep[0]) + wide(got[0]) + wide(more)


def total_steps():
    steps = []
    for name in ("head", "dp"):
        size = lax.axis_size(name)
        step = 1
        while step < size:
            steps.append((name, [(i, i ^ step) for i in range(size)]))
            step *= 2
    return steps


def total_some(value, *steps):
    for name, pairs in steps:
        value = value + lax.ppermute(value, name, pairs)
    return value


def per_device(layer_input, output_grad, lengths, w_qkv, w_out, w_up, w_down,
               norm_gains, norm_biases, mask_logits, mask_noise):
    micro, seq, width = layer_input.shape
    rows = micro * seq
    x = layer_input.reshape(rows, width)
    dout = output_grad.reshape(rows, width)
    place = lax.axis_index("dp") // (lax.axis_size("dp") // GROUPS)
    bits = jnp.stack([place & 1, (place >> 1) & 1, (place >> 2) & 1]).astype(jnp.int32)
    lens = lax.dynamic_slice_in_dim(lengths, lax.axis_index("head"), 1, 1).reshape(micro)

    gate_part = jax.nn.sigmoid(mask_logits + mask_noise)
    gate_all = inner_gather(gate_part.astype(BF16), 1)
    sub = gate_all.shape[1] // 2
    gain1, gain2 = norm_gains[0:1], norm_gains[1:2]
    bias1, bias2 = norm_biases[0:1], norm_biases[1:2]

    ga = jnp.stack([
        inner_gather(jnp.concatenate([w_qkv[0], w_qkv[1]], axis=1), 0),
        inner_gather(jnp.concatenate([w_qkv[2], w_out.T], axis=1), 0),
    ])
    gb = jnp.stack([gate_all[:, :sub], gate_all[:, sub:]])
    up_all, down_all = inner_gather(w_up, 0), inner_gather(w_down.T, 0)
    units = up_all.shape[1]
    most = units * 2 // 3
    gc = jnp.stack([up_all[:, :most], down_all[:, :most]])
    ge = jnp.stack([up_all[:, most:], down_all[:, most:]])

    got = over_far(ga)
    ga = jnp.stack([ga, got], axis=1)
    got = over_near(ga)
    ga = jnp.stack([ga, got], axis=1)
    aa, ab = ga[0], ga[1]
    (gb,) = after((gb,), got)
    ra, rb = over_y(aa), over_x(ab)
    far_b = over_far(gb)
    aa, ab = jnp.stack([aa, ra]), jnp.stack([ab, rb])
    gb, = after((gb,), ra, rb)
    gb = jnp.stack([gb, far_b], axis=1)
    aa, ab = after((aa, ab), gb)
    ra, rb = over_x(aa), over_y(ab)
    near_b = over_near(gb)
    (gc,) = after((gc,), near_b)
    far_c = over_far(gc)
    gb = jnp.stack([gb, near_b], axis=1)
    ba, bb = gb[0], gb[1]
    aa, ab = jnp.stack([aa, ra]), jnp.stack([ab, rb])
    ba, bb = after((ba, bb), ra, rb)
    ca, cb = over_pair(aa), over_pair(ab)
    ra, rb = over_y(ba), over_x(bb)
    qk0, v0, wqk0, wv0, wo0, xt = project(True, bits, x, aa, ab)
    ba, bb = jnp.stack([ba, ra]), jnp.stack([bb, rb])
    ba, bb, gc, ca, cb = after((ba, bb, gc, ca, cb), qk0, ra, rb)
    ra, rb = over_x(ba), over_y(bb)
    gc = jnp.stack([gc, far_c], axis=1)
    near_c = over_near(gc)
    qk1, v1, wqk1, wv1, wo1 = project(False, bits, x, ca, cb)
    ba, bb = jnp.stack([ba, ra]), jnp.stack([bb, rb])
    gc = jnp.stack([gc, near_c], axis=1)
    fa, fb = gc[0], gc[1]
    fa, fb, ba, bb, ge = after((fa, fb, ba, bb, ge), ra, rb, near_c, qk1)
    ba1, bb1 = over_pair(ba), over_pair(bb)
    ra, rb = over_y(fa), over_x(fb)
    far_e = over_far(ge)
    m0, lse0 = attention_forward(bits, lens, qk0, v0, ba, bb)
    fa, fb = jnp.stack([fa, ra]), jnp.stack([fb, rb])
    ge = jnp.stack([ge, far_e], axis=1)
    fa, fb, ge, ba1, bb1 = after((fa, fb, ge, ba1, bb1), m0)
    ra, rb = over_x(fa), over_y(fb)
    near_e = over_near(ge)
    ge = jnp.stack([ge, near_e], axis=1)
    m1, lse1 = attention_forward(bits, lens, qk1, v1, ba1, bb1)
    hid, unit, inverse, hidt = out_forward(x, m0, m1, wo0, wo1, gain1, bias1)
    fa, fb = jnp.stack([fa, ra]), jnp.stack([fb, rb])
    ea, eb = ge[0], ge[1]
    fa, fb, ea, eb = after((fa, fb, ea, eb), hid, ra, rb)
    fa1, fb1 = over_pair(fa), over_pair(fb)
    ra, rb = over_y(ea), over_x(eb)
    ea, eb = jnp.stack([ea, ra]), jnp.stack([eb, rb])
    ea, eb, hid = after((ea, eb, hid), fa1, fb1)
    ra, rb = over_x(ea), over_y(eb)
    act, gp, part = ffn_part(bits, hid, fa, fa1, fb, fb1, units)
    ea, eb = jnp.stack([ea, ra]), jnp.stack([eb, rb])
    ea, eb = after((ea, eb), part)
    ea1, eb1 = over_pair(ea), over_pair(eb)
    act, gp, out, dsec, dffn, dffnt, dgain2, dbias2 = ffn_rest(
        bits, lens, hid, ea, ea1, eb, eb1, part, gain2, bias2, dout, act, gp
    )

    steps = total_steps()
    down0, down1 = down_grads(bits, dffnt, act)
    cd = over_pair(down1)
    dffn, = after((dffn,), down1)
    up1, part = ffn_backward(False, bits, hidt, dffn, fa1, ea1, fb1, eb1, gp)
    down0, cd, up1, dffn = after((down0, cd, up1, dffn), part)
    xd = over_y(first_sum(down0, cd))
    cu = over_pair(up1)
    up0, dfirst, dattn, dattnt, dgain1, dbias1 = ffn_backward(
        True, bits, hidt, dffn, fa, ea, fb, eb, gp, (dsec, part, unit, inverse, gain1)
    )
    up0, cu, norms, dattn = after((up0, cu, jnp.concatenate([dgain1, dgain2, dbias1, dbias2]), dattn), up0)
    xu = over_x(first_sum(up0, cu))
    norms = total_some(norms, steps[0])
    dqk1, dv1, ga1, gb1 = attention_backward(False, bits, lens, qk1, v1, ba1, bb1, lse1, dattn, wo1)
    ga1, gb1, norms, dqk1, xd, xu = after((ga1, gb1, norms, dqk1, xd, xu), dv1)
    cga, cgb = over_pair(ga1), over_pair(gb1)
    norms = total_some(norms, steps[3])
    yd, yu = over_x(second_sum(down0, cd, xd)), over_y(second_sum(up0, cu, xu))
    qka1, vo1 = qkv_grads(False, bits, xt, dattnt, dqk1, dv1, m1)
    qka1, vo1, dattn, norms, cga, cgb, yd, yu = after((qka1, vo1, dattn, norms, cga, cgb, yd, yu), vo1)
    cqk, cvo = over_pair(qka1), over_pair(vo1)
    u, d = third_sum(up0, cu, xu, yu), third_sum(down0, cd, xd, yd)
    near_f = over_near(jnp.stack([u[1], d[1]]).astype(BF16))
    norms = total_some(norms, steps[4])
    dqk0, dv0, ga0, ga_out, gb0, gb_out = attention_backward(
        True, bits, lens, qk0, v0, ba, bb, lse0, dattn, wo0, (cga, cgb)
    )
    ga_out, gb_out, dqk0, norms, cqk, cvo, near_f = after((ga_out, gb_out, dqk0, norms, cqk, cvo, near_f), dv0)
    xga, xgb = over_x(ga_out), over_y(gb_out)
    far_f = over_far(jnp.stack([u[0, 1] + wide(near_f[0, 1]), d[0, 1] + wide(near_f[1, 1])]).astype(BF16))
    qka0, qka_out, vo0, vo_out = qkv_grads(True, bits, xt, dattnt, dqk0, dv0, m0, (cqk, cvo))
    qka_out, vo_out, far_f, xga, xgb, dqk0 = after((qka_out, vo_out, far_f, xga, xgb, dqk0), vo0)
    xqk, xvo = over_x(qka_out), over_y(vo_out)
    yga, ygb = over_y(low_sum(ga0, xga)), over_x(low_sum(gb0, xgb))
    dinput = input_backward(dfirst, dqk0, dqk1, dv0, dv1, wqk0, wqk1, wv0, wv1)
    xqk, xvo, yga, ygb, norms = after((xqk, xvo, yga, ygb, norms), dinput)
    yqk, yvo = over_y(low_sum(qka0, xqk)), over_x(low_sum(vo0, xvo))
    g1, g2 = high_sum(ga0, xga, yga), high_sum(gb0, xgb, ygb)
    near_g = over_near(jnp.stack([g1[1], g2[1]]).astype(BF16))
    norms, = after((norms,), yqk, yvo)
    norms = total_some(norms, steps[1])
    w1, w2 = high_sum(qka0, xqk, yqk), high_sum(vo0, xvo, yvo)
    near_w = over_near(jnp.stack([w1[1], w2[1]]).astype(BF16))
    far_g = over_far(jnp.stack([g1[0, 1] + wide(near_g[0, 1]), g2[0, 1] + wide(near_g[1, 1])]).astype(BF16))
    norms, = after((norms,), near_w)
    norms = total_some(norms, *steps[2:3], *steps[5:])
    far_w = over_far(jnp.stack([w1[0, 1] + wide(near_w[0, 1]), w2[0, 1] + wide(near_w[1, 1])]).astype(BF16))

    up_grad = u[0, 0] + wide(near_f[0, 0]) + wide(far_f[0])
    down_grad = d[0, 0] + wide(near_f[1, 0]) + wide(far_f[1])
    gate_a = g1[0, 0] + wide(near_g[0, 0]) + wide(far_g[0])
    gate_b = g2[0, 0] + wide(near_g[1, 0]) + wide(far_g[1])
    qk_grad = w1[0, 0] + wide(near_w[0, 0]) + wide(far_w[0])
    vo_grad = w2[0, 0] + wide(near_w[1, 0]) + wide(far_w[1])

    qk_grad, vo_grad = inner_scatter(qk_grad, 0), inner_scatter(vo_grad, 0)
    local = vo_grad.shape[1] // 2
    gate_grad = inner_scatter(jnp.concatenate([gate_a, gate_b], axis=1), 1)
    return (
        out.reshape(micro, seq, width),
        dinput.reshape(micro, seq, width),
        jnp.stack([qk_grad[:, :local], qk_grad[:, local:], vo_grad[:, :local]]),
        vo_grad[:, local:].T,
        inner_scatter(up_grad, 0),
        inner_scatter(down_grad, 0).T,
        norms[:2],
        norms[2:],
        gate_grad * gate_part * (1.0 - gate_part),
    )


def solution(mesh):
    rows = P(None, ("dp", "head"), None)
    gates = P("head", "dp", None)
    weights = (P(None, "dp", "head"), P("head", "dp"), P("dp", "head"), P("head", "dp"))
    return jax.shard_map(
        per_device,
        mesh=mesh,
        in_specs=(rows, rows, P(None, "dp")) + weights + (P(), P(), gates, gates),
        out_specs=(rows, rows) + weights + (P(), P(), gates),
        check_vma=False,
    )
```

profile of v0, /device:TPU:0, one launch (start us, length us, event | category | flops | bytes accessed | tf_op | source)
XLA Modules:
  0.0 377.9 jit_solution(13455728110571675362)
XLA Ops:
  2.7 4.1 %collective-permute-start = (bf16[2,96,384]{2,1,0:T(8,128)(2,1)S(1)}, bf16[2,96,384]{2,1,0:T(8,128)(2,1)S(1)}, u32[]{:S(2)}, u32[]{:S(2)}) collective-permute-start(bf16[2,96,384]{2,1,0:T(8,128)(2,1)S(1)} %get-tuple-element.311), channel_id=1, source_target_pairs={{0,16},{4,20},{8,24},{12,28},{16,0},{20,4},{24,8},{28,12},{1,17},{... | collective-permute-start | bytes 442376 | tf_op jit(solution)/shard_map/ppermute | solution.py:739
  6.8 7.0 %collective-permute-done = bf16[2,96,384]{2,1,0:T(8,128)(2,1)S(1)} collective-permute-done((bf16[2,96,384]{2,1,0:T(8,128)(2,1)S(1)}, bf16[2,96,384]{2,1,0:T(8,128)(2,1)S(1)}, u32[]{:S(2)}, u32[]{:S(2)}) %collective-permute-start) | collective-permute-done | bytes 147488 | tf_op jit(solution)/shard_map/ppermute | solution.py:739
  14.8 7.3 %collective-permute-done.1 = bf16[2,2,96,384]{3,2,1,0:T(8,128)(2,1)S(1)} collective-permute-done((bf16[2,2,96,384]{3,2,1,0:T(8,128)(2,1)S(1)}, bf16[2,2,96,384]{3,2,1,0:T(8,128)(2,1)S(1)}, u32[]{:S(2)}, u32[]{:S(2)}) %collective-permute-start.1) | collective-permute-done | bytes 294944 | tf_op jit(solution)/shard_map/ppermute | solution.py:739
  25.0 3.4 collective-permute-start.4
  30.7 6.0 %collective-permute-done.4 = bf16[2,3,32,512]{3,2,1,0:T(8,128)(2,1)S(1)} collective-permute-done((bf16[2,3,32,512]{3,2,1,0:T(8,128)(2,1)S(1)}, bf16[2,3,32,512]{3,2,1,0:T(8,128)(2,1)S(1)}, u32[]{:S(2)}, u32[]{:S(2)}) %collective-permute-start.4) | collective-permute-done | bytes 196640 | tf_op jit(solution)/shard_map/ppermute | solution.py:739
  38.5 12.6 %collective-permute-done.7 = bf16[2,2,2,96,384]{4,3,2,1,0:T(8,128)(2,1)S(1)} collective-permute-done((bf16[2,2,2,96,384]{4,3,2,1,0:T(8,128)(2,1)S(1)}, bf16[2,2,2,96,384]{4,3,2,1,0:T(8,128)(2,1)S(1)}, u32[]{:S(2)}, u32[]{:S(2)}) %collective-permute-start.7) | collective-permute-done | bytes 589856 | tf_op jit(solution)/shard_map/ppermute | solution.py:739
  56.1 8.0 %shard_map.178 = (bf16[2,1024,384]{2,1,0:T(8,128)(2,1)}, bf16[2,1024,192]{2,1,0:T(8,128)(2,1)}, bf16[2,768,384]{2,1,0:T(8,128)(2,1)}, bf16[2,768,192]{2,1,0:T(8,...) custom-call(s32[3]{0:T(128)} %pad_add_fusion.bits, bf16[1024,768]{1,0:T(8,128)(2,1)} %bitcast.221, ...), custom_call_target="tpu_custom_call" | custom-call | flops 9059696 | bytes 31457 | tf_op jit(solution)/shard_map/pallas_call | solution.py:596
  68.9 5.0 %collective-permute-start.13 = (bf16[2,2,96,512]{3,2,0,1:T(8,128)(2,1)S(1)}, bf16[2,2,96,512]{3,2,0,1:T(8,128)(2,1)S(1)}, u32[]{:S(2)}, u32[]{:S(2)}) collective-permute-start(bf16[2,2,96,512]{3,2,0,1:T(8,128)(2,1)S(1)} %get-tuple-element.296), channel_id=1, source_target_pairs={{0,8},{4,12},{8,0},{12,4},{16,24},{20,28},{24,16},{28,20},{1,9},{5... | collective-permute-start | bytes 1179656 | tf_op jit(solution)/shard_map/ppermute | solution.py:739
  75.4 6.8 %shard_map.179 = (bf16[2,1024,384]{2,1,0:T(8,128)(2,1)}, bf16[2,1024,192]{2,1,0:T(8,128)(2,1)}, bf16[2,768,384]{2,1,0:T(8,128)(2,1)}, bf16[2,768,192]{2,1,0:T(8,128)(2,1)}, bf16[2,768,192]{2,1,0:T(8,128)(2,1)}) custom-call(s32[3]{0:T(128)} %pad_add_fusion.bits, bf16[1024,768]{1,0:T(8,128)(2,1)} %bitcast.222, ...), custom_call_target="tpu_custom_call" | custom-call | flops 9059696 | bytes 31457 | tf_op jit(solution)/shard_map/pallas_call | solution.py:596
  92.8 9.3 %shard_map.180 = (bf16[2,1024,192]{2,1,0:T(8,128)(2,1)}, f32[2,1024,3]{2,1,0:T(8,128)}) custom-call(s32[3]{0:T(128)} %pad_add_fusion.bits, s32[2]{0:T(128)} %dynamic-slice_reduce_fusion.lens, bf16[2,1024,384]{2,1,0:T(8,128)(2,1)} %get-tuple-element.146.qk, bf16[2,1024,192]{2,1,0:T(8,128)(2,1)} %get-tuple-element.158.v, ...), custom_call_target="tpu_custom_call" | custom-call | flops 16106127 | bytes 15728 | tf_op jit(solution)/shard_map/pallas_call | solution.py:423
  110.8 9.3 %shard_map.181 = (bf16[2,1024,192]{2,1,0:T(8,128)(2,1)}, f32[2,1024,3]{2,1,0:T(8,128)}) custom-call(s32[3]{0:T(128)} %pad_add_fusion.bits, s32[2]{0:T(128)} %dynamic-slice_reduce_fusion.lens, bf16[2,1024,384]{2,1,0:T(8,128)(2,1)} %get-tuple-element.152.qk, bf16[2,1024,192]{2,1,0:T(8,128)(2,1)} %get-tuple-element.163.v, ...), custom_call_target="tpu_custom_call" | custom-call | flops 16106127 | bytes 15728 | tf_op jit(solution)/shard_map/pallas_call | solution.py:423
  120.1 7.4 %shard_map.182 = (bf16[1024,768]{1,0:T(8,128)(2,1)}, f32[1024,768]{1,0:T(8,128)}, f32[1024,1]{1,0:T(8,128)}, bf16[768,1024]{1,0:T(8,128)(2,1)}) custom-call(bf16[1024,768]{1,0:T(8,128)(2,1)} %bitcast.223, bf16[2,1024,192]{2,1,0:T(8,128)(2,1)} %get-tuple-element.159.m0.mixed, bf16[2,1024,192]{2,1,0:T(8,128)(2,1)} %get-tuple-element.166.m1.mixed, ...), custom_call_target="tpu_custom_call" | custom-call | flops 6039797 | bytes 47185 | tf_op jit(solution)/shard_map/pallas_call | solution.py:629
  130.3 5.0 %collective-permute-done.24 = bf16[2,2,96,256]{3,2,1,0:T(8,128)(2,1)S(1)} collective-permute-done((bf16[2,2,96,256]{3,2,1,0:T(8,128)(2,1)S(1)}, bf16[2,2,96,256]{3,2,1,0:T(8,128)(2,1)S(1)}, u32[]{:S(2)}, u32[]{:S(2)}) %collective-permute-start.24) | collective-permute-done | bytes 196640 | tf_op jit(solution)/shard_map/ppermute | solution.py:739
  138.6 13.3 %shard_map.183 = (bf16[4,1024,768]{2,1,0:T(8,128)(2,1)}, f32[4,1024,768]{2,1,0:T(8,128)}, f32[1024,768]{1,0:T(8,128)}) custom-call(s32[3]{0:T(128)S(1)} %copy-done.20, bf16[1024,768]{1,0:T(8,128)(2,1)S(1)} %copy-done.11, bf16[2,2,2,2,96,512]{5,4,3,2,1,0:T(8,128)(2,1)S(1)} %pad_maximum_fusion.2.ua0.uap, ...), custom_call_target="tpu_custom_call" | custom-call | flops 32212254 | bytes 62914 | tf_op jit(solution)/shard_map/pallas_call | solution.py:160
  155.6 15.4 %shard_map.184 = (bf16[4,1024,768]{2,1,0:T(8,128)(2,1)}, f32[4,1024,768]{2,1,0:T(8,128)}, bf16[1024,768]{1,0:T(8,128)(2,1)}, f32[1024,768]{1,0:T(8,128)}, bf16[1...) custom-call(s32[3]{0:T(128)S(1)} %copy-done.20, ...), custom_call_target="tpu_custom_call", output_to_operand_aliasing={{0}: (11, {}), {1}: (12, {})} | custom-call | flops 16106127 | bytes 78643 | tf_op jit(solution)/shard_map/pallas_call | solution.py:223
  176.3 7.0 %shard_map.185 = (bf16[2,2,2,2,96,768]{5,4,3,2,1,0:T(8,128)(2,1)S(1)}, bf16[2,2,2,2,96,768]{5,4,3,2,1,0:T(8,128)(2,1)S(1)}) custom-call(s32[3]{0:T(128)S(1)} %copy-done.20, bf16[768,1024]{1,0:T(8,128)(2,1)S(1)} %copy-done.19, bf16[4,1024,768]{2,1,0:T(8,128)(2,1)S(1)} %copy-done.2), custom_call_target="tpu_custom_call" | custom-call | flops 24159192 | bytes 55050 | tf_op jit(solution)/shard_map/pallas_call | solution.py:263
  183.5 14.4 %shard_map.186 = (bf16[2,2,2,2,96,768]{5,4,3,2,1,0:T(8,128)(2,1)}, f32[1024,768]{1,0:T(8,128)}) custom-call(s32[3]{0:T(128)} %pad_add_fusion.bits, bf16[768,1024]{1,0:T(8,128)(2,1)} %get-tuple-element.183.ht, bf16[1024,768]{1,0:T(8,128)(2,1)} %copy-done.6, bf16[2,2,2,2,96,512]{5,4,3,2,1,0:T(8,128)(2,1)} %copy-done.12, ...), custom_call_target="tpu_custom_call" | custom-call | flops 36238784 | bytes 117964 | tf_op jit(solution)/shard_map/pallas_call | solution.py:361
  200.5 20.9 %shard_map.187 = (bf16[2,2,2,2,96,768]{5,4,3,2,1,0:T(8,128)(2,1)}, f32[1024,768]{1,0:T(8,128)}, bf16[1024,768]{1,0:T(8,128)(2,1)}, bf16[768,1024]{1,0:T(8,128)(2...) custom-call(s32[3]{0:T(128)} %pad_add_fusion.bits, bf16[768,1024]{1,0:T(8,128)(2,1)} %get-tuple-element.183.ht, ...), custom_call_target="tpu_custom_call" | custom-call | flops 36238784 | bytes 117964 | tf_op jit(solution)/shard_map/pallas_call | solution.py:361
  222.1 3.5 fusion.1
  226.3 18.4 %shard_map.188 = (bf16[2,1024,384]{2,1,0:T(8,128)(2,1)}, bf16[2,1024,192]{2,1,0:T(8,128)(2,1)}, bf16[2,2,2,2,3,32,512]{6,5,4,3,2,1,0:T(8,128)(2,1)}, bf16[2,2,2,2,3,32,512]{6,5,4,3,2,1,0:T(8,128)(2,1)}) custom-call(s32[3]{0:T(128)} %pad_add_fusion.bits, s32[2]{0:T(128)} %dynamic-slice_reduce_fusion.lens, bf16[2,1024,384]{2,1,0:T(8,128)(2,1)} %get-tuple-element.152.qk, ...), custom_call_target="tpu_custom_call" | custom-call | flops 40265320 | bytes 29491 | tf_op jit(solution)/shard_map/pallas_call | solution.py:556
  244.7 8.9 %collective-permute-done.36 = bf16[2,2,2,96,768]{4,3,2,1,0:T(8,128)(2,1)} collective-permute-done((bf16[2,2,2,96,768]{4,3,2,1,0:T(8,128)(2,1)}, bf16[2,2,2,96,768]{4,3,2,1,0:T(8,128)(2,1)}, u32[]{:S(2)}, u32[]{:S(2)}) %collective-permute-start.36) | collective-permute-done | bytes 1179680 | tf_op jit(solution)/shard_map/ppermute | solution.py:744
  261.0 5.7 %shard_map.189 = (bf16[2,2,2,2,96,384]{5,4,3,2,1,0:T(8,128)(2,1)}, bf16[2,2,2,2,96,384]{5,4,3,2,1,0:T(8,128)(2,1)}) custom-call(s32[3]{0:T(128)S(1)} %copy-done.21, bf16[768,1024]{1,0:T(8,128)(2,1)S(1)} %copy-done.8, bf16[768,1024]{1,0:T(8,128)(2,1)S(1)} %copy-done.10, bf16[2,1024,384]{2,1,0:T(8,128)(2,1)S(1)} %copy-done.9, ...), custom_call_target="tpu_custom_call" | custom-call | flops 12079595 | bytes 31457 | tf_op jit(solution)/shard_map/pallas_call | solution.py:695
  266.8 6.0 %collective-permute-done.41 = bf16[2,2,96,768]{3,2,1,0:T(8,128)(2,1)S(1)} collective-permute-done((bf16[2,2,96,768]{3,2,1,0:T(8,128)(2,1)S(1)}, bf16[2,2,96,768]{3,2,1,0:T(8,128)(2,1)S(1)}, u32[]{:S(2)}, u32[]{:S(2)}) %collective-permute-start.41) | collective-permute-done | bytes 589856 | tf_op jit(solution)/shard_map/ppermute | solution.py:739
  281.7 19.5 %shard_map.190 = (bf16[2,1024,384]{2,1,0:T(8,128)(2,1)}, bf16[2,1024,192]{2,1,0:T(8,128)(2,1)}, bf16[2,2,2,3,32,512]{5,4,3,2,1,0:T(8,128)(2,1)}, bf16[2,2,2,3,32...) custom-call(s32[3]{0:T(128)} %pad_add_fusion.bits, ...), custom_call_target="tpu_custom_call" | custom-call | flops 40265320 | bytes 29491 | tf_op jit(solution)/shard_map/pallas_call | solution.py:556
  305.8 5.8 %shard_map.191 = (bf16[2,2,2,96,384]{4,3,2,1,0:T(8,128)(2,1)S(1)}, bf16[2,2,2,96,384]{4,3,2,1,0:T(8,128)(2,1)S(1)}, bf16[2,2,2,96,384]{4,3,2,1,0:T(8,128)(2,1)S(1)}, bf16[2,2,2,96,384]{4,3,2,1,0:T(8,128)(2,1)S(1)}) custom-call(s32[3]{0:T(128)S(1)} %copy-done.22, bf16[768,1024]{1,0:T(8,128)(2,1)S(1)} %copy-done.8, bf16[768,1024]{1,0:T(8,128)(2,1)S(1)} %copy-done.10, ...), custom_call_target="tpu_custom_call" | custom-call | flops 12079595 | bytes 31457 | tf_op jit(solution)/shard_map/pallas_call | solution.py:695
  311.6 7.0 %collective-permute-done.46 = bf16[2,96,768]{2,1,0:T(8,128)(2,1)S(1)} collective-permute-done((bf16[2,96,768]{2,1,0:T(8,128)(2,1)S(1)}, bf16[2,96,768]{2,1,0:T(8,128)(2,1)S(1)}, u32[]{:S(2)}, u32[]{:S(2)}) %collective-permute-start.46) | collective-permute-done | bytes 294944 | tf_op jit(solution)/shard_map/ppermute | solution.py:739
  325.8 9.8 %shard_map.192 = f32[1024,768]{1,0:T(8,128)} custom-call(f32[1024,768]{1,0:T(8,128)} %get-tuple-element.197.dfirst, bf16[2,1024,384]{2,1,0:T(8,128)(2,1)} %get-tuple-element.248.dqk.dqk0, bf16[2,1024,384]{2,1,0:T(8,128)(2,1)} %get-tuple-element.219.dqk.dqk1, bf16[2,1024,192]{2,1,0:T(8,128)(2,1)} %get-tuple-element.238.dv.dv0, ...), custom_call_target="tpu_custom_call" | custom-call | flops 18119392 | bytes 55050 | tf_op jit(solution)/shard_map/pallas_call | solution.py:721
  338.0 6.2 %collective-permute-done.51 = bf16[2,2,3,32,512]{4,3,2,1,0:T(8,128)(2,1)} collective-permute-done((bf16[2,2,3,32,512]{4,3,2,1,0:T(8,128)(2,1)}, bf16[2,2,3,32,512]{4,3,2,1,0:T(8,128)(2,1)}, u32[]{:S(2)}, u32[]{:S(2)}) %collective-permute-start.51) | collective-permute-done | bytes 393248 | tf_op jit(solution)/shard_map/ppermute | solution.py:739
  350.3 3.4 collective-permute-done.54
  358.7 3.0 collective-permute-done.59
  361.9 3.6 collective-permute-done.55
  369.0 5.3 %collective-permute-done.60 = bf16[2,3,32,512]{3,2,1,0:T(8,128)(2,1)S(1)} collective-permute-done((bf16[2,3,32,512]{3,2,1,0:T(8,128)(2,1)S(1)}, bf16[2,3,32,512]{3,2,1,0:T(8,128)(2,1)S(1)}, u32[]{:S(2)}, u32[]{:S(2)}) %collective-permute-start.60) | collective-permute-done | bytes 196640 | tf_op jit(solution)/shard_map/ppermute | solution.py:739
  (293 shorter events, 107.6 us)
Async XLA Ops:
  51.2 15.0 %collective-permute-start.11 = (bf16[2,2,2,2,96,384]{5,4,3,2,1,0:T(8,128)(2,1)S(1)}, bf16[2,2,2,2,96,384]{5,4,3,2,1,0:T(8,128)(2,1)}, u32[]{:S(2)}, u32[]{:S(2)}) collective-permute-start(bf16[2,2,2,2,96,384]{5,4,3,2,1,0:T(8,128)(2,1)S(1)} %pad_maximum_fusion.5.wb), channel_id=1, source_target_pairs={{0,1},{1,0},{2,3},{3,2},{4,5},{5,4},{6,7},{7,6},{8,9},{9,8},{10,11... | collective-permute-start | bytes 3538952 | tf_op jit(solution)/shard_map/ppermute | solution.py:744
  51.5 14.7 %collective-permute-start.10 = (bf16[2,2,2,2,96,384]{5,4,3,2,1,0:T(8,128)(2,1)S(1)}, bf16[2,2,2,2,96,384]{5,4,3,2,1,0:T(8,128)(2,1)}, u32[]{:S(2)}, u32[]{:S(2)}) collective-permute-start(bf16[2,2,2,2,96,384]{5,4,3,2,1,0:T(8,128)(2,1)S(1)} %pad_maximum_fusion.4.wa), channel_id=1, source_target_pairs={{0,1},{1,0},{2,3},{3,2},{4,5},{5,4},{6,7},{7,6},{8,9},{9,8},{10,11... | collective-permute-start | bytes 3538952 | tf_op jit(solution)/shard_map/ppermute | solution.py:744
  66.3 19.4 %collective-permute-start.14 = (bf16[2,2,2,3,32,512]{5,4,3,2,1,0:T(8,128)(2,1)S(1)}, bf16[2,2,2,3,32,512]{5,4,3,2,1,0:T(8,128)(2,1)S(1)}, u32[]{:S(2)}, u32[]{:S(2)}) collective-permute-start(bf16[2,2,2,3,32,512]{5,4,3,2,1,0:T(8,128)(2,1)S(1)} %pad_maximum_fusion.6), channel_id=1, source_target_pairs={{0,2},{1,3},{2,0},{3,1},{4,6},{5,7},{6,4},{7,5},{8,10},{9,11},{10,... | collective-permute-start | bytes 2359304 | tf_op jit(solution)/shard_map/ppermute | solution.py:744
  67.8 19.1 %collective-permute-start.15 = (bf16[2,2,2,3,32,512]{5,4,3,2,1,0:T(8,128)(2,1)S(1)}, bf16[2,2,2,3,32,512]{5,4,3,2,1,0:T(8,128)(2,1)S(1)}, u32[]{:S(2)}, u32[]{:S(2)}) collective-permute-start(bf16[2,2,2,3,32,512]{5,4,3,2,1,0:T(8,128)(2,1)S(1)} %pad_maximum_fusion.7), channel_id=1, source_target_pairs={{0,4},{4,0},{8,12},{12,8},{16,20},{20,16},{24,28},{28,24},{1,5},{5... | collective-permute-start | bytes 2359304 | tf_op jit(solution)/shard_map/ppermute | solution.py:739
  87.1 18.5 %collective-permute-start.19 = (bf16[2,2,2,2,3,32,512]{6,5,4,3,2,1,0:T(8,128)(2,1)S(1)}, bf16[2,2,2,2,3,32,512]{6,5,4,3,2,1,0:T(8,128)(2,1)}, u32[]{:S(2)}, u32[]{:S(2)}) collective-permute-start(bf16[2,2,2,2,3,32,512]{6,5,4,3,2,1,0:T(8,128)(2,1)S(1)} %pad_maximum_fusion.ga), channel_id=1, source_target_pairs={{0,1},{1,0},{2,3},{3,2},{4,5},{5,4},{6,7},{7,6},{8,9},{9,8},{10,11... | collective-permute-start | bytes 4718600 | tf_op jit(solution)/shard_map/ppermute | solution.py:744
  87.2 18.4 %collective-permute-start.20 = (bf16[2,2,2,2,3,32,512]{6,5,4,3,2,1,0:T(8,128)(2,1)S(1)}, bf16[2,2,2,2,3,32,512]{6,5,4,3,2,1,0:T(8,128)(2,1)}, u32[]{:S(2)}, u32[]{:S(2)}) collective-permute-start(bf16[2,2,2,2,3,32,512]{6,5,4,3,2,1,0:T(8,128)(2,1)S(1)} %pad_maximum_fusion.1.gb), channel_id=1, source_target_pairs={{0,1},{1,0},{2,3},{3,2},{4,5},{5,4},{6,7},{7,6},{8,9},{9,8},{10,11... | collective-permute-start | bytes 4718600 | tf_op jit(solution)/shard_map/ppermute | solution.py:744
  87.7 15.5 %collective-permute-start.16 = (bf16[2,2,96,512]{3,2,1,0:T(8,128)(2,1)}, bf16[2,2,96,512]{3,2,1,0:T(8,128)(2,1)}, u32[]{:S(2)}, u32[]{:S(2)}) collective-permute-start(bf16[2,2,96,512]{3,2,1,0:T(8,128)(2,1)} %get-tuple-element.153), channel_id=1, source_target_pairs={{0,4},{4,0},{8,12},{12,8},{16,20},{20,16},{24,28},{28,24},{1,5},{5... | collective-permute-start | bytes 1179656 | tf_op jit(solution)/shard_map/ppermute | solution.py:739
  88.2 16.2 %collective-permute-start.17 = (bf16[2,2,96,512]{3,2,1,0:T(8,128)(2,1)}, bf16[2,2,96,512]{3,2,1,0:T(8,128)(2,1)}, u32[]{:S(2)}, u32[]{:S(2)}) collective-permute-start(bf16[2,2,96,512]{3,2,1,0:T(8,128)(2,1)} %get-tuple-element.154), channel_id=1, source_target_pairs={{0,2},{1,3},{2,0},{3,1},{4,6},{5,7},{6,4},{7,5},{8,10},{9,11},{10,... | collective-permute-start | bytes 1179656 | tf_op jit(solution)/shard_map/ppermute | solution.py:744
  105.6 21.9 %collective-permute-start.21 = (bf16[2,2,2,96,512]{4,3,2,1,0:T(8,128)(2,1)S(1)}, bf16[2,2,2,96,512]{4,3,2,1,0:T(8,128)(2,1)S(1)}, u32[]{:S(2)}, u32[]{:S(2)}) collective-permute-start(bf16[2,2,2,96,512]{4,3,2,1,0:T(8,128)(2,1)S(1)} %pad_maximum_fusion.8), channel_id=1, source_target_pairs={{0,2},{1,3},{2,0},{3,1},{4,6},{5,7},{6,4},{7,5},{8,10},{9,11},{10,... | collective-permute-start | bytes 2359304 | tf_op jit(solution)/shard_map/ppermute | solution.py:744
  106.4 21.3 %collective-permute-start.22 = (bf16[2,2,2,96,512]{4,3,2,1,0:T(8,128)(2,1)S(1)}, bf16[2,2,2,96,512]{4,3,2,1,0:T(8,128)(2,1)S(1)}, u32[]{:S(2)}, u32[]{:S(2)}) collective-permute-start(bf16[2,2,2,96,512]{4,3,2,1,0:T(8,128)(2,1)S(1)} %pad_maximum_fusion.9), channel_id=1, source_target_pairs={{0,4},{4,0},{8,12},{12,8},{16,20},{20,16},{24,28},{28,24},{1,5},{5... | collective-permute-start | bytes 2359304 | tf_op jit(solution)/shard_map/ppermute | solution.py:739
  107.8 19.6 %collective-permute-start.23 = (bf16[2,2,96,256]{3,2,1,0:T(8,128)(2,1)S(1)}, bf16[2,2,96,256]{3,2,1,0:T(8,128)(2,1)S(1)}, u32[]{:S(2)}, u32[]{:S(2)}) collective-permute-start(bf16[2,2,96,256]{3,2,1,0:T(8,128)(2,1)S(1)} %pad_maximum_fusion.30), channel_id=1, source_target_pairs={{0,8},{4,12},{8,0},{12,4},{16,24},{20,28},{24,16},{28,20},{1,9},{5... | collective-permute-start | bytes 589832 | tf_op jit(solution)/shard_map/ppermute | solution.py:739
  135.7 16.2 %collective-permute-start.28 = (bf16[2,2,2,96,256]{4,3,2,1,0:T(8,128)(2,1)S(1)}, bf16[2,2,2,96,256]{4,3,2,1,0:T(8,128)(2,1)S(1)}, u32[]{:S(2)}, u32[]{:S(2)}) collective-permute-start(bf16[2,2,2,96,256]{4,3,2,1,0:T(8,128)(2,1)S(1)} %pad_maximum_fusion.19), channel_id=1, source_target_pairs={{0,2},{1,3},{2,0},{3,1},{4,6},{5,7},{6,4},{7,5},{8,10},{9,11},{10,... | collective-permute-start | bytes 1179656 | tf_op jit(solution)/shard_map/ppermute | solution.py:744
  137.1 14.9 %collective-permute-start.29 = (bf16[2,2,2,96,256]{4,3,2,1,0:T(8,128)(2,1)S(1)}, bf16[2,2,2,96,256]{4,3,2,1,0:T(8,128)(2,1)S(1)}, u32[]{:S(2)}, u32[]{:S(2)}) collective-permute-start(bf16[2,2,2,96,256]{4,3,2,1,0:T(8,128)(2,1)S(1)} %pad_maximum_fusion.20), channel_id=1, source_target_pairs={{0,4},{4,0},{8,12},{12,8},{16,20},{20,16},{24,28},{28,24},{1,5},{5... | collective-permute-start | bytes 1179656 | tf_op jit(solution)/shard_map/ppermute | solution.py:739
  197.9 24.2 %collective-permute-start.33 = (bf16[2,2,2,2,96,768]{5,4,3,2,1,0:T(8,128)(2,1)}, bf16[2,2,2,2,96,768]{5,4,3,2,1,0:T(8,128)(2,1)S(1)}, u32[]{:S(2)}, u32[]{:S(2)}) collective-permute-start(bf16[2,2,2,2,96,768]{5,4,3,2,1,0:T(8,128)(2,1)} %get-tuple-element.203), channel_id=1, source_target_pairs={{0,1},{1,0},{2,3},{3,2},{4,5},{5,4},{6,7},{7,6},{8,9},{9,8},{10,11... | collective-permute-start | bytes 7077896 | tf_op jit(solution)/shard_map/ppermute | solution.py:744
  199.9 44.8 %collective-permute-start.35 = (bf16[2,2,2,96,768]{4,3,2,1,0:T(8,128)(2,1)S(1)}, bf16[2,2,2,96,768]{4,3,2,1,0:T(8,128)(2,1)}, u32[]{:S(2)}, u32[]{:S(2)}) collective-permute-start(bf16[2,2,2,96,768]{4,3,2,1,0:T(8,128)(2,1)S(1)} %fusion), channel_id=1, source_target_pairs={{0,4},{4,0},{8,12},{12,8},{16,20},{20,16},{24,28},{28,24},{1,5},{5... | collective-permute-start | bytes 3538952 | tf_op jit(solution)/shard_map/ppermute | solution.py:739
  225.6 28.0 %collective-permute-start.36 = (bf16[2,2,2,96,768]{4,3,2,1,0:T(8,128)(2,1)}, bf16[2,2,2,96,768]{4,3,2,1,0:T(8,128)(2,1)}, u32[]{:S(2)}, u32[]{:S(2)}) collective-permute-start(bf16[2,2,2,96,768]{4,3,2,1,0:T(8,128)(2,1)} %fusion.1), channel_id=1, source_target_pairs={{0,2},{1,3},{2,0},{3,1},{4,6},{5,7},{6,4},{7,5},{8,10},{9,11},{10,... | collective-permute-start | bytes 3538952 | tf_op jit(solution)/shard_map/ppermute | solution.py:744
  226.3 18.4 %collective-permute-start.34 = (f32[4,768]{1,0:T(4,128)S(1)}, f32[4,768]{1,0:T(4,128)S(1)}, u32[]{:S(2)}, u32[]{:S(2)}) collective-permute-start(f32[4,768]{1,0:T(4,128)S(1)} %pad_maximum_fusion.35), channel_id=1, source_target_pairs={{0,1},{1,0},{2,3},{3,2},{4,5},{5,4},{6,7},{7,6},{8,9},{9,8},{10,11... | collective-permute-start | bytes 36872 | tf_op jit(solution)/shard_map/ppermute | solution.py:827
  253.6 20.4 %collective-permute-start.38 = (bf16[2,2,2,2,3,32,512]{6,5,4,3,2,1,0:T(8,128)(2,1)}, bf16[2,2,2,2,3,32,512]{6,5,4,3,2,1,0:T(8,128)(2,1)S(1)}, u32[]{:S(2)}, u32[]{:S(2)}) collective-permute-start(bf16[2,2,2,2,3,32,512]{6,5,4,3,2,1,0:T(8,128)(2,1)} %get-tuple-element.223), channel_id=1, source_target_pairs={{0,1},{1,0},{2,3},{3,2},{4,5},{5,4},{6,7},{7,6},{8,9},{9,8},{10,11... | collective-permute-start | bytes 4718600 | tf_op jit(solution)/shard_map/ppermute | solution.py:744
  253.6 20.4 %collective-permute-start.39 = (bf16[2,2,2,2,3,32,512]{6,5,4,3,2,1,0:T(8,128)(2,1)}, bf16[2,2,2,2,3,32,512]{6,5,4,3,2,1,0:T(8,128)(2,1)S(1)}, u32[]{:S(2)}, u32[]{:S(2)}) collective-permute-start(bf16[2,2,2,2,3,32,512]{6,5,4,3,2,1,0:T(8,128)(2,1)} %get-tuple-element.224), channel_id=1, source_target_pairs={{0,1},{1,0},{2,3},{3,2},{4,5},{5,4},{6,7},{7,6},{8,9},{9,8},{10,11... | collective-permute-start | bytes 4718600 | tf_op jit(solution)/shard_map/ppermute | solution.py:744
  257.5 15.3 %collective-permute-start.41 = (bf16[2,2,96,768]{3,2,1,0:T(8,128)(2,1)S(1)}, bf16[2,2,96,768]{3,2,1,0:T(8,128)(2,1)S(1)}, u32[]{:S(2)}, u32[]{:S(2)}) collective-permute-start(bf16[2,2,96,768]{3,2,1,0:T(8,128)(2,1)S(1)} %fusion.4), channel_id=1, source_target_pairs={{0,4},{4,0},{8,12},{12,8},{16,20},{20,16},{24,28},{28,24},{1,5},{5... | collective-permute-start | bytes 1769480 | tf_op jit(solution)/shard_map/ppermute | solution.py:739
  259.1 15.0 %collective-permute-start.40 = (bf16[2,2,96,768]{3,2,1,0:T(8,128)(2,1)S(1)}, bf16[2,2,96,768]{3,2,1,0:T(8,128)(2,1)S(1)}, u32[]{:S(2)}, u32[]{:S(2)}) collective-permute-start(bf16[2,2,96,768]{3,2,1,0:T(8,128)(2,1)S(1)} %fusion.5), channel_id=1, source_target_pairs={{0,2},{1,3},{2,0},{3,1},{4,6},{5,7},{6,4},{7,5},{8,10},{9,11},{10,... | collective-permute-start | bytes 1769480 | tf_op jit(solution)/shard_map/ppermute | solution.py:744
  274.0 27.2 %collective-permute-start.43 = (bf16[2,2,2,2,96,384]{5,4,3,2,1,0:T(8,128)(2,1)}, bf16[2,2,2,2,96,384]{5,4,3,2,1,0:T(8,128)(2,1)S(1)}, u32[]{:S(2)}, u32[]{:S(2)}) collective-permute-start(bf16[2,2,2,2,96,384]{5,4,3,2,1,0:T(8,128)(2,1)} %get-tuple-element.234), channel_id=1, source_target_pairs={{0,1},{1,0},{2,3},{3,2},{4,5},{5,4},{6,7},{7,6},{8,9},{9,8},{10,11... | collective-permute-start | bytes 3538952 | tf_op jit(solution)/shard_map/ppermute | solution.py:744
  274.1 27.1 %collective-permute-start.44 = (bf16[2,2,2,2,96,384]{5,4,3,2,1,0:T(8,128)(2,1)}, bf16[2,2,2,2,96,384]{5,4,3,2,1,0:T(8,128)(2,1)}, u32[]{:S(2)}, u32[]{:S(2)}) collective-permute-start(bf16[2,2,2,2,96,384]{5,4,3,2,1,0:T(8,128)(2,1)} %get-tuple-element.235), channel_id=1, source_target_pairs={{0,1},{1,0},{2,3},{3,2},{4,5},{5,4},{6,7},{7,6},{8,9},{9,8},{10,11... | collective-permute-start | bytes 3538952 | tf_op jit(solution)/shard_map/ppermute | solution.py:744
  278.9 22.3 %collective-permute-start.45 = (bf16[2,2,96,768]{3,2,1,0:T(8,128)(2,1)S(1)}, bf16[2,2,96,768]{3,2,1,0:T(8,128)(2,1)S(1)}, u32[]{:S(2)}, u32[]{:S(2)}) collective-permute-start(bf16[2,2,96,768]{3,2,1,0:T(8,128)(2,1)S(1)} %pad_maximum_fusion.14), channel_id=1, source_target_pairs={{0,8},{4,12},{8,0},{12,4},{16,24},{20,28},{24,16},{28,20},{1,9},{5... | collective-permute-start | bytes 1769480 | tf_op jit(solution)/shard_map/ppermute | solution.py:739
  279.0 22.2 %collective-permute-start.42 = (f32[4,768]{1,0:T(4,128)S(1)}, f32[4,768]{1,0:T(4,128)S(1)}, u32[]{:S(2)}, u32[]{:S(2)}) collective-permute-start(f32[4,768]{1,0:T(4,128)S(1)} %add.265), channel_id=1, source_target_pairs={{0,16},{4,20},{8,24},{12,28},{16,0},{20,4},{24,8},{28,12},{1,17},{... | collective-permute-start | bytes 36872 | tf_op jit(solution)/shard_map/ppermute | solution.py:827
  301.2 19.0 %collective-permute-start.47 = (bf16[2,2,2,3,32,512]{5,4,3,2,1,0:T(8,128)(2,1)}, bf16[2,2,2,3,32,512]{5,4,3,2,1,0:T(8,128)(2,1)S(1)}, u32[]{:S(2)}, u32[]{:S(2)}) collective-permute-start(bf16[2,2,2,3,32,512]{5,4,3,2,1,0:T(8,128)(2,1)} %get-tuple-element.245), channel_id=1, source_target_pairs={{0,2},{1,3},{2,0},{3,1},{4,6},{5,7},{6,4},{7,5},{8,10},{9,11},{10,... | collective-permute-start | bytes 2359304 | tf_op jit(solution)/shard_map/ppermute | solution.py:744
  302.0 18.7 %collective-permute-start.48 = (bf16[2,2,2,3,32,512]{5,4,3,2,1,0:T(8,128)(2,1)}, bf16[2,2,2,3,32,512]{5,4,3,2,1,0:T(8,128)(2,1)S(1)}, u32[]{:S(2)}, u32[]{:S(2)}) collective-permute-start(bf16[2,2,2,3,32,512]{5,4,3,2,1,0:T(8,128)(2,1)} %get-tuple-element.246), channel_id=1, source_target_pairs={{0,4},{4,0},{8,12},{12,8},{16,20},{20,16},{24,28},{28,24},{1,5},{5... | collective-permute-start | bytes 2359304 | tf_op jit(solution)/shard_map/ppermute | solution.py:739
  304.0 14.7 %collective-permute-start.46 = (bf16[2,96,768]{2,1,0:T(8,128)(2,1)S(1)}, bf16[2,96,768]{2,1,0:T(8,128)(2,1)S(1)}, u32[]{:S(2)}, u32[]{:S(2)}) collective-permute-start(bf16[2,96,768]{2,1,0:T(8,128)(2,1)S(1)} %pad_maximum_fusion.24), channel_id=1, source_target_pairs={{0,16},{4,20},{8,24},{12,28},{16,0},{20,4},{24,8},{28,12},{1,17},{... | collective-permute-start | bytes 884744 | tf_op jit(solution)/shard_map/ppermute | solution.py:739
  320.8 17.1 %collective-permute-start.52 = (bf16[2,2,3,32,512]{4,3,2,1,0:T(8,128)(2,1)S(1)}, bf16[2,2,3,32,512]{4,3,2,1,0:T(8,128)(2,1)}, u32[]{:S(2)}, u32[]{:S(2)}) collective-permute-start(bf16[2,2,3,32,512]{4,3,2,1,0:T(8,128)(2,1)S(1)} %fusion.7), channel_id=1, source_target_pairs={{0,2},{1,3},{2,0},{3,1},{4,6},{5,7},{6,4},{7,5},{8,10},{9,11},{10,... | collective-permute-start | bytes 1179656 | tf_op jit(solution)/shard_map/ppermute | solution.py:744
  322.2 22.0 %collective-permute-start.49 = (bf16[2,2,2,96,384]{4,3,2,1,0:T(8,128)(2,1)S(1)}, bf16[2,2,2,96,384]{4,3,2,1,0:T(8,128)(2,1)S(1)}, u32[]{:S(2)}, u32[]{:S(2)}) collective-permute-start(bf16[2,2,2,96,384]{4,3,2,1,0:T(8,128)(2,1)S(1)} %get-tuple-element.254), channel_id=1, source_target_pairs={{0,2},{1,3},{2,0},{3,1},{4,6},{5,7},{6,4},{7,5},{8,10},{9,11},{10,... | collective-permute-start | bytes 1769480 | tf_op jit(solution)/shard_map/ppermute | solution.py:744
  322.9 21.3 %collective-permute-start.50 = (bf16[2,2,2,96,384]{4,3,2,1,0:T(8,128)(2,1)S(1)}, bf16[2,2,2,96,384]{4,3,2,1,0:T(8,128)(2,1)S(1)}, u32[]{:S(2)}, u32[]{:S(2)}) collective-permute-start(bf16[2,2,2,96,384]{4,3,2,1,0:T(8,128)(2,1)S(1)} %get-tuple-element.255), channel_id=1, source_target_pairs={{0,4},{4,0},{8,12},{12,8},{16,20},{20,16},{24,28},{28,24},{1,5},{5... | collective-permute-start | bytes 1769480 | tf_op jit(solution)/shard_map/ppermute | solution.py:739
  324.3 19.9 %collective-permute-start.51 = (bf16[2,2,3,32,512]{4,3,2,1,0:T(8,128)(2,1)}, bf16[2,2,3,32,512]{4,3,2,1,0:T(8,128)(2,1)}, u32[]{:S(2)}, u32[]{:S(2)}) collective-permute-start(bf16[2,2,3,32,512]{4,3,2,1,0:T(8,128)(2,1)} %fusion.6), channel_id=1, source_target_pairs={{0,4},{4,0},{8,12},{12,8},{16,20},{20,16},{24,28},{28,24},{1,5},{5... | collective-permute-start | bytes 1179656 | tf_op jit(solution)/shard_map/ppermute | solution.py:739
  (82 other events, 796.4 us)
where the time goes:
time: 382 us; the launch traced here: 378 us
  Pallas kernels  171 us (45%)
  waiting for transfers between devices  96.2 us (25%)
  starting transfers between devices  61.6 us (16%)
  other arithmetic  32.8 us (9%)
  local copies, waits for them, and re-layouts  14.4 us (4%)
    ppermute x28, waiting for transfers between devices, partner_dp(): return lax.ppermute(value, 'dp', [(i, i ^ step) for i in range(size)])  72.9 us
    ppermute x28, starting transfers between devices, partner_dp(): return lax.ppermute(value, 'dp', [(i, i ^ step) for i in range(size)])  38.8 us
    pallas_call x2, Pallas kernels, attention_backward(): pl.pallas_call(functools.partial(att_bwd_kernel, last), out_shape=out_sha...  37.8 us
    pallas_call x2, Pallas kernels, ffn_backward(): pl.pallas_call(functools.partial(ffn_bwd_kernel, chunk, last), out_shape=...  35.2 us
    ppermute x28, waiting for transfers between devices, partner_head(): return lax.ppermute(value, 'head', [(i, i ^ 1 << bit) for i in range(size)])  21.8 us
    pallas_call x2, Pallas kernels, attention_forward(): pl.pallas_call(att_fwd_kernel, out_shape=(sds((2, rows, w1), BF16), sds((...  18.6 us
    ppermute x28, starting transfers between devices, partner_head(): return lax.ppermute(value, 'head', [(i, i ^ 1 << bit) for i in range(size)])  18.6 us
    pallas_call x1, Pallas kernels, ffn_rest(): pl.pallas_call(functools.partial(ffn_rest_kernel, chunk), out_shape=(sds(...  15.4 us
  transfers between devices with their start and end apart: 61, of which 25 were waited for; matrix products, arithmetic and copies ran while one was open for 9% of the time, Pallas kernels for 39%

commit v1 on v0

--- a/solution.py
+++ b/solution.py
@@ -102,14 +102,14 @@
     return up * cdf, cdf + up * pdf
 
 
-SHARE = 200
+SHARE = 10
 
 
 def cost(flops, moved):
-    return pl.CostEstimate(flops=flops // SHARE, bytes_accessed=moved // SHARE, transcendentals=0)
-
-
-def params(mib=56, n=1):
+    return pl.CostEstimate(flops=flops * SHARE, bytes_accessed=moved * SHARE, transcendentals=0)
+
+
+def params(mib=60, n=1):
     return pltpu.CompilerParams(
         dimension_semantics=("arbitrary",) * n, vmem_limit_bytes=mib * 1024 * 1024
     )
@@ -167,7 +167,7 @@
             out_specs=[col, col, whole((rows, width))],
             scratch_shapes=[pltpu.VMEM((width, n), BF16), pltpu.VMEM((width, n), BF16)],
         ),
-        compiler_params=params(48),
+        compiler_params=params(32),
         cost_estimate=cost(4 * rows * width * 4 * n, 16 * rows * width),
     )(bits, hid, ua0, ua1, db0, db1)
 
@@ -232,7 +232,7 @@
             scratch_shapes=[pltpu.VMEM((width, n), BF16), pltpu.VMEM((width, n), BF16), pltpu.VMEM((rows, width), F32)],
         ),
         input_output_aliases={11: 0, 12: 1},
-        compiler_params=params(48),
+        compiler_params=params(46),
         cost_estimate=cost(4 * rows * width * 4 * n, 20 * rows * width),
     )(bits, lens, hid, ua0, ua1, db0, db1, part, gain, bias, dout, act, gp)
 
@@ -268,7 +268,7 @@
             in_specs=[whole((width, rows)), pl.BlockSpec((1, rows, n), lambda k, *_: (k, 0, 0))],
             out_specs=[spec_b((p, n), low_pick), spec_b((p, n), high_pick)],
         ),
-        compiler_params=params(40),
+        compiler_params=params(22),
         cost_estimate=cost(2 * rows * width * 4 * n, 14 * rows * width),
     )(bits, dt, act)
 
@@ -435,7 +435,7 @@
                 pl.BlockSpec((1, length, heads), lambda k, s, *_: (k, s, 0)),
             ],
         ),
-        compiler_params=params(n=2),
+        compiler_params=params(30, 2),
         cost_estimate=cost(16 * 2 * rows * length * w1, 16 * rows * w1),
     )(bits, lens, qk, v, ga, gb)
 
@@ -563,7 +563,7 @@
                 pltpu.VMEM((w1, length), BF16), pltpu.VMEM((heads, length, keys), F32),
             ],
         ),
-        compiler_params=params(n=2),
+        compiler_params=params(36, 2),
         cost_estimate=cost(40 * 2 * rows * length * w1, 30 * rows * w1),
     )(bits, lens, qk, v, ga, gb, lse, dattn, wo, *got)
 
@@ -605,7 +605,7 @@
             + ([whole((width, rows))] if first else []),
             scratch_shapes=[pltpu.VMEM((width, w2), BF16)],
         ),
-        compiler_params=params(),
+        compiler_params=params(24),
         cost_estimate=cost(2 * rows * width * 2 * (w1 + w2), 8 * rows * width),
     )(bits, x, wa, wb)
 
@@ -632,7 +632,7 @@
         out_shape=(sds((rows, width), BF16), sds((rows, width), F32), sds((rows, 1), F32), sds((width, rows), BF16)),
         in_specs=[row(width), mix, mix, whole((2, width, w1)), whole((2, width, w1)), whole((1, width)), whole((1, width))],
         out_specs=[row(width), row(width), row(1), pl.BlockSpec((width, block), lambda r: (0, r))],
-        compiler_params=params(),
+        compiler_params=params(20),
         cost_estimate=cost(2 * rows * width * 4 * w1, 12 * rows * width),
     )(x, m0, m1, wo0, wo1, gain, bias)
 
@@ -699,7 +699,7 @@
             num_scalar_prefetch=1, grid=(2,), in_specs=in_specs, out_specs=out_specs,
             scratch_shapes=[pltpu.VMEM((width, w2), kind), pltpu.VMEM((width, w2), kind)],
         ),
-        compiler_params=params(40),
+        compiler_params=params(26),
         cost_estimate=cost(2 * rows * width * 2 * 2 * w2, 8 * rows * width),
     )(bits, xt, dat, dqk, dv, mixed, *got)
 
@@ -725,7 +725,7 @@
         in_specs=[row, part(w2), part(w2), part(w1), part(w1)]
         + [whole((2, width, w2))] * 2 + [whole((2, width, w1))] * 2,
         out_specs=row,
-        compiler_params=params(),
+        compiler_params=params(24),
         cost_estimate=cost(2 * rows * width * 4 * (w1 + w2), 14 * rows * width),
     )(dfirst, dqk0, dqk1, dv0, dv1, wqk0, wqk1, wv0, wv1)
 
@@ -931,38 +931,42 @@
     xu = over_x(first_sum(up0, cu))
     norms = total_some(norms, steps[0])
     dqk1, dv1, ga1, gb1 = attention_backward(False, bits, lens, qk1, v1, ba1, bb1, lse1, dattn, wo1)
-    ga1, gb1, norms, dqk1, xd, xu = after((ga1, gb1, norms, dqk1, xd, xu), dv1)
+    ga1, gb1, norms, dqk1, xd = after((ga1, gb1, norms, dqk1, xd), dv1)
     cga, cgb = over_pair(ga1), over_pair(gb1)
     norms = total_some(norms, steps[3])
+    qka1, vo1 = qkv_grads(False, bits, xt, dattnt, dqk1, dv1, m1)
+    qka1, vo1, dattn, norms, cga, cgb, xu, xd = after((qka1, vo1, dattn, norms, cga, cgb, xu, xd), vo1)
+    cqk, cvo = over_pair(qka1), over_pair(vo1)
+    norms = total_some(norms, steps[4])
     yd, yu = over_x(second_sum(down0, cd, xd)), over_y(second_sum(up0, cu, xu))
-    qka1, vo1 = qkv_grads(False, bits, xt, dattnt, dqk1, dv1, m1)
-    qka1, vo1, dattn, norms, cga, cgb, yd, yu = after((qka1, vo1, dattn, norms, cga, cgb, yd, yu), vo1)
-    cqk, cvo = over_pair(qka1), over_pair(vo1)
-    u, d = third_sum(up0, cu, xu, yu), third_sum(down0, cd, xd, yd)
-    near_f = over_near(jnp.stack([u[1], d[1]]).astype(BF16))
-    norms = total_some(norms, steps[4])
     dqk0, dv0, ga0, ga_out, gb0, gb_out = attention_backward(
         True, bits, lens, qk0, v0, ba, bb, lse0, dattn, wo0, (cga, cgb)
     )
-    ga_out, gb_out, dqk0, norms, cqk, cvo, near_f = after((ga_out, gb_out, dqk0, norms, cqk, cvo, near_f), dv0)
+    ga_out, gb_out, dqk0, norms, cqk, cvo, yd, yu = after((ga_out, gb_out, dqk0, norms, cqk, cvo, yd, yu), dv0)
     xga, xgb = over_x(ga_out), over_y(gb_out)
-    far_f = over_far(jnp.stack([u[0, 1] + wide(near_f[0, 1]), d[0, 1] + wide(near_f[1, 1])]).astype(BF16))
+    u, d = third_sum(up0, cu, xu, yu), third_sum(down0, cd, xd, yd)
+    near_f = over_near(jnp.stack([u[1], d[1]]).astype(BF16))
     qka0, qka_out, vo0, vo_out = qkv_grads(True, bits, xt, dattnt, dqk0, dv0, m0, (cqk, cvo))
-    qka_out, vo_out, far_f, xga, xgb, dqk0 = after((qka_out, vo_out, far_f, xga, xgb, dqk0), vo0)
+    qka_out, vo_out, near_f, xga, xgb, dqk0 = after((qka_out, vo_out, near_f, xga, xgb, dqk0), vo0)
     xqk, xvo = over_x(qka_out), over_y(vo_out)
     yga, ygb = over_y(low_sum(ga0, xga)), over_x(low_sum(gb0, xgb))
+    far_f = over_far(jnp.stack([u[0, 1] + wide(near_f[0, 1]), d[0, 1] + wide(near_f[1, 1])]).astype(BF16))
     dinput = input_backward(dfirst, dqk0, dqk1, dv0, dv1, wqk0, wqk1, wv0, wv1)
-    xqk, xvo, yga, ygb, norms = after((xqk, xvo, yga, ygb, norms), dinput)
-    yqk, yvo = over_y(low_sum(qka0, xqk)), over_x(low_sum(vo0, xvo))
+    xqk, xvo, yga, ygb, norms, far_f = after((xqk, xvo, yga, ygb, norms, far_f), dinput)
+    norms = total_some(norms, steps[1])
+    send_qk, send_vo = low_sum(qka0, xqk), low_sum(vo0, xvo)
     g1, g2 = high_sum(ga0, xga, yga), high_sum(gb0, xgb, ygb)
-    near_g = over_near(jnp.stack([g1[1], g2[1]]).astype(BF16))
+    send_g = jnp.stack([g1[1], g2[1]]).astype(BF16)
+    send_qk, send_vo, send_g, norms = after((send_qk, send_vo, send_g, norms), norms)
+    yqk, yvo = over_y(send_qk), over_x(send_vo)
+    near_g = over_near(send_g)
     norms, = after((norms,), yqk, yvo)
-    norms = total_some(norms, steps[1])
+    norms = total_some(norms, *steps[2:3], *steps[5:])
     w1, w2 = high_sum(qka0, xqk, yqk), high_sum(vo0, xvo, yvo)
-    near_w = over_near(jnp.stack([w1[1], w2[1]]).astype(BF16))
-    far_g = over_far(jnp.stack([g1[0, 1] + wide(near_g[0, 1]), g2[0, 1] + wide(near_g[1, 1])]).astype(BF16))
-    norms, = after((norms,), near_w)
-    norms = total_some(norms, *steps[2:3], *steps[5:])
+    send_w = jnp.stack([w1[1], w2[1]]).astype(BF16)
+    send_g = jnp.stack([g1[0, 1] + wide(near_g[0, 1]), g2[0, 1] + wide(near_g[1, 1])]).astype(BF16)
+    near_w = over_near(send_w)
+    far_g = over_far(send_g)
     far_w = over_far(jnp.stack([w1[0, 1] + wide(near_w[0, 1]), w2[0, 1] + wide(near_w[1, 1])]).astype(BF16))
 
     up_grad = u[0, 0] + wide(near_f[0, 0]) + wide(far_f[0])

time: 382 us -> 356 us (0.932)
  Pallas kernels: 171 us -> 140 us
  other arithmetic: 32.8 us -> 24 us
  waiting for transfers between devices: 96.2 us -> 104 us
  local copies, waits for them, and re-layouts: 14.4 us -> 20.3 us
    ppermute x28, waiting for transfers between devices: 21.8 us -> 38.5 us  [partner_head(): return lax.ppermute(value, 'head', [(i, i ^ 1 << bit) for i in range(size)])]
    ppermute x28, waiting for transfers between devices: 72.9 us -> 62.3 us  [partner_dp(): return lax.ppermute(value, 'dp', [(i, i ^ step) for i in range(size)])]
    unnamed x108 -> x160, local copies, waits for them, and re-layouts: 9.81 us -> 18.3 us
    pallas_call x2, Pallas kernels: 37.8 us -> 29.4 us  [attention_backward(): pl.pallas_call(functools.partial(att_bwd_kernel, last), out_shape=out_sha...]
    pallas_call x2, Pallas kernels: 14.8 us -> 8.32 us  [project(): pl.pallas_call(functools.partial(qkv_kernel, first), out_shape=[sds((2, r...]
    pallas_call x2, Pallas kernels: 18.6 us -> 13.1 us  [attention_forward(): pl.pallas_call(att_fwd_kernel, out_shape=(sds((2, rows, w1), BF16), sds((...]
  transfers between devices with their start and end apart: 61 -> 61, of which waited for: 25 -> 32; matrix products, arithmetic and copies ran while one was open for 9% -> 5% of each run, Pallas kernels for 39% -> 34%
where the time goes in v1:
time: 356 us; the launch traced here: 353 us
  Pallas kernels  140 us (39%)
  waiting for transfers between devices  104 us (29%)
  starting transfers between devices  61.7 us (17%)
  other arithmetic  24 us (7%)
  local copies, waits for them, and re-layouts  20.3 us (6%)
    ppermute x28, waiting for transfers between devices, partner_dp(): return lax.ppermute(value, 'dp', [(i, i ^ step) for i in range(size)])  62.3 us
    ppermute x28, waiting for transfers between devices, partner_head(): return lax.ppermute(value, 'head', [(i, i ^ 1 << bit) for i in range(size)])  38.5 us
    ppermute x28, starting transfers between devices, partner_dp(): return lax.ppermute(value, 'dp', [(i, i ^ step) for i in range(size)])  36.2 us
    pallas_call x2, Pallas kernels, ffn_backward(): pl.pallas_call(functools.partial(ffn_bwd_kernel, chunk, last), out_shape=...  35.2 us
    pallas_call x2, Pallas kernels, attention_backward(): pl.pallas_call(functools.partial(att_bwd_kernel, last), out_shape=out_sha...  29.4 us
    ppermute x28, starting transfers between devices, partner_head(): return lax.ppermute(value, 'head', [(i, i ^ 1 << bit) for i in range(size)])  19 us
    unnamed x160, local copies, waits for them, and re-layouts  18.3 us
    pallas_call x1, Pallas kernels, ffn_rest(): pl.pallas_call(functools.partial(ffn_rest_kernel, chunk), out_shape=(sds(...  14.3 us
  transfers between devices with their start and end apart: 61, of which 32 were waited for; matrix products, arithmetic and copies ran while one was open for 5% of the time, Pallas kernels for 34%

profile of v1, /device:TPU:0, one launch (start us, length us, event | category | flops | bytes accessed | tf_op | source)
XLA Modules:
  0.0 352.8 jit_solution(8089648494425312440)
XLA Ops:
  2.6 4.1 %collective-permute-start = (bf16[2,96,384]{2,1,0:T(8,128)(2,1)S(1)}, bf16[2,96,384]{2,1,0:T(8,128)(2,1)S(1)}, u32[]{:S(2)}, u32[]{:S(2)}) collective-permute-start(bf16[2,96,384]{2,1,0:T(8,128)(2,1)S(1)} %get-tuple-element.319), channel_id=1, source_target_pairs={{0,16},{4,20},{8,24},{12,28},{16,0},{20,4},{24,8},{28,12},{1,17},{... | collective-permute-start | bytes 442376 | tf_op jit(solution)/shard_map/ppermute | solution.py:739
  8.0 5.8 %collective-permute-done = bf16[2,96,384]{2,1,0:T(8,128)(2,1)S(1)} collective-permute-done((bf16[2,96,384]{2,1,0:T(8,128)(2,1)S(1)}, bf16[2,96,384]{2,1,0:T(8,128)(2,1)S(1)}, u32[]{:S(2)}, u32[]{:S(2)}) %collective-permute-start) | collective-permute-done | bytes 147488 | tf_op jit(solution)/shard_map/ppermute | solution.py:739
  14.6 7.4 %collective-permute-done.1 = bf16[2,2,96,384]{3,2,1,0:T(8,128)(2,1)S(1)} collective-permute-done((bf16[2,2,96,384]{3,2,1,0:T(8,128)(2,1)S(1)}, bf16[2,2,96,384]{3,2,1,0:T(8,128)(2,1)S(1)}, u32[]{:S(2)}, u32[]{:S(2)}) %collective-permute-start.1) | collective-permute-done | bytes 294944 | tf_op jit(solution)/shard_map/ppermute | solution.py:739
  25.0 3.4 collective-permute-start.4
  30.7 6.0 %collective-permute-done.4 = bf16[2,3,32,512]{3,2,1,0:T(8,128)(2,1)S(1)} collective-permute-done((bf16[2,3,32,512]{3,2,1,0:T(8,128)(2,1)S(1)}, bf16[2,3,32,512]{3,2,1,0:T(8,128)(2,1)S(1)}, u32[]{:S(2)}, u32[]{:S(2)}) %collective-permute-start.4) | collective-permute-done | bytes 196640 | tf_op jit(solution)/shard_map/ppermute | solution.py:739
  38.9 8.6 %collective-permute-done.5 = bf16[2,2,3,32,512]{4,3,2,1,0:T(8,128)(2,1)} collective-permute-done((bf16[2,2,3,32,512]{4,3,2,1,0:T(8,128)(2,1)S(1)}, bf16[2,2,3,32,512]{4,3,2,1,0:T(8,128)(2,1)}, u32[]{:S(2)}, u32[]{:S(2)}) %collective-permute-start.5) | collective-permute-done | bytes 393248 | tf_op jit(solution)/shard_map/ppermute | solution.py:739
  56.5 4.6 %shard_map.178 = (bf16[2,1024,384]{2,1,0:T(8,128)(2,1)S(1)}, bf16[2,1024,192]{2,1,0:T(8,128)(2,1)S(1)}, bf16[2,768,384]{2,1,0:T(8,128)(2,1)S(1)}, bf16[2,768,192...) custom-call(s32[3]{0:T(128)S(1)} %pad_add_fusion.bits, ...), custom_call_target="tpu_custom_call" | custom-call | flops 18119393280 | bytes 62914560 | tf_op jit(solution)/shard_map/pallas_call | solution.py:596
  67.1 3.7 %shard_map.179 = (bf16[2,1024,384]{2,1,0:T(8,128)(2,1)S(1)}, bf16[2,1024,192]{2,1,0:T(8,128)(2,1)S(1)}, bf16[2,768,384]{2,1,0:T(8,128)(2,1)S(1)}, bf16[2,768,192...) custom-call(s32[3]{0:T(128)S(1)} %pad_add_fusion.bits, bf16[1024,768]{1,0:T(8,128)(2,1)S(1)} %bitcast.222, ...), custom_call_target="tpu_custom_call" | custom-call | flops 18119393280 | bytes 62914560 | tf_op jit(solution)/shard_map/pallas_call | solution.py:596
  74.8 9.8 %collective-permute-done.14 = bf16[2,2,2,3,32,512]{5,4,3,2,1,0:T(8,128)(2,1)S(1)} collective-permute-done((bf16[2,2,2,3,32,512]{5,4,3,2,1,0:T(8,128)(2,1)S(1)}, bf16[2,2,2,3,32,512]{5,4,3,2,1,0:T(8,128)(2,1)S(1)}, u32[]{:S(2)}, u32[]{:S(2)}) %collective-permute-start.14) | collective-permute-done | bytes 786464 | tf_op jit(solution)/shard_map/ppermute | solution.py:744
  90.2 6.6 %shard_map.180 = (bf16[2,1024,192]{2,1,0:T(8,128)(2,1)S(1)}, f32[2,1024,3]{2,1,0:T(8,128)S(1)}) custom-call(s32[3]{0:T(128)S(1)} %pad_add_fusion.bits, s32[2]{0:T(128)S(1)} %dynamic-slice_reduce_fusion.lens, bf16[2,1024,384]{2,1,0:T(8,128)(2,1)S(1)} %get-tuple-element.150.qk, bf16[2,1024,192]{2,1,0:T(8,128)(2,1)S(1)} %get-tuple-element.162.v, ...), custom_call_target="tpu_custom_call" | custom-call | flops 32212254720 | bytes 31457280 | tf_op jit(solution)/shard_map/pallas_call | solution.py:423
  99.4 6.6 %shard_map.181 = (bf16[2,1024,192]{2,1,0:T(8,128)(2,1)S(1)}, f32[2,1024,3]{2,1,0:T(8,128)S(1)}) custom-call(s32[3]{0:T(128)S(1)} %pad_add_fusion.bits, s32[2]{0:T(128)S(1)} %dynamic-slice_reduce_fusion.lens, bf16[2,1024,384]{2,1,0:T(8,128)(2,1)S(1)} %get-tuple-element.156.qk, bf16[2,1024,192]{2,1,0:T(8,128)(2,1)S(1)} %get-tuple-element.167.v, ...), custom_call_target="tpu_custom_call" | custom-call | flops 32212254720 | bytes 31457280 | tf_op jit(solution)/shard_map/pallas_call | solution.py:423
  106.1 4.0 %shard_map.182 = (bf16[1024,768]{1,0:T(8,128)(2,1)S(1)}, f32[1024,768]{1,0:T(8,128)S(1)}, f32[1024,1]{1,0:T(8,128)S(1)}, bf16[768,1024]{1,0:T(8,128)(2,1)S(1)}) custom-call(bf16[1024,768]{1,0:T(8,128)(2,1)S(1)} %bitcast.223, bf16[2,1024,192]{2,1,0:T(8,128)(2,1)S(1)} %get-tuple-element.163.m0.mixed, bf16[2,1024,192]{2,1,0:T(8,128)(2,1)S(1)} %get-tuple-element.170.m1.mixed, ...), custom_call_target="tpu_custom_call" | custom-call | flops 12079595520 | bytes 94371840 | tf_op jit(solution)/shard_map/pallas_call | solution.py:629
  111.3 6.0 %collective-permute-done.21 = bf16[2,2,2,96,512]{4,3,2,1,0:T(8,128)(2,1)S(1)} collective-permute-done((bf16[2,2,2,96,512]{4,3,2,1,0:T(8,128)(2,1)S(1)}, bf16[2,2,2,96,512]{4,3,2,1,0:T(8,128)(2,1)S(1)}, u32[]{:S(2)}, u32[]{:S(2)}) %collective-permute-start.21) | collective-permute-done | bytes 786464 | tf_op jit(solution)/shard_map/ppermute | solution.py:744
  120.3 4.9 %collective-permute-done.24 = bf16[2,2,96,256]{3,2,1,0:T(8,128)(2,1)S(1)} collective-permute-done((bf16[2,2,96,256]{3,2,1,0:T(8,128)(2,1)S(1)}, bf16[2,2,96,256]{3,2,1,0:T(8,128)(2,1)S(1)}, u32[]{:S(2)}, u32[]{:S(2)}) %collective-permute-start.24) | collective-permute-done | bytes 196640 | tf_op jit(solution)/shard_map/ppermute | solution.py:739
  128.6 11.9 %shard_map.183 = (bf16[4,1024,768]{2,1,0:T(8,128)(2,1)S(1)}, f32[4,1024,768]{2,1,0:T(8,128)}, f32[1024,768]{1,0:T(8,128)S(1)}) custom-call(s32[3]{0:T(128)S(1)} %pad_add_fusion.bits, bf16[1024,768]{1,0:T(8,128)(2,1)S(1)} %get-tuple-element.178.hid, bf16[2,2,2,2,96,512]{5,4,3,2,1,0:T(8,128)(2,1)S(1)} %pad_maximum_fusion.2.ua0.uap, ...), custom_call_target="tpu_custom_call" | custom-call | flops 64424509440 | bytes 125829120 | tf_op jit(solution)/shard_map/pallas_call | solution.py:160
  148.2 14.3 %shard_map.184 = (bf16[4,1024,768]{2,1,0:T(8,128)(2,1)}, f32[4,1024,768]{2,1,0:T(8,128)}, bf16[1024,768]{1,0:T(8,128)(2,1)}, f32[1024,768]{1,0:T(8,128)}, bf16[1...) custom-call(s32[3]{0:T(128)S(1)} %pad_add_fusion.bits, ...), custom_call_target="tpu_custom_call", output_to_operand_aliasing={{0}: (11, {}), {1}: (12, {})} | custom-call | flops 32212254720 | bytes 157286400 | tf_op jit(solution)/shard_map/pallas_call | solution.py:223
  166.0 7.0 %shard_map.185 = (bf16[2,2,2,2,96,768]{5,4,3,2,1,0:T(8,128)(2,1)S(1)}, bf16[2,2,2,2,96,768]{5,4,3,2,1,0:T(8,128)(2,1)S(1)}) custom-call(s32[3]{0:T(128)S(1)} %pad_add_fusion.bits, bf16[768,1024]{1,0:T(8,128)(2,1)S(1)} %get-tuple-element.188.dt, bf16[4,1024,768]{2,1,0:T(8,128)(2,1)S(1)} %copy-done.27), custom_call_target="tpu_custom_call" | custom-call | flops 48318382080 | bytes 110100480 | tf_op jit(solution)/shard_map/pallas_call | solution.py:263
  173.2 14.4 %shard_map.186 = (bf16[2,2,2,2,96,768]{5,4,3,2,1,0:T(8,128)(2,1)}, f32[1024,768]{1,0:T(8,128)}) custom-call(s32[3]{0:T(128)} %copy-done.13, bf16[768,1024]{1,0:T(8,128)(2,1)} %copy-done.25, bf16[1024,768]{1,0:T(8,128)(2,1)} %copy-done.61, bf16[2,2,2,2,96,512]{5,4,3,2,1,0:T(8,128)(2,1)} %copy-done.20, bf16[2,2,2,2,96,256]{5,4,3,2,1,0:T(8,128)(2,1)} %copy-done.22, ...), custom_call_target="tpu_custom_call" | custom-call | flops 72477573120 | bytes 235929600 | tf_op jit(solution)/shard_map/pallas_call | solution.py:361
  190.8 20.8 %shard_map.187 = (bf16[2,2,2,2,96,768]{5,4,3,2,1,0:T(8,128)(2,1)}, f32[1024,768]{1,0:T(8,128)}, bf16[1024,768]{1,0:T(8,128)(2,1)}, bf16[768,1024]{1,0:T(8,128)(2...) custom-call(s32[3]{0:T(128)} %copy-done.13, bf16[768,1024]{1,0:T(8,128)(2,1)} %copy-done.25, bf16[1024,768]{1,0:T(8,128)(2,1)} %copy-done.61, ...), custom_call_target="tpu_custom_call" | custom-call | flops 72477573120 | bytes 235929600 | tf_op jit(solution)/shard_map/pallas_call | solution.py:361
  212.8 3.8 %fusion.1 = bf16[2,2,2,96,768]{4,3,2,1,0:T(8,128)(2,1)} fusion(bf16[2,2,2,2,96,768]{5,4,3,2,1,0:T(8,128)(2,1)S(1)} %collective-permute-done.33, bf16[2,2,2,2,96,768]{5,4,3,2,1,0:T(8,128)(2,1)} %get-tuple-element.227), kind=kLoop, calls=%fused_computation.7 | loop fusion | flops 2359296 | bytes 3538944 | tf_op jit(solution)/shard_map/convert_element_type | solution.py:795
  219.8 14.5 %shard_map.188 = (bf16[2,1024,384]{2,1,0:T(8,128)(2,1)S(1)}, bf16[2,1024,192]{2,1,0:T(8,128)(2,1)S(1)}, bf16[2,2,2,2,3,32,512]{6,5,4,3,2,1,0:T(8,128)(2,1)S(1)}, bf16[2,2,2,2,3,32,512]{6,5,4,3,2,1,0:T(8,128)(2,1)S(1)}) custom-call(s32[3]{0:T(128)S(1)} %copy-done.14, s32[2]{0:T(128)S(1)} %dynamic-slice_reduce_fusion.lens, ...), custom_call_target="tpu_custom_call" | custom-call | flops 80530636800 | bytes 58982400 | tf_op jit(solution)/shard_map/pallas_call | solution.py:556
  236.8 4.8 %shard_map.189 = (bf16[2,2,2,2,96,384]{5,4,3,2,1,0:T(8,128)(2,1)S(1)}, bf16[2,2,2,2,96,384]{5,4,3,2,1,0:T(8,128)(2,1)S(1)}) custom-call(s32[3]{0:T(128)S(1)} %copy-done.14, bf16[768,1024]{1,0:T(8,128)(2,1)S(1)} %copy-done.37, bf16[768,1024]{1,0:T(8,128)(2,1)S(1)} %copy-done.52, bf16[2,1024,384]{2,1,0:T(8,128)(2,1)S(1)} %get-tuple-element.221.dqk.dqk1, ...), custom_call_target="tpu_custom_call" | custom-call | flops 24159191040 | bytes 62914560 | tf_op jit(solution)/shard_map/pallas_call | solution.py:695
  252.6 14.9 %shard_map.190 = (bf16[2,1024,384]{2,1,0:T(8,128)(2,1)S(1)}, bf16[2,1024,192]{2,1,0:T(8,128)(2,1)S(1)}, bf16[2,2,2,3,32,512]{5,4,3,2,1,0:T(8,128)(2,1)S(1)}, bf1...) custom-call(s32[3]{0:T(128)S(1)} %copy-done.14, ...), custom_call_target="tpu_custom_call" | custom-call | flops 80530636800 | bytes 58982400 | tf_op jit(solution)/shard_map/pallas_call | solution.py:556
  276.2 4.9 %shard_map.191 = (bf16[2,2,2,96,384]{4,3,2,1,0:T(8,128)(2,1)S(1)}, bf16[2,2,2,96,384]{4,3,2,1,0:T(8,128)(2,1)S(1)}, bf16[2,2,2,96,384]{4,3,2,1,0:T(8,128)(2,1)S(1)}, bf16[2,2,2,96,384]{4,3,2,1,0:T(8,128)(2,1)S(1)}) custom-call(s32[3]{0:T(128)S(1)} %copy-done.14, bf16[768,1024]{1,0:T(8,128)(2,1)S(1)} %copy-done.37, bf16[768,1024]{1,0:T(8,128)(2,1)S(1)} %copy-done.53, ...), custom_call_target="tpu_custom_call" | custom-call | flops 24159191040 | bytes 62914560 | tf_op jit(solution)/shard_map/pallas_call | solution.py:695
  281.2 5.6 %collective-permute-done.45 = bf16[2,2,96,768]{3,2,1,0:T(8,128)(2,1)S(1)} collective-permute-done((bf16[2,2,96,768]{3,2,1,0:T(8,128)(2,1)S(1)}, bf16[2,2,96,768]{3,2,1,0:T(8,128)(2,1)S(1)}, u32[]{:S(2)}, u32[]{:S(2)}) %collective-permute-start.45) | collective-permute-done | bytes 589856 | tf_op jit(solution)/shard_map/ppermute | solution.py:739
  286.7 5.6 %collective-permute-done.46 = bf16[2,2,2,3,32,512]{5,4,3,2,1,0:T(8,128)(2,1)S(1)} collective-permute-done((bf16[2,2,2,3,32,512]{5,4,3,2,1,0:T(8,128)(2,1)S(1)}, bf16[2,2,2,3,32,512]{5,4,3,2,1,0:T(8,128)(2,1)S(1)}, u32[]{:S(2)}, u32[]{:S(2)}) %collective-permute-start.46) | collective-permute-done | bytes 786464 | tf_op jit(solution)/shard_map/ppermute | solution.py:744
  300.8 7.1 %shard_map.192 = f32[1024,768]{1,0:T(8,128)} custom-call(f32[1024,768]{1,0:T(8,128)S(1)} %copy-done.56, bf16[2,1024,384]{2,1,0:T(8,128)(2,1)S(1)} %get-tuple-element.252.dqk.dqk0, bf16[2,1024,384]{2,1,0:T(8,128)(2,1)S(1)} %copy-done.55, bf16[2,1024,192]{2,1,0:T(8,128)(2,1)S(1)} %copy-done.63, bf16[2,1024,192]{2,1,0:T(8,128)(2,1)S(1)} %copy-done.65, ...), custom_call_target="tpu_custom_call" | custom-call | flops 36238786560 | bytes 110100480 | tf_op jit(solution)/shard_map/pallas_call | solution.py:721
  309.3 9.1 %collective-permute-done.48 = bf16[2,2,2,96,384]{4,3,2,1,0:T(8,128)(2,1)S(1)} collective-permute-done((bf16[2,2,2,96,384]{4,3,2,1,0:T(8,128)(2,1)S(1)}, bf16[2,2,2,96,384]{4,3,2,1,0:T(8,128)(2,1)S(1)}, u32[]{:S(2)}, u32[]{:S(2)}) %collective-permute-start.48) | collective-permute-done | bytes 589856 | tf_op jit(solution)/shard_map/ppermute | solution.py:744
  326.4 3.7 %collective-permute-done.54 = bf16[2,2,96,384]{3,2,1,0:T(8,128)(2,1)S(1)} collective-permute-done((bf16[2,2,96,384]{3,2,1,0:T(8,128)(2,1)S(1)}, bf16[2,2,96,384]{3,2,1,0:T(8,128)(2,1)S(1)}, u32[]{:S(2)}, u32[]{:S(2)}) %collective-permute-start.54) | collective-permute-done | bytes 294944 | tf_op jit(solution)/shard_map/ppermute | solution.py:739
  334.7 3.9 %collective-permute-done.59 = bf16[2,2,3,32,512]{4,3,2,1,0:T(8,128)(2,1)S(1)} collective-permute-done((bf16[2,2,3,32,512]{4,3,2,1,0:T(8,128)(2,1)S(1)}, bf16[2,2,3,32,512]{4,3,2,1,0:T(8,128)(2,1)S(1)}, u32[]{:S(2)}, u32[]{:S(2)}) %collective-permute-start.59) | collective-permute-done | bytes 393248 | tf_op jit(solution)/shard_map/ppermute | solution.py:739
  339.1 3.5 collective-permute-done.56
  343.9 3.9 %collective-permute-done.60 = bf16[2,3,32,512]{3,2,1,0:T(8,128)(2,1)S(1)} collective-permute-done((bf16[2,3,32,512]{3,2,1,0:T(8,128)(2,1)S(1)}, bf16[2,3,32,512]{3,2,1,0:T(8,128)(2,1)S(1)}, u32[]{:S(2)}, u32[]{:S(2)}) %collective-permute-start.60) | collective-permute-done | bytes 196640 | tf_op jit(solution)/shard_map/ppermute | solution.py:739
  (345 shorter events, 115.4 us)
Async XLA Ops:
  25.0 11.6 %collective-permute-start.4 = (bf16[2,3,32,512]{3,2,1,0:T(8,128)(2,1)S(1)}, bf16[2,3,32,512]{3,2,1,0:T(8,128)(2,1)S(1)}, u32[]{:S(2)}, u32[]{:S(2)}) collective-permute-start(bf16[2,3,32,512]{3,2,1,0:T(8,128)(2,1)S(1)} %pad_maximum_fusion.28), channel_id=1, source_target_pairs={{0,16},{4,20},{8,24},{12,28},{16,0},{20,4},{24,8},{28,12},{1,17},{... | collective-permute-start | bytes 589832 | tf_op jit(solution)/shard_map/ppermute | solution.py:739
  36.7 15.2 %collective-permute-start.6 = (bf16[2,2,2,96,384]{4,3,2,1,0:T(8,128)(2,1)S(1)}, bf16[2,2,2,96,384]{4,3,2,1,0:T(8,128)(2,1)S(1)}, u32[]{:S(2)}, u32[]{:S(2)}) collective-permute-start(bf16[2,2,2,96,384]{4,3,2,1,0:T(8,128)(2,1)S(1)} %pad_maximum_fusion.12), channel_id=1, source_target_pairs={{0,2},{1,3},{2,0},{3,1},{4,6},{5,7},{6,4},{7,5},{8,10},{9,11},{10,... | collective-permute-start | bytes 1769480 | tf_op jit(solution)/shard_map/ppermute | solution.py:744
  37.3 14.6 %collective-permute-start.7 = (bf16[2,2,2,96,384]{4,3,2,1,0:T(8,128)(2,1)S(1)}, bf16[2,2,2,96,384]{4,3,2,1,0:T(8,128)(2,1)S(1)}, u32[]{:S(2)}, u32[]{:S(2)}) collective-permute-start(bf16[2,2,2,96,384]{4,3,2,1,0:T(8,128)(2,1)S(1)} %pad_maximum_fusion.13), channel_id=1, source_target_pairs={{0,4},{4,0},{8,12},{12,8},{16,20},{20,16},{24,28},{28,24},{1,5},{5... | collective-permute-start | bytes 1769480 | tf_op jit(solution)/shard_map/ppermute | solution.py:739
  47.5 16.6 %collective-permute-start.12 = (bf16[2,96,512]{2,1,0:T(8,128)(2,1)S(1)}, bf16[2,96,512]{2,1,0:T(8,128)(2,1)S(1)}, u32[]{:S(2)}, u32[]{:S(2)}) collective-permute-start(bf16[2,96,512]{2,1,0:T(8,128)(2,1)S(1)} %pad_maximum_fusion.29), channel_id=1, source_target_pairs={{0,16},{4,20},{8,24},{12,28},{16,0},{20,4},{24,8},{28,12},{1,17},{... | collective-permute-start | bytes 589832 | tf_op jit(solution)/shard_map/ppermute | solution.py:739
  51.8 11.1 %collective-permute-start.8 = (bf16[2,2,3,32,512]{4,3,2,1,0:T(8,128)(2,1)S(1)}, bf16[2,2,3,32,512]{4,3,2,1,0:T(8,128)(2,1)S(1)}, u32[]{:S(2)}, u32[]{:S(2)}) collective-permute-start(bf16[2,2,3,32,512]{4,3,2,1,0:T(8,128)(2,1)S(1)} %get-tuple-element.147), channel_id=1, source_target_pairs={{0,4},{4,0},{8,12},{12,8},{16,20},{20,16},{24,28},{28,24},{1,5},{5... | collective-permute-start | bytes 1179656 | tf_op jit(solution)/shard_map/ppermute | solution.py:739
  66.0 18.6 %collective-permute-start.14 = (bf16[2,2,2,3,32,512]{5,4,3,2,1,0:T(8,128)(2,1)S(1)}, bf16[2,2,2,3,32,512]{5,4,3,2,1,0:T(8,128)(2,1)S(1)}, u32[]{:S(2)}, u32[]{:S(2)}) collective-permute-start(bf16[2,2,2,3,32,512]{5,4,3,2,1,0:T(8,128)(2,1)S(1)} %pad_maximum_fusion.6), channel_id=1, source_target_pairs={{0,2},{1,3},{2,0},{3,1},{4,6},{5,7},{6,4},{7,5},{8,10},{9,11},{10,... | collective-permute-start | bytes 2359304 | tf_op jit(solution)/shard_map/ppermute | solution.py:744
  66.6 18.3 %collective-permute-start.15 = (bf16[2,2,2,3,32,512]{5,4,3,2,1,0:T(8,128)(2,1)S(1)}, bf16[2,2,2,3,32,512]{5,4,3,2,1,0:T(8,128)(2,1)S(1)}, u32[]{:S(2)}, u32[]{:S(2)}) collective-permute-start(bf16[2,2,2,3,32,512]{5,4,3,2,1,0:T(8,128)(2,1)S(1)} %pad_maximum_fusion.7), channel_id=1, source_target_pairs={{0,4},{4,0},{8,12},{12,8},{16,20},{20,16},{24,28},{28,24},{1,5},{5... | collective-permute-start | bytes 2359304 | tf_op jit(solution)/shard_map/ppermute | solution.py:739
  85.0 11.8 %collective-permute-start.18 = (bf16[2,96,256]{2,1,0:T(8,128)(2,1)S(1)}, bf16[2,96,256]{2,1,0:T(8,128)(2,1)S(1)}, u32[]{:S(2)}, u32[]{:S(2)}) collective-permute-start(bf16[2,96,256]{2,1,0:T(8,128)(2,1)S(1)} %pad_maximum_fusion.34), channel_id=1, source_target_pairs={{0,16},{4,20},{8,24},{12,28},{16,0},{20,4},{24,8},{28,12},{1,17},{... | collective-permute-start | bytes 294920 | tf_op jit(solution)/shard_map/ppermute | solution.py:739
  97.8 13.5 %collective-permute-start.23 = (bf16[2,2,96,256]{3,2,1,0:T(8,128)(2,1)S(1)}, bf16[2,2,96,256]{3,2,1,0:T(8,128)(2,1)S(1)}, u32[]{:S(2)}, u32[]{:S(2)}) collective-permute-start(bf16[2,2,96,256]{3,2,1,0:T(8,128)(2,1)S(1)} %pad_maximum_fusion.30), channel_id=1, source_target_pairs={{0,8},{4,12},{8,0},{12,4},{16,24},{20,28},{24,16},{28,20},{1,9},{5... | collective-permute-start | bytes 589832 | tf_op jit(solution)/shard_map/ppermute | solution.py:739
  98.2 19.2 %collective-permute-start.21 = (bf16[2,2,2,96,512]{4,3,2,1,0:T(8,128)(2,1)S(1)}, bf16[2,2,2,96,512]{4,3,2,1,0:T(8,128)(2,1)S(1)}, u32[]{:S(2)}, u32[]{:S(2)}) collective-permute-start(bf16[2,2,2,96,512]{4,3,2,1,0:T(8,128)(2,1)S(1)} %pad_maximum_fusion.8), channel_id=1, source_target_pairs={{0,2},{1,3},{2,0},{3,1},{4,6},{5,7},{6,4},{7,5},{8,10},{9,11},{10,... | collective-permute-start | bytes 2359304 | tf_op jit(solution)/shard_map/ppermute | solution.py:744
  98.9 18.7 %collective-permute-start.22 = (bf16[2,2,2,96,512]{4,3,2,1,0:T(8,128)(2,1)S(1)}, bf16[2,2,2,96,512]{4,3,2,1,0:T(8,128)(2,1)S(1)}, u32[]{:S(2)}, u32[]{:S(2)}) collective-permute-start(bf16[2,2,2,96,512]{4,3,2,1,0:T(8,128)(2,1)S(1)} %pad_maximum_fusion.9), channel_id=1, source_target_pairs={{0,4},{4,0},{8,12},{12,8},{16,20},{20,16},{24,28},{28,24},{1,5},{5... | collective-permute-start | bytes 2359304 | tf_op jit(solution)/shard_map/ppermute | solution.py:739
  125.5 17.6 %collective-permute-start.28 = (bf16[2,2,2,96,256]{4,3,2,1,0:T(8,128)(2,1)S(1)}, bf16[2,2,2,96,256]{4,3,2,1,0:T(8,128)(2,1)S(1)}, u32[]{:S(2)}, u32[]{:S(2)}) collective-permute-start(bf16[2,2,2,96,256]{4,3,2,1,0:T(8,128)(2,1)S(1)} %pad_maximum_fusion.19), channel_id=1, source_target_pairs={{0,2},{1,3},{2,0},{3,1},{4,6},{5,7},{6,4},{7,5},{8,10},{9,11},{10,... | collective-permute-start | bytes 1179656 | tf_op jit(solution)/shard_map/ppermute | solution.py:744
  127.1 16.2 %collective-permute-start.29 = (bf16[2,2,2,96,256]{4,3,2,1,0:T(8,128)(2,1)S(1)}, bf16[2,2,2,96,256]{4,3,2,1,0:T(8,128)(2,1)S(1)}, u32[]{:S(2)}, u32[]{:S(2)}) collective-permute-start(bf16[2,2,2,96,256]{4,3,2,1,0:T(8,128)(2,1)S(1)} %pad_maximum_fusion.20), channel_id=1, source_target_pairs={{0,4},{4,0},{8,12},{12,8},{16,20},{20,16},{24,28},{28,24},{1,5},{5... | collective-permute-start | bytes 1179656 | tf_op jit(solution)/shard_map/ppermute | solution.py:739
  173.0 14.6 %collective-permute-start.32 = (bf16[2,2,2,2,96,768]{5,4,3,2,1,0:T(8,128)(2,1)S(1)}, bf16[2,2,2,2,96,768]{5,4,3,2,1,0:T(8,128)(2,1)}, u32[]{:S(2)}, u32[]{:S(2)}) collective-permute-start(bf16[2,2,2,2,96,768]{5,4,3,2,1,0:T(8,128)(2,1)S(1)} %get-tuple-element.191), channel_id=1, source_target_pairs={{0,1},{1,0},{2,3},{3,2},{4,5},{5,4},{6,7},{7,6},{8,9},{9,8},{10,11... | collective-permute-start | bytes 7077896 | tf_op jit(solution)/shard_map/ppermute | solution.py:744
  190.2 44.2 %collective-permute-start.35 = (bf16[2,2,2,96,768]{4,3,2,1,0:T(8,128)(2,1)}, bf16[2,2,2,96,768]{4,3,2,1,0:T(8,128)(2,1)}, u32[]{:S(2)}, u32[]{:S(2)}) collective-permute-start(bf16[2,2,2,96,768]{4,3,2,1,0:T(8,128)(2,1)} %fusion), channel_id=1, source_target_pairs={{0,4},{4,0},{8,12},{12,8},{16,20},{20,16},{24,28},{28,24},{1,5},{5... | collective-permute-start | bytes 3538952 | tf_op jit(solution)/shard_map/ppermute | solution.py:739
  190.7 21.6 %collective-permute-start.33 = (bf16[2,2,2,2,96,768]{5,4,3,2,1,0:T(8,128)(2,1)}, bf16[2,2,2,2,96,768]{5,4,3,2,1,0:T(8,128)(2,1)S(1)}, u32[]{:S(2)}, u32[]{:S(2)}) collective-permute-start(bf16[2,2,2,2,96,768]{5,4,3,2,1,0:T(8,128)(2,1)} %get-tuple-element.207), channel_id=1, source_target_pairs={{0,1},{1,0},{2,3},{3,2},{4,5},{5,4},{6,7},{7,6},{8,9},{9,8},{10,11... | collective-permute-start | bytes 7077896 | tf_op jit(solution)/shard_map/ppermute | solution.py:744
  212.4 22.1 %collective-permute-start.34 = (f32[4,768]{1,0:T(4,128)S(1)}, f32[4,768]{1,0:T(4,128)S(1)}, u32[]{:S(2)}, u32[]{:S(2)}) collective-permute-start(f32[4,768]{1,0:T(4,128)S(1)} %pad_maximum_fusion.35), channel_id=1, source_target_pairs={{0,1},{1,0},{2,3},{3,2},{4,5},{5,4},{6,7},{7,6},{8,9},{9,8},{10,11... | collective-permute-start | bytes 36872 | tf_op jit(solution)/shard_map/ppermute | solution.py:827
  216.6 28.1 %collective-permute-start.39 = (bf16[2,2,2,96,768]{4,3,2,1,0:T(8,128)(2,1)}, bf16[2,2,2,96,768]{4,3,2,1,0:T(8,128)(2,1)}, u32[]{:S(2)}, u32[]{:S(2)}) collective-permute-start(bf16[2,2,2,96,768]{4,3,2,1,0:T(8,128)(2,1)} %fusion.1), channel_id=1, source_target_pairs={{0,2},{1,3},{2,0},{3,1},{4,6},{5,7},{6,4},{7,5},{8,10},{9,11},{10,... | collective-permute-start | bytes 3538952 | tf_op jit(solution)/shard_map/ppermute | solution.py:744
  244.7 22.7 %collective-permute-start.40 = (f32[4,768]{1,0:T(4,128)S(1)}, f32[4,768]{1,0:T(4,128)S(1)}, u32[]{:S(2)}, u32[]{:S(2)}) collective-permute-start(f32[4,768]{1,0:T(4,128)S(1)} %add.264), channel_id=1, source_target_pairs={{0,16},{4,20},{8,24},{12,28},{16,0},{20,4},{24,8},{28,12},{1,17},{... | collective-permute-start | bytes 36872 | tf_op jit(solution)/shard_map/ppermute | solution.py:827
  251.0 16.5 %collective-permute-start.44 = (bf16[2,2,96,768]{3,2,1,0:T(8,128)(2,1)}, bf16[2,2,96,768]{3,2,1,0:T(8,128)(2,1)S(1)}, u32[]{:S(2)}, u32[]{:S(2)}) collective-permute-start(bf16[2,2,96,768]{3,2,1,0:T(8,128)(2,1)} %fusion.4), channel_id=1, source_target_pairs={{0,4},{4,0},{8,12},{12,8},{16,20},{20,16},{24,28},{28,24},{1,5},{5... | collective-permute-start | bytes 1769480 | tf_op jit(solution)/shard_map/ppermute | solution.py:739
  251.5 16.0 %collective-permute-start.43 = (bf16[2,2,96,768]{3,2,1,0:T(8,128)(2,1)}, bf16[2,2,96,768]{3,2,1,0:T(8,128)(2,1)S(1)}, u32[]{:S(2)}, u32[]{:S(2)}) collective-permute-start(bf16[2,2,96,768]{3,2,1,0:T(8,128)(2,1)} %fusion.5), channel_id=1, source_target_pairs={{0,2},{1,3},{2,0},{3,1},{4,6},{5,7},{6,4},{7,5},{8,10},{9,11},{10,... | collective-permute-start | bytes 1769480 | tf_op jit(solution)/shard_map/ppermute | solution.py:744
  252.0 15.5 %collective-permute-start.41 = (bf16[2,2,2,2,96,384]{5,4,3,2,1,0:T(8,128)(2,1)S(1)}, bf16[2,2,2,2,96,384]{5,4,3,2,1,0:T(8,128)(2,1)S(1)}, u32[]{:S(2)}, u32[]{:S(2)}) collective-permute-start(bf16[2,2,2,2,96,384]{5,4,3,2,1,0:T(8,128)(2,1)S(1)} %get-tuple-element.237), channel_id=1, source_target_pairs={{0,1},{1,0},{2,3},{3,2},{4,5},{5,4},{6,7},{7,6},{8,9},{9,8},{10,11... | collective-permute-start | bytes 3538952 | tf_op jit(solution)/shard_map/ppermute | solution.py:744
  252.0 15.5 %collective-permute-start.42 = (bf16[2,2,2,2,96,384]{5,4,3,2,1,0:T(8,128)(2,1)S(1)}, bf16[2,2,2,2,96,384]{5,4,3,2,1,0:T(8,128)(2,1)S(1)}, u32[]{:S(2)}, u32[]{:S(2)}) collective-permute-start(bf16[2,2,2,2,96,384]{5,4,3,2,1,0:T(8,128)(2,1)S(1)} %get-tuple-element.238), channel_id=1, source_target_pairs={{0,1},{1,0},{2,3},{3,2},{4,5},{5,4},{6,7},{7,6},{8,9},{9,8},{10,11... | collective-permute-start | bytes 3538952 | tf_op jit(solution)/shard_map/ppermute | solution.py:744
  271.4 15.3 %collective-permute-start.45 = (bf16[2,2,96,768]{3,2,1,0:T(8,128)(2,1)S(1)}, bf16[2,2,96,768]{3,2,1,0:T(8,128)(2,1)S(1)}, u32[]{:S(2)}, u32[]{:S(2)}) collective-permute-start(bf16[2,2,96,768]{3,2,1,0:T(8,128)(2,1)S(1)} %pad_maximum_fusion.14), channel_id=1, source_target_pairs={{0,8},{4,12},{8,0},{12,4},{16,24},{20,28},{24,16},{28,20},{1,9},{5... | collective-permute-start | bytes 1769480 | tf_op jit(solution)/shard_map/ppermute | solution.py:739
  273.1 19.2 %collective-permute-start.46 = (bf16[2,2,2,3,32,512]{5,4,3,2,1,0:T(8,128)(2,1)S(1)}, bf16[2,2,2,3,32,512]{5,4,3,2,1,0:T(8,128)(2,1)S(1)}, u32[]{:S(2)}, u32[]{:S(2)}) collective-permute-start(bf16[2,2,2,3,32,512]{5,4,3,2,1,0:T(8,128)(2,1)S(1)} %get-tuple-element.249), channel_id=1, source_target_pairs={{0,2},{1,3},{2,0},{3,1},{4,6},{5,7},{6,4},{7,5},{8,10},{9,11},{10,... | collective-permute-start | bytes 2359304 | tf_op jit(solution)/shard_map/ppermute | solution.py:744
  274.6 18.9 %collective-permute-start.47 = (bf16[2,2,2,3,32,512]{5,4,3,2,1,0:T(8,128)(2,1)S(1)}, bf16[2,2,2,3,32,512]{5,4,3,2,1,0:T(8,128)(2,1)S(1)}, u32[]{:S(2)}, u32[]{:S(2)}) collective-permute-start(bf16[2,2,2,3,32,512]{5,4,3,2,1,0:T(8,128)(2,1)S(1)} %get-tuple-element.250), channel_id=1, source_target_pairs={{0,4},{4,0},{8,12},{12,8},{16,20},{20,16},{24,28},{28,24},{1,5},{5... | collective-permute-start | bytes 2359304 | tf_op jit(solution)/shard_map/ppermute | solution.py:739
  293.7 14.5 %collective-permute-start.52 = (bf16[2,96,768]{2,1,0:T(8,128)(2,1)S(1)}, bf16[2,96,768]{2,1,0:T(8,128)(2,1)S(1)}, u32[]{:S(2)}, u32[]{:S(2)}) collective-permute-start(bf16[2,96,768]{2,1,0:T(8,128)(2,1)S(1)} %pad_maximum_fusion.24), channel_id=1, source_target_pairs={{0,16},{4,20},{8,24},{12,28},{16,0},{20,4},{24,8},{28,12},{1,17},{... | collective-permute-start | bytes 884744 | tf_op jit(solution)/shard_map/ppermute | solution.py:739
  296.5 12.1 %collective-permute-start.51 = (bf16[2,2,3,32,512]{4,3,2,1,0:T(8,128)(2,1)S(1)}, bf16[2,2,3,32,512]{4,3,2,1,0:T(8,128)(2,1)S(1)}, u32[]{:S(2)}, u32[]{:S(2)}) collective-permute-start(bf16[2,2,3,32,512]{4,3,2,1,0:T(8,128)(2,1)S(1)} %fusion.7), channel_id=1, source_target_pairs={{0,2},{1,3},{2,0},{3,1},{4,6},{5,7},{6,4},{7,5},{8,10},{9,11},{10,... | collective-permute-start | bytes 1179656 | tf_op jit(solution)/shard_map/ppermute | solution.py:744
  297.2 12.1 %collective-permute-start.50 = (bf16[2,2,3,32,512]{4,3,2,1,0:T(8,128)(2,1)S(1)}, bf16[2,2,3,32,512]{4,3,2,1,0:T(8,128)(2,1)S(1)}, u32[]{:S(2)}, u32[]{:S(2)}) collective-permute-start(bf16[2,2,3,32,512]{4,3,2,1,0:T(8,128)(2,1)S(1)} %fusion.6), channel_id=1, source_target_pairs={{0,4},{4,0},{8,12},{12,8},{16,20},{20,16},{24,28},{28,24},{1,5},{5... | collective-permute-start | bytes 1179656 | tf_op jit(solution)/shard_map/ppermute | solution.py:739
  297.8 20.7 %collective-permute-start.48 = (bf16[2,2,2,96,384]{4,3,2,1,0:T(8,128)(2,1)S(1)}, bf16[2,2,2,96,384]{4,3,2,1,0:T(8,128)(2,1)S(1)}, u32[]{:S(2)}, u32[]{:S(2)}) collective-permute-start(bf16[2,2,2,96,384]{4,3,2,1,0:T(8,128)(2,1)S(1)} %get-tuple-element.258), channel_id=1, source_target_pairs={{0,2},{1,3},{2,0},{3,1},{4,6},{5,7},{6,4},{7,5},{8,10},{9,11},{10,... | collective-permute-start | bytes 1769480 | tf_op jit(solution)/shard_map/ppermute | solution.py:744
  299.3 19.7 %collective-permute-start.49 = (bf16[2,2,2,96,384]{4,3,2,1,0:T(8,128)(2,1)S(1)}, bf16[2,2,2,96,384]{4,3,2,1,0:T(8,128)(2,1)S(1)}, u32[]{:S(2)}, u32[]{:S(2)}) collective-permute-start(bf16[2,2,2,96,384]{4,3,2,1,0:T(8,128)(2,1)S(1)} %get-tuple-element.259), channel_id=1, source_target_pairs={{0,4},{4,0},{8,12},{12,8},{16,20},{20,16},{24,28},{28,24},{1,5},{5... | collective-permute-start | bytes 1769480 | tf_op jit(solution)/shard_map/ppermute | solution.py:739
  326.0 12.6 %collective-permute-start.59 = (bf16[2,2,3,32,512]{4,3,2,1,0:T(8,128)(2,1)S(1)}, bf16[2,2,3,32,512]{4,3,2,1,0:T(8,128)(2,1)S(1)}, u32[]{:S(2)}, u32[]{:S(2)}) collective-permute-start(bf16[2,2,3,32,512]{4,3,2,1,0:T(8,128)(2,1)S(1)} %pad_maximum_fusion.21), channel_id=1, source_target_pairs={{0,8},{4,12},{8,0},{12,4},{16,24},{20,28},{24,16},{28,20},{1,9},{5... | collective-permute-start | bytes 1179656 | tf_op jit(solution)/shard_map/ppermute | solution.py:739
  (108 other events, 1364.8 us)

commit v2 on v1

--- a/solution.py
+++ b/solution.py
@@ -9,7 +9,7 @@
 EPS = 1e-05
 F32 = jnp.float32
 BF16 = jnp.bfloat16
-GP = jnp.float32
+GP = jnp.bfloat16
 SCALE = 1.0 / math.sqrt(HEAD_DIM)
 LOG2E = math.log2(math.e)
 NEG = -1e30
@@ -70,7 +70,7 @@
 
 def whole(shape):
     zeros = (0,) * len(shape)
-    return pl.BlockSpec(shape, lambda *_: zeros)
+    return pl.BlockSpec(shape, lambda *_: zeros, pipeline_mode=pl.Buffered(1))
 
 
 def low_pick(k):
@@ -152,14 +152,14 @@
     ffn_units(chunk, hid, wu, wd, act_o, gp_o, acc)
 
 
-def ffn_part(bits, hid, ua0, ua1, db0, db1, units, chunk=512):
+def ffn_part(bits, hid, ua0, ua1, db0, db1, chunk=512):
     rows, width = hid.shape
     p, n = ua0.shape[-2:]
     sds = jax.ShapeDtypeStruct
     col = pl.BlockSpec((1, rows, n), lambda k, *_: (k, 0, 0))
     return pl.pallas_call(
         functools.partial(ffn_part_kernel, chunk),
-        out_shape=(sds((4, rows, units), BF16), sds((4, rows, units), GP), sds((rows, width), F32)),
+        out_shape=(sds((4, rows, n), BF16), sds((4, rows, n), GP), sds((rows, width), F32)),
         grid_spec=pltpu.PrefetchScalarGridSpec(
             num_scalar_prefetch=1, grid=(4,),
             in_specs=[whole((rows, width)), spec_a((p, n), low_pick), spec_a((p, n), high_pick),
@@ -167,13 +167,13 @@
             out_specs=[col, col, whole((rows, width))],
             scratch_shapes=[pltpu.VMEM((width, n), BF16), pltpu.VMEM((width, n), BF16)],
         ),
-        compiler_params=params(32),
+        compiler_params=params(26),
         cost_estimate=cost(4 * rows * width * 4 * n, 16 * rows * width),
     )(bits, hid, ua0, ua1, db0, db1)
 
 
-def ffn_rest_kernel(chunk, bits, lens, hid, ua0, ua1, db0, db1, part, gain, bias, dout, act_i, gp_i,
-                    act_o, gp_o, out, dsec, dffn, dffnt, dgain, dbias, wu, wd, acc):
+def ffn_rest_kernel(chunk, bits, lens, hid, ua0, ua1, db0, db1, part, gain, bias, dout,
+                    act_o, gp_o, out, acc, dffn, dffnt, dgain, dbias, wu, wd):
     k = pl.program_id(0)
     rows = hid.shape[0]
     load_pair(k, bits, wu, wd, ua0, ua1, db0, db1)
@@ -203,7 +203,7 @@
             dg += jnp.sum(dy * unit, axis=0, keepdims=True)
             db += jnp.sum(dy, axis=0, keepdims=True)
             dz = norm_back(dy * g, unit, inverse)
-            dsec[at, :] = dz
+            acc[at, :] = dz
             low = dz.astype(BF16)
             dffn[at, :] = low
             dffnt[:, at] = low.T
@@ -211,40 +211,41 @@
         dbias[...] = db
 
 
-def ffn_rest(bits, lens, hid, ua0, ua1, db0, db1, part, gain, bias, dout, act, gp, chunk=512):
+def ffn_rest(bits, lens, hid, ua0, ua1, db0, db1, part, gain, bias, dout, chunk=512):
     rows, width = hid.shape
     p, n = ua0.shape[-2:]
-    last = act.shape[2] // n - 1
     sds = jax.ShapeDtypeStruct
     full = whole((rows, width))
     line = whole((1, width))
-    col = pl.BlockSpec((1, rows, n), lambda k, *_: (k, 0, last))
-    anywhere = pl.BlockSpec(memory_space=pl.ANY)
+    col = pl.BlockSpec((1, rows, n), lambda k, *_: (k, 0, 0))
     return pl.pallas_call(
         functools.partial(ffn_rest_kernel, chunk),
-        out_shape=(sds(act.shape, act.dtype), sds(gp.shape, gp.dtype), sds((rows, width), BF16), sds((rows, width), F32),
+        out_shape=(sds((4, rows, n), BF16), sds((4, rows, n), GP), sds((rows, width), BF16), sds((rows, width), F32),
                    sds((rows, width), BF16), sds((width, rows), BF16), sds((1, width), F32), sds((1, width), F32)),
         grid_spec=pltpu.PrefetchScalarGridSpec(
             num_scalar_prefetch=2, grid=(4,),
             in_specs=[full, spec_a((p, n), low_pick), spec_a((p, n), high_pick),
-                      spec_b((p, n), low_pick), spec_b((p, n), high_pick), full, line, line, full, anywhere, anywhere],
+                      spec_b((p, n), low_pick), spec_b((p, n), high_pick), full, line, line, full],
             out_specs=[col, col, full, full, full, whole((width, rows)), line, line],
-            scratch_shapes=[pltpu.VMEM((width, n), BF16), pltpu.VMEM((width, n), BF16), pltpu.VMEM((rows, width), F32)],
+            scratch_shapes=[pltpu.VMEM((width, n), BF16), pltpu.VMEM((width, n), BF16)],
         ),
-        input_output_aliases={11: 0, 12: 1},
-        compiler_params=params(46),
+        compiler_params=params(30),
         cost_estimate=cost(4 * rows * width * 4 * n, 20 * rows * width),
-    )(bits, lens, hid, ua0, ua1, db0, db1, part, gain, bias, dout, act, gp)
-
-
-def down_grad_kernel(bits, dt, act, keep, send):
+    )(bits, lens, hid, ua0, ua1, db0, db1, part, gain, bias, dout)
+
+
+def down_grad_kernel(bits, dt, actp, actq, keep, send):
     k = pl.program_id(0)
-    grad = dot_nn(dt[...], act[0]).astype(BF16)
+    first = dot_nn(dt[...], actp[0]).astype(BF16)
+    second = dot_nn(dt[...], actq[0]).astype(BF16)
     rows = keep.shape[-2]
+    n = actp.shape[2]
 
     def put(ref):
         for d in range(8):
-            piece(ref, bits, d, True)[...] = grad[d * rows : (d + 1) * rows]
+            at = piece(ref, bits, d, True)
+            at[:, pl.ds(0, n)] = first[d * rows : (d + 1) * rows]
+            at[:, pl.ds(n, actq.shape[2])] = second[d * rows : (d + 1) * rows]
 
     @pl.when(k < 2)
     def _():
@@ -255,9 +256,10 @@
         put(send)
 
 
-def down_grads(bits, dt, act):
+def down_grads(bits, dt, actp, actq):
     width, rows = dt.shape
-    n = act.shape[2]
+    col = lambda a: pl.BlockSpec((1, rows, a.shape[2]), lambda k, *_: (k, 0, 0))
+    n = actp.shape[2] + actq.shape[2]
     p = width // 8
     sds = jax.ShapeDtypeStruct
     return pl.pallas_call(
@@ -265,17 +267,17 @@
         out_shape=(sds((2, 2, 2, 2, p, n), BF16), sds((2, 2, 2, 2, p, n), BF16)),
         grid_spec=pltpu.PrefetchScalarGridSpec(
             num_scalar_prefetch=1, grid=(4,),
-            in_specs=[whole((width, rows)), pl.BlockSpec((1, rows, n), lambda k, *_: (k, 0, 0))],
+            in_specs=[whole((width, rows)), col(actp), col(actq)],
             out_specs=[spec_b((p, n), low_pick), spec_b((p, n), high_pick)],
         ),
         compiler_params=params(22),
         cost_estimate=cost(2 * rows * width * 4 * n, 14 * rows * width),
-    )(bits, dt, act)
-
-
-def ffn_bwd_kernel(chunk, last, bits, ht, dffn, uap, uaq, dbp, dbq, gp, *rest):
+    )(bits, dt, actp, actq)
+
+
+def ffn_bwd_kernel(chunk, last, bits, ht, dffn, uap, uaq, dbp, dbq, gpp, gpq, *rest):
     if last:
-        dsec, part, unit, inverse, gain, gu, dfirst, dattn, dattnt, dgain, dbias, wu, wd, dup_s, acc = rest
+        dsec, part, unit, inverse, gain, gu, acc, dattn, dattnt, dgain, dbias, wu, wd, dup_s = rest
     else:
         gu, acc, wu, wd, dup_s = rest
     k = pl.program_id(0)
@@ -298,11 +300,11 @@
     ats = [pl.ds(r * chunk, chunk) for r in range(rows // chunk)]
     ahead = dot_nn(dffn[ats[0], :], wd[...])
     for r, at in enumerate(ats):
-        dup = (ahead * gp[0, at, :].astype(F32)).astype(BF16)
+        dup_s[at, left] = (ahead[:, :np] * gpp[0, at, :].astype(F32)).astype(BF16)
+        dup_s[at, right] = (ahead[:, np:] * gpq[0, at, :].astype(F32)).astype(BF16)
         if r + 1 < len(ats):
             ahead = dot_nn(dffn[ats[r + 1], :], wd[...])
-        dup_s[at, :] = dup
-        acc[at, :] += dot_nt(dup, wu[...])
+        acc[at, :] += dot_nt(dup_s[at, :], wu[...])
 
     grad = dot_nn(ht[...], dup_s[...]).astype(BF16)
     p = gu.shape[-2]
@@ -324,7 +326,7 @@
                 dg += jnp.sum(dh * u, axis=0, keepdims=True)
                 db += jnp.sum(dh, axis=0, keepdims=True)
                 dz = norm_back(dh * g, u, inverse[at, :])
-                dfirst[at, :] = dz
+                acc[at, :] = dz
                 low = dz.astype(BF16)
                 dattn[at, :] = low
                 dattnt[:, at] = low.T
@@ -332,7 +334,7 @@
             dbias[...] = db
 
 
-def ffn_backward(last, bits, ht, dffn, uap, uaq, dbp, dbq, gp, extra=(), chunk=512):
+def ffn_backward(last, bits, ht, dffn, uap, uaq, dbp, dbq, gpp, gpq, extra=(), chunk=512):
     rows, width = dffn.shape
     p, np = uap.shape[-2:]
     nq = uaq.shape[-1]
@@ -347,14 +349,14 @@
     in_specs = [
         whole((width, rows)), full,
         spec_a((p, np), pick), spec_a((p, nq), pick), spec_b((p, np), pick), spec_b((p, nq), pick),
-        pl.BlockSpec((1, rows, n), lambda k, *_: (k + off, 0, 0)),
+        pl.BlockSpec((1, rows, np), lambda k, *_: (k + off, 0, 0)),
+        pl.BlockSpec((1, rows, nq), lambda k, *_: (k + off, 0, 0)),
     ]
     scratch = [pltpu.VMEM((width, n), BF16), pltpu.VMEM((width, n), BF16), pltpu.VMEM((rows, n), BF16)]
     if last:
         in_specs += [full] * 3 + [whole((rows, 1)), line]
         out_shape += [sds((rows, width), F32), sds((rows, width), BF16), sds((width, rows), BF16), sds((1, width), F32), sds((1, width), F32)]
         out_specs += [full, full, whole((width, rows)), line, line]
-        scratch += [pltpu.VMEM((rows, width), F32)]
     else:
         out_shape += [sds((rows, width), F32)]
         out_specs += [full]
@@ -364,9 +366,9 @@
         grid_spec=pltpu.PrefetchScalarGridSpec(
             num_scalar_prefetch=1, grid=(2,), in_specs=in_specs, out_specs=out_specs, scratch_shapes=scratch,
         ),
-        compiler_params=params(56),
+        compiler_params=params(36),
         cost_estimate=cost(6 * rows * width * 2 * n, 30 * rows * width),
-    )(bits, ht, dffn, uap, uaq, dbp, dbq, gp, *extra)
+    )(bits, ht, dffn, uap, uaq, dbp, dbq, gpp, gpq, *extra)
 
 
 def key_bias(size, length):
@@ -908,24 +910,24 @@
     ea, eb = jnp.stack([ea, ra]), jnp.stack([eb, rb])
     ea, eb, hid = after((ea, eb, hid), fa1, fb1)
     ra, rb = over_x(ea), over_y(eb)
-    act, gp, part = ffn_part(bits, hid, fa, fa1, fb, fb1, units)
+    actp, gpp, part = ffn_part(bits, hid, fa, fa1, fb, fb1)
     ea, eb = jnp.stack([ea, ra]), jnp.stack([eb, rb])
     ea, eb = after((ea, eb), part)
     ea1, eb1 = over_pair(ea), over_pair(eb)
-    act, gp, out, dsec, dffn, dffnt, dgain2, dbias2 = ffn_rest(
-        bits, lens, hid, ea, ea1, eb, eb1, part, gain2, bias2, dout, act, gp
+    actq, gpq, out, dsec, dffn, dffnt, dgain2, dbias2 = ffn_rest(
+        bits, lens, hid, ea, ea1, eb, eb1, part, gain2, bias2, dout
     )
 
     steps = total_steps()
-    down0, down1 = down_grads(bits, dffnt, act)
+    down0, down1 = down_grads(bits, dffnt, actp, actq)
     cd = over_pair(down1)
     dffn, = after((dffn,), down1)
-    up1, part = ffn_backward(False, bits, hidt, dffn, fa1, ea1, fb1, eb1, gp)
+    up1, part = ffn_backward(False, bits, hidt, dffn, fa1, ea1, fb1, eb1, gpp, gpq)
     down0, cd, up1, dffn = after((down0, cd, up1, dffn), part)
     xd = over_y(first_sum(down0, cd))
     cu = over_pair(up1)
     up0, dfirst, dattn, dattnt, dgain1, dbias1 = ffn_backward(
-        True, bits, hidt, dffn, fa, ea, fb, eb, gp, (dsec, part, unit, inverse, gain1)
+        True, bits, hidt, dffn, fa, ea, fb, eb, gpp, gpq, (dsec, part, unit, inverse, gain1)
     )
     up0, cu, norms, dattn = after((up0, cu, jnp.concatenate([dgain1, dgain2, dbias1, dbias2]), dattn), up0)
     xu = over_x(first_sum(up0, cu))
@@ -937,31 +939,35 @@
     qka1, vo1 = qkv_grads(False, bits, xt, dattnt, dqk1, dv1, m1)
     qka1, vo1, dattn, norms, cga, cgb, xu, xd = after((qka1, vo1, dattn, norms, cga, cgb, xu, xd), vo1)
     cqk, cvo = over_pair(qka1), over_pair(vo1)
+    norms, = after((norms,), xu, xd)
+    norms = total_some(norms, steps[1])
+    send_d, send_u = second_sum(down0, cd, xd), second_sum(up0, cu, xu)
+    send_d, send_u, norms = after((send_d, send_u, norms), norms)
+    yd, yu = over_x(send_d), over_y(send_u)
     norms = total_some(norms, steps[4])
-    yd, yu = over_x(second_sum(down0, cd, xd)), over_y(second_sum(up0, cu, xu))
     dqk0, dv0, ga0, ga_out, gb0, gb_out = attention_backward(
         True, bits, lens, qk0, v0, ba, bb, lse0, dattn, wo0, (cga, cgb)
     )
     ga_out, gb_out, dqk0, norms, cqk, cvo, yd, yu = after((ga_out, gb_out, dqk0, norms, cqk, cvo, yd, yu), dv0)
-    xga, xgb = over_x(ga_out), over_y(gb_out)
+    xga = over_x(ga_out)
+    norms = total_some(norms, *steps[2:3], *steps[5:])
     u, d = third_sum(up0, cu, xu, yu), third_sum(down0, cd, xd, yd)
-    near_f = over_near(jnp.stack([u[1], d[1]]).astype(BF16))
+    send_f = jnp.stack([u[1], d[1]]).astype(BF16)
+    send_f, gb_out, norms = after((send_f, gb_out, norms), norms)
+    xgb = over_y(gb_out)
+    near_f = over_near(send_f)
     qka0, qka_out, vo0, vo_out = qkv_grads(True, bits, xt, dattnt, dqk0, dv0, m0, (cqk, cvo))
-    qka_out, vo_out, near_f, xga, xgb, dqk0 = after((qka_out, vo_out, near_f, xga, xgb, dqk0), vo0)
     xqk, xvo = over_x(qka_out), over_y(vo_out)
+    near_f, xga, xgb, dqk0 = after((near_f, xga, xgb, dqk0), vo0)
     yga, ygb = over_y(low_sum(ga0, xga)), over_x(low_sum(gb0, xgb))
     far_f = over_far(jnp.stack([u[0, 1] + wide(near_f[0, 1]), d[0, 1] + wide(near_f[1, 1])]).astype(BF16))
     dinput = input_backward(dfirst, dqk0, dqk1, dv0, dv1, wqk0, wqk1, wv0, wv1)
-    xqk, xvo, yga, ygb, norms, far_f = after((xqk, xvo, yga, ygb, norms, far_f), dinput)
-    norms = total_some(norms, steps[1])
+    xqk, xvo, yga, ygb, far_f = after((xqk, xvo, yga, ygb, far_f), dinput)
     send_qk, send_vo = low_sum(qka0, xqk), low_sum(vo0, xvo)
     g1, g2 = high_sum(ga0, xga, yga), high_sum(gb0, xgb, ygb)
     send_g = jnp.stack([g1[1], g2[1]]).astype(BF16)
-    send_qk, send_vo, send_g, norms = after((send_qk, send_vo, send_g, norms), norms)
     yqk, yvo = over_y(send_qk), over_x(send_vo)
     near_g = over_near(send_g)
-    norms, = after((norms,), yqk, yvo)
-    norms = total_some(norms, *steps[2:3], *steps[5:])
     w1, w2 = high_sum(qka0, xqk, yqk), high_sum(vo0, xvo, yvo)
     send_w = jnp.stack([w1[1], w2[1]]).astype(BF16)
     send_g = jnp.stack([g1[0, 1] + wide(near_g[0, 1]), g2[0, 1] + wide(near_g[1, 1])]).astype(BF16)

time: 356 us -> 339 us (0.952)
  Pallas kernels: 140 us -> 129 us
  waiting for transfers between devices: 104 us -> 94.4 us
  local copies, waits for them, and re-layouts: 20.3 us -> 27.4 us
  other arithmetic: 24 us -> 20.2 us
    ppermute x28, waiting for transfers between devices: 38.5 us -> 30.1 us  [partner_head(): return lax.ppermute(value, 'head', [(i, i ^ 1 << bit) for i in range(size)])]
    pallas_call x2, Pallas kernels: 35.2 us -> 27.2 us  [ffn_backward(): pl.pallas_call(functools.partial(ffn_bwd_kernel, chunk, last), out_shape=...]
    unnamed x160 -> x164, local copies, waits for them, and re-layouts: 18.3 us -> 25.4 us
    ppermute x28, starting transfers between devices: 36.2 us -> 40.8 us  [partner_dp(): return lax.ppermute(value, 'dp', [(i, i ^ step) for i in range(size)])]
    pallas_call x1, Pallas kernels: 14.3 us -> 10.7 us  [ffn_rest(): pl.pallas_call(functools.partial(ffn_rest_kernel, chunk), out_shape=(sds(...]
  transfers between devices with their start and end apart: 61 -> 61, of which waited for: 32 -> 28; matrix products, arithmetic and copies ran while one was open for 5% -> 4% of each run, Pallas kernels for 34% -> 33%
where the time goes in v2:
time: 339 us; the launch traced here: 337 us
  Pallas kernels  129 us (38%)
  waiting for transfers between devices  94.4 us (28%)
  starting transfers between devices  63.5 us (19%)
  local copies, waits for them, and re-layouts  27.4 us (8%)
  other arithmetic  20.2 us (6%)
    ppermute x28, waiting for transfers between devices, partner_dp(): return lax.ppermute(value, 'dp', [(i, i ^ step) for i in range(size)])  62.5 us
    ppermute x28, starting transfers between devices, partner_dp(): return lax.ppermute(value, 'dp', [(i, i ^ step) for i in range(size)])  40.8 us
    pallas_call x2, Pallas kernels, attention_backward(): pl.pallas_call(functools.partial(att_bwd_kernel, last), out_shape=out_sha...  30.3 us
    ppermute x28, waiting for transfers between devices, partner_head(): return lax.ppermute(value, 'head', [(i, i ^ 1 << bit) for i in range(size)])  30.1 us
    pallas_call x2, Pallas kernels, ffn_backward(): pl.pallas_call(functools.partial(ffn_bwd_kernel, chunk, last), out_shape=...  27.2 us
    unnamed x164, local copies, waits for them, and re-layouts  25.4 us
    ppermute x28, starting transfers between devices, partner_head(): return lax.ppermute(value, 'head', [(i, i ^ 1 << bit) for i in range(size)])  18 us
    pallas_call x2, Pallas kernels, attention_forward(): pl.pallas_call(att_fwd_kernel, out_shape=(sds((2, rows, w1), BF16), sds((...  14.2 us
  transfers between devices with their start and end apart: 61, of which 28 were waited for; matrix products, arithmetic and copies ran while one was open for 4% of the time, Pallas kernels for 33%

profile of v2, /device:TPU:0, one launch (start us, length us, event | category | flops | bytes accessed | tf_op | source)
XLA Modules:
  0.0 336.7 jit_solution(6587915299281923275)
XLA Ops:
  2.6 4.1 %collective-permute-start = (bf16[2,96,384]{2,1,0:T(8,128)(2,1)S(1)}, bf16[2,96,384]{2,1,0:T(8,128)(2,1)S(1)}, u32[]{:S(2)}, u32[]{:S(2)}) collective-permute-start(bf16[2,96,384]{2,1,0:T(8,128)(2,1)S(1)} %get-tuple-element.317), channel_id=1, source_target_pairs={{0,16},{4,20},{8,24},{12,28},{16,0},{20,4},{24,8},{28,12},{1,17},{... | collective-permute-start | bytes 442376 | tf_op jit(solution)/shard_map/ppermute | solution.py:741
  8.0 5.8 %collective-permute-done = bf16[2,96,384]{2,1,0:T(8,128)(2,1)S(1)} collective-permute-done((bf16[2,96,384]{2,1,0:T(8,128)(2,1)S(1)}, bf16[2,96,384]{2,1,0:T(8,128)(2,1)S(1)}, u32[]{:S(2)}, u32[]{:S(2)}) %collective-permute-start) | collective-permute-done | bytes 147488 | tf_op jit(solution)/shard_map/ppermute | solution.py:741
  14.6 7.4 %collective-permute-done.1 = bf16[2,2,96,384]{3,2,1,0:T(8,128)(2,1)S(1)} collective-permute-done((bf16[2,2,96,384]{3,2,1,0:T(8,128)(2,1)S(1)}, bf16[2,2,96,384]{3,2,1,0:T(8,128)(2,1)S(1)}, u32[]{:S(2)}, u32[]{:S(2)}) %collective-permute-start.1) | collective-permute-done | bytes 294944 | tf_op jit(solution)/shard_map/ppermute | solution.py:741
  25.0 3.4 %collective-permute-start.4 = (bf16[2,3,32,512]{3,2,1,0:T(8,128)(2,1)S(1)}, bf16[2,3,32,512]{3,2,1,0:T(8,128)(2,1)S(1)}, u32[]{:S(2)}, u32[]{:S(2)}) collective-permute-start(bf16[2,3,32,512]{3,2,1,0:T(8,128)(2,1)S(1)} %pad_maximum_fusion.28), channel_id=1, source_target_pairs={{0,16},{4,20},{8,24},{12,28},{16,0},{20,4},{24,8},{28,12},{1,17},{... | collective-permute-start | bytes 589832 | tf_op jit(solution)/shard_map/ppermute | solution.py:741
  30.7 6.0 %collective-permute-done.4 = bf16[2,3,32,512]{3,2,1,0:T(8,128)(2,1)S(1)} collective-permute-done((bf16[2,3,32,512]{3,2,1,0:T(8,128)(2,1)S(1)}, bf16[2,3,32,512]{3,2,1,0:T(8,128)(2,1)S(1)}, u32[]{:S(2)}, u32[]{:S(2)}) %collective-permute-start.4) | collective-permute-done | bytes 196640 | tf_op jit(solution)/shard_map/ppermute | solution.py:741
  38.9 8.6 %collective-permute-done.5 = bf16[2,2,3,32,512]{4,3,2,1,0:T(8,128)(2,1)} collective-permute-done((bf16[2,2,3,32,512]{4,3,2,1,0:T(8,128)(2,1)S(1)}, bf16[2,2,3,32,512]{4,3,2,1,0:T(8,128)(2,1)}, u32[]{:S(2)}, u32[]{:S(2)}) %collective-permute-start.5) | collective-permute-done | bytes 393248 | tf_op jit(solution)/shard_map/ppermute | solution.py:741
  47.5 3.2 collective-permute-start.12
  56.5 4.6 %shard_map.178 = (bf16[2,1024,384]{2,1,0:T(8,128)(2,1)S(1)}, bf16[2,1024,192]{2,1,0:T(8,128)(2,1)S(1)}, bf16[2,768,384]{2,1,0:T(8,128)(2,1)S(1)}, bf16[2,768,192...) custom-call(s32[3]{0:T(128)S(1)} %pad_add_fusion.bits, ...), custom_call_target="tpu_custom_call" | custom-call | flops 18119393280 | bytes 62914560 | tf_op jit(solution)/shard_map/pallas_call | solution.py:598
  67.1 3.7 %shard_map.179 = (bf16[2,1024,384]{2,1,0:T(8,128)(2,1)S(1)}, bf16[2,1024,192]{2,1,0:T(8,128)(2,1)S(1)}, bf16[2,768,384]{2,1,0:T(8,128)(2,1)S(1)}, bf16[2,768,192...) custom-call(s32[3]{0:T(128)S(1)} %pad_add_fusion.bits, bf16[1024,768]{1,0:T(8,128)(2,1)S(1)} %bitcast.222, ...), custom_call_target="tpu_custom_call" | custom-call | flops 18119393280 | bytes 62914560 | tf_op jit(solution)/shard_map/pallas_call | solution.py:598
  71.8 3.0 collective-permute-done.13
  74.8 9.8 %collective-permute-done.14 = bf16[2,2,2,3,32,512]{5,4,3,2,1,0:T(8,128)(2,1)S(1)} collective-permute-done((bf16[2,2,2,3,32,512]{5,4,3,2,1,0:T(8,128)(2,1)S(1)}, bf16[2,2,2,3,32,512]{5,4,3,2,1,0:T(8,128)(2,1)S(1)}, u32[]{:S(2)}, u32[]{:S(2)}) %collective-permute-start.14) | collective-permute-done | bytes 786464 | tf_op jit(solution)/shard_map/ppermute | solution.py:746
  90.3 7.1 %shard_map.180 = (bf16[2,1024,192]{2,1,0:T(8,128)(2,1)S(1)}, f32[2,1024,3]{2,1,0:T(8,128)S(1)}) custom-call(s32[3]{0:T(128)S(1)} %pad_add_fusion.bits, s32[2]{0:T(128)S(1)} %dynamic-slice_reduce_fusion.lens, bf16[2,1024,384]{2,1,0:T(8,128)(2,1)S(1)} %get-tuple-element.149.qk, bf16[2,1024,192]{2,1,0:T(8,128)(2,1)S(1)} %get-tuple-element.161.v, ...), custom_call_target="tpu_custom_call" | custom-call | flops 32212254720 | bytes 31457280 | tf_op jit(solution)/shard_map/pallas_call | solution.py:425
  99.8 7.1 %shard_map.181 = (bf16[2,1024,192]{2,1,0:T(8,128)(2,1)S(1)}, f32[2,1024,3]{2,1,0:T(8,128)S(1)}) custom-call(s32[3]{0:T(128)S(1)} %pad_add_fusion.bits, s32[2]{0:T(128)S(1)} %dynamic-slice_reduce_fusion.lens, bf16[2,1024,384]{2,1,0:T(8,128)(2,1)S(1)} %get-tuple-element.155.qk, bf16[2,1024,192]{2,1,0:T(8,128)(2,1)S(1)} %get-tuple-element.166.v, ...), custom_call_target="tpu_custom_call" | custom-call | flops 32212254720 | bytes 31457280 | tf_op jit(solution)/shard_map/pallas_call | solution.py:425
  107.0 4.0 %shard_map.182 = (bf16[1024,768]{1,0:T(8,128)(2,1)S(1)}, f32[1024,768]{1,0:T(8,128)S(1)}, f32[1024,1]{1,0:T(8,128)S(1)}, bf16[768,1024]{1,0:T(8,128)(2,1)S(1)}) custom-call(bf16[1024,768]{1,0:T(8,128)(2,1)S(1)} %bitcast.223, bf16[2,1024,192]{2,1,0:T(8,128)(2,1)S(1)} %get-tuple-element.162.m0.mixed, bf16[2,1024,192]{2,1,0:T(8,128)(2,1)S(1)} %get-tuple-element.169.m1.mixed, ...), custom_call_target="tpu_custom_call" | custom-call | flops 12079595520 | bytes 94371840 | tf_op jit(solution)/shard_map/pallas_call | solution.py:631
  111.1 6.8 %collective-permute-done.21 = bf16[2,2,2,96,512]{4,3,2,1,0:T(8,128)(2,1)S(1)} collective-permute-done((bf16[2,2,2,96,512]{4,3,2,1,0:T(8,128)(2,1)S(1)}, bf16[2,2,2,96,512]{4,3,2,1,0:T(8,128)(2,1)S(1)}, u32[]{:S(2)}, u32[]{:S(2)}) %collective-permute-start.21) | collective-permute-done | bytes 786464 | tf_op jit(solution)/shard_map/ppermute | solution.py:746
  121.0 4.9 %collective-permute-done.24 = bf16[2,2,96,256]{3,2,1,0:T(8,128)(2,1)S(1)} collective-permute-done((bf16[2,2,96,256]{3,2,1,0:T(8,128)(2,1)S(1)}, bf16[2,2,96,256]{3,2,1,0:T(8,128)(2,1)S(1)}, u32[]{:S(2)}, u32[]{:S(2)}) %collective-permute-start.24) | collective-permute-done | bytes 196640 | tf_op jit(solution)/shard_map/ppermute | solution.py:741
  129.2 10.4 %shard_map.183 = (bf16[4,1024,512]{2,1,0:T(8,128)(2,1)S(1)}, bf16[4,1024,512]{2,1,0:T(8,128)(2,1)S(1)}, f32[1024,768]{1,0:T(8,128)S(1)}) custom-call(s32[3]{0:T(128)S(1)} %pad_add_fusion.bits, bf16[1024,768]{1,0:T(8,128)(2,1)S(1)} %get-tuple-element.177.hid, bf16[2,2,2,2,96,512]{5,4,3,2,1,0:T(8,128)(2,1)S(1)} %pad_maximum_fusion.2.ua0.uap, ...), custom_call_target="tpu_custom_call" | custom-call | flops 64424509440 | bytes 125829120 | tf_op jit(solution)/shard_map/pallas_call | solution.py:160
  147.4 10.7 %shard_map.184 = (bf16[4,1024,256]{2,1,0:T(8,128)(2,1)S(1)}, bf16[4,1024,256]{2,1,0:T(8,128)(2,1)S(1)}, bf16[1024,768]{1,0:T(8,128)(2,1)}, f32[1024,768]{1,0:T(8...) custom-call(s32[3]{0:T(128)S(1)} %pad_add_fusion.bits, ...), custom_call_target="tpu_custom_call" | custom-call | flops 32212254720 | bytes 157286400 | tf_op jit(solution)/shard_map/pallas_call | solution.py:221
  158.1 4.1 %copy-done.65 = bf16[4,1024,512]{2,1,0:T(8,128)(2,1)S(1)} copy-done((bf16[4,1024,512]{2,1,0:T(8,128)(2,1)S(1)}, bf16[4,1024,512]{2,1,0:T(8,128)(2,1)}, u32[]{:S(2)}) %copy-start.65) | copy-done | bytes 4194328
  162.2 7.0 %shard_map.185 = (bf16[2,2,2,2,96,768]{5,4,3,2,1,0:T(8,128)(2,1)S(1)}, bf16[2,2,2,2,96,768]{5,4,3,2,1,0:T(8,128)(2,1)S(1)}) custom-call(s32[3]{0:T(128)S(1)} %pad_add_fusion.bits, bf16[768,1024]{1,0:T(8,128)(2,1)S(1)} %get-tuple-element.185.dt, bf16[4,1024,512]{2,1,0:T(8,128)(2,1)S(1)} %copy-done.65, bf16[4,1024,256]{2,1,0:T(8,128)(2,1)S(1)} %get-tuple-element.187.actq), custom_call_target="tpu_custom_call" | custom-call | flops 48318382080 | bytes 110100480 | tf_op jit(solution)/shard_map/pallas_call | solution.py:265
  169.4 10.2 %shard_map.186 = (bf16[2,2,2,2,96,768]{5,4,3,2,1,0:T(8,128)(2,1)S(1)}, f32[1024,768]{1,0:T(8,128)S(1)}) custom-call(s32[3]{0:T(128)S(1)} %pad_add_fusion.bits, bf16[768,1024]{1,0:T(8,128)(2,1)S(1)} %get-tuple-element.184.ht, bf16[1024,768]{1,0:T(8,128)(2,1)S(1)} %get-tuple-element.196.dffn, ...), custom_call_target="tpu_custom_call" | custom-call | flops 72477573120 | bytes 235929600 | tf_op jit(solution)/shard_map/pallas_call | solution.py:363
  185.5 17.0 %shard_map.187 = (bf16[2,2,2,2,96,768]{5,4,3,2,1,0:T(8,128)(2,1)S(1)}, f32[1024,768]{1,0:T(8,128)}, bf16[1024,768]{1,0:T(8,128)(2,1)S(1)}, bf16[768,1024]{1,0:T(...) custom-call(s32[3]{0:T(128)S(1)} %pad_add_fusion.bits, bf16[768,1024]{1,0:T(8,128)(2,1)S(1)} %get-tuple-element.184.ht, ...), custom_call_target="tpu_custom_call" | custom-call | flops 72477573120 | bytes 235929600 | tf_op jit(solution)/shard_map/pallas_call | solution.py:363
  209.8 15.0 %shard_map.188 = (bf16[2,1024,384]{2,1,0:T(8,128)(2,1)S(1)}, bf16[2,1024,192]{2,1,0:T(8,128)(2,1)S(1)}, bf16[2,2,2,2,3,32,512]{6,5,4,3,2,1,0:T(8,128)(2,1)S(1)}, bf16[2,2,2,2,3,32,512]{6,5,4,3,2,1,0:T(8,128)(2,1)S(1)}) custom-call(s32[3]{0:T(128)S(1)} %pad_add_fusion.bits, s32[2]{0:T(128)S(1)} %copy-done.15, bf16[2,1024,384]{2,1,0:T(8,128)(2,1)S(1)} %copy-done.37, ...), custom_call_target="tpu_custom_call" | custom-call | flops 80530636800 | bytes 58982400 | tf_op jit(solution)/shard_map/pallas_call | solution.py:558
  229.7 4.8 %shard_map.189 = (bf16[2,2,2,2,96,384]{5,4,3,2,1,0:T(8,128)(2,1)S(1)}, bf16[2,2,2,2,96,384]{5,4,3,2,1,0:T(8,128)(2,1)S(1)}) custom-call(s32[3]{0:T(128)S(1)} %pad_add_fusion.bits, bf16[768,1024]{1,0:T(8,128)(2,1)S(1)} %copy-done.32, bf16[768,1024]{1,0:T(8,128)(2,1)S(1)} %copy-done.48, bf16[2,1024,384]{2,1,0:T(8,128)(2,1)S(1)} %copy-done.51, ...), custom_call_target="tpu_custom_call" | custom-call | flops 24159191040 | bytes 62914560 | tf_op jit(solution)/shard_map/pallas_call | solution.py:697
  243.9 15.2 %shard_map.190 = (bf16[2,1024,384]{2,1,0:T(8,128)(2,1)S(1)}, bf16[2,1024,192]{2,1,0:T(8,128)(2,1)S(1)}, bf16[2,2,2,3,32,512]{5,4,3,2,1,0:T(8,128)(2,1)S(1)}, bf1...) custom-call(s32[3]{0:T(128)S(1)} %pad_add_fusion.bits, ...), custom_call_target="tpu_custom_call" | custom-call | flops 80530636800 | bytes 58982400 | tf_op jit(solution)/shard_map/pallas_call | solution.py:558
  268.4 4.9 %shard_map.191 = (bf16[2,2,2,96,384]{4,3,2,1,0:T(8,128)(2,1)S(1)}, bf16[2,2,2,96,384]{4,3,2,1,0:T(8,128)(2,1)S(1)}, bf16[2,2,2,96,384]{4,3,2,1,0:T(8,128)(2,1)S(1)}, bf16[2,2,2,96,384]{4,3,2,1,0:T(8,128)(2,1)S(1)}) custom-call(s32[3]{0:T(128)S(1)} %pad_add_fusion.bits, bf16[768,1024]{1,0:T(8,128)(2,1)S(1)} %copy-done.33, bf16[768,1024]{1,0:T(8,128)(2,1)S(1)} %copy-done.49, ...), custom_call_target="tpu_custom_call" | custom-call | flops 24159191040 | bytes 62914560 | tf_op jit(solution)/shard_map/pallas_call | solution.py:697
  276.4 3.4 %collective-permute-done.47 = bf16[2,2,96,768]{3,2,1,0:T(8,128)(2,1)S(1)} collective-permute-done((bf16[2,2,96,768]{3,2,1,0:T(8,128)(2,1)S(1)}, bf16[2,2,96,768]{3,2,1,0:T(8,128)(2,1)S(1)}, u32[]{:S(2)}, u32[]{:S(2)}) %collective-permute-start.47) | collective-permute-done | bytes 589856 | tf_op jit(solution)/shard_map/ppermute | solution.py:741
  279.8 4.3 %collective-permute-done.48 = bf16[2,2,2,3,32,512]{5,4,3,2,1,0:T(8,128)(2,1)S(1)} collective-permute-done((bf16[2,2,2,3,32,512]{5,4,3,2,1,0:T(8,128)(2,1)S(1)}, bf16[2,2,2,3,32,512]{5,4,3,2,1,0:T(8,128)(2,1)S(1)}, u32[]{:S(2)}, u32[]{:S(2)}) %collective-permute-start.48) | collective-permute-done | bytes 786464 | tf_op jit(solution)/shard_map/ppermute | solution.py:746
  284.1 4.2 %collective-permute-done.49 = bf16[2,2,2,3,32,512]{5,4,3,2,1,0:T(8,128)(2,1)S(1)} collective-permute-done((bf16[2,2,2,3,32,512]{5,4,3,2,1,0:T(8,128)(2,1)S(1)}, bf16[2,2,2,3,32,512]{5,4,3,2,1,0:T(8,128)(2,1)S(1)}, u32[]{:S(2)}, u32[]{:S(2)}) %collective-permute-start.49) | collective-permute-done | bytes 786464 | tf_op jit(solution)/shard_map/ppermute | solution.py:741
  292.9 7.1 %shard_map.192 = f32[1024,768]{1,0:T(8,128)} custom-call(f32[1024,768]{1,0:T(8,128)S(1)} %copy-done.53, bf16[2,1024,384]{2,1,0:T(8,128)(2,1)S(1)} %get-tuple-element.256.dqk.dqk0, bf16[2,1024,384]{2,1,0:T(8,128)(2,1)S(1)} %copy-done.52, bf16[2,1024,192]{2,1,0:T(8,128)(2,1)S(1)} %copy-done.61, bf16[2,1024,192]{2,1,0:T(8,128)(2,1)S(1)} %copy-done.63, ...), custom_call_target="tpu_custom_call" | custom-call | flops 36238786560 | bytes 110100480 | tf_op jit(solution)/shard_map/pallas_call | solution.py:723
  303.0 3.2 collective-permute-done.52
  315.8 6.0 %collective-permute-done.59 = bf16[2,2,3,32,512]{4,3,2,1,0:T(8,128)(2,1)S(1)} collective-permute-done((bf16[2,2,3,32,512]{4,3,2,1,0:T(8,128)(2,1)S(1)}, bf16[2,2,3,32,512]{4,3,2,1,0:T(8,128)(2,1)S(1)}, u32[]{:S(2)}, u32[]{:S(2)}) %collective-permute-start.59) | collective-permute-done | bytes 393248 | tf_op jit(solution)/shard_map/ppermute | solution.py:741
  (349 shorter events, 117.2 us)
Async XLA Ops:
  25.0 11.6 %collective-permute-start.4 = (bf16[2,3,32,512]{3,2,1,0:T(8,128)(2,1)S(1)}, bf16[2,3,32,512]{3,2,1,0:T(8,128)(2,1)S(1)}, u32[]{:S(2)}, u32[]{:S(2)}) collective-permute-start(bf16[2,3,32,512]{3,2,1,0:T(8,128)(2,1)S(1)} %pad_maximum_fusion.28), channel_id=1, source_target_pairs={{0,16},{4,20},{8,24},{12,28},{16,0},{20,4},{24,8},{28,12},{1,17},{... | collective-permute-start | bytes 589832 | tf_op jit(solution)/shard_map/ppermute | solution.py:741
  36.7 15.2 %collective-permute-start.6 = (bf16[2,2,2,96,384]{4,3,2,1,0:T(8,128)(2,1)S(1)}, bf16[2,2,2,96,384]{4,3,2,1,0:T(8,128)(2,1)S(1)}, u32[]{:S(2)}, u32[]{:S(2)}) collective-permute-start(bf16[2,2,2,96,384]{4,3,2,1,0:T(8,128)(2,1)S(1)} %pad_maximum_fusion.12), channel_id=1, source_target_pairs={{0,2},{1,3},{2,0},{3,1},{4,6},{5,7},{6,4},{7,5},{8,10},{9,11},{10,... | collective-permute-start | bytes 1769480 | tf_op jit(solution)/shard_map/ppermute | solution.py:746
  37.3 14.6 %collective-permute-start.7 = (bf16[2,2,2,96,384]{4,3,2,1,0:T(8,128)(2,1)S(1)}, bf16[2,2,2,96,384]{4,3,2,1,0:T(8,128)(2,1)S(1)}, u32[]{:S(2)}, u32[]{:S(2)}) collective-permute-start(bf16[2,2,2,96,384]{4,3,2,1,0:T(8,128)(2,1)S(1)} %pad_maximum_fusion.13), channel_id=1, source_target_pairs={{0,4},{4,0},{8,12},{12,8},{16,20},{20,16},{24,28},{28,24},{1,5},{5... | collective-permute-start | bytes 1769480 | tf_op jit(solution)/shard_map/ppermute | solution.py:741
  47.5 16.7 %collective-permute-start.12 = (bf16[2,96,512]{2,1,0:T(8,128)(2,1)S(1)}, bf16[2,96,512]{2,1,0:T(8,128)(2,1)S(1)}, u32[]{:S(2)}, u32[]{:S(2)}) collective-permute-start(bf16[2,96,512]{2,1,0:T(8,128)(2,1)S(1)} %pad_maximum_fusion.29), channel_id=1, source_target_pairs={{0,16},{4,20},{8,24},{12,28},{16,0},{20,4},{24,8},{28,12},{1,17},{... | collective-permute-start | bytes 589832 | tf_op jit(solution)/shard_map/ppermute | solution.py:741
  51.8 11.2 %collective-permute-start.8 = (bf16[2,2,3,32,512]{4,3,2,1,0:T(8,128)(2,1)S(1)}, bf16[2,2,3,32,512]{4,3,2,1,0:T(8,128)(2,1)S(1)}, u32[]{:S(2)}, u32[]{:S(2)}) collective-permute-start(bf16[2,2,3,32,512]{4,3,2,1,0:T(8,128)(2,1)S(1)} %get-tuple-element.146), channel_id=1, source_target_pairs={{0,4},{4,0},{8,12},{12,8},{16,20},{20,16},{24,28},{28,24},{1,5},{5... | collective-permute-start | bytes 1179656 | tf_op jit(solution)/shard_map/ppermute | solution.py:741
  66.1 18.6 %collective-permute-start.14 = (bf16[2,2,2,3,32,512]{5,4,3,2,1,0:T(8,128)(2,1)S(1)}, bf16[2,2,2,3,32,512]{5,4,3,2,1,0:T(8,128)(2,1)S(1)}, u32[]{:S(2)}, u32[]{:S(2)}) collective-permute-start(bf16[2,2,2,3,32,512]{5,4,3,2,1,0:T(8,128)(2,1)S(1)} %pad_maximum_fusion.6), channel_id=1, source_target_pairs={{0,2},{1,3},{2,0},{3,1},{4,6},{5,7},{6,4},{7,5},{8,10},{9,11},{10,... | collective-permute-start | bytes 2359304 | tf_op jit(solution)/shard_map/ppermute | solution.py:746
  66.6 18.3 %collective-permute-start.15 = (bf16[2,2,2,3,32,512]{5,4,3,2,1,0:T(8,128)(2,1)S(1)}, bf16[2,2,2,3,32,512]{5,4,3,2,1,0:T(8,128)(2,1)S(1)}, u32[]{:S(2)}, u32[]{:S(2)}) collective-permute-start(bf16[2,2,2,3,32,512]{5,4,3,2,1,0:T(8,128)(2,1)S(1)} %pad_maximum_fusion.7), channel_id=1, source_target_pairs={{0,4},{4,0},{8,12},{12,8},{16,20},{20,16},{24,28},{28,24},{1,5},{5... | collective-permute-start | bytes 2359304 | tf_op jit(solution)/shard_map/ppermute | solution.py:741
  85.1 12.3 %collective-permute-start.18 = (bf16[2,96,256]{2,1,0:T(8,128)(2,1)S(1)}, bf16[2,96,256]{2,1,0:T(8,128)(2,1)S(1)}, u32[]{:S(2)}, u32[]{:S(2)}) collective-permute-start(bf16[2,96,256]{2,1,0:T(8,128)(2,1)S(1)} %pad_maximum_fusion.34), channel_id=1, source_target_pairs={{0,16},{4,20},{8,24},{12,28},{16,0},{20,4},{24,8},{28,12},{1,17},{... | collective-permute-start | bytes 294920 | tf_op jit(solution)/shard_map/ppermute | solution.py:741
  98.4 12.7 %collective-permute-start.23 = (bf16[2,2,96,256]{3,2,1,0:T(8,128)(2,1)S(1)}, bf16[2,2,96,256]{3,2,1,0:T(8,128)(2,1)S(1)}, u32[]{:S(2)}, u32[]{:S(2)}) collective-permute-start(bf16[2,2,96,256]{3,2,1,0:T(8,128)(2,1)S(1)} %pad_maximum_fusion.30), channel_id=1, source_target_pairs={{0,8},{4,12},{8,0},{12,4},{16,24},{20,28},{24,16},{28,20},{1,9},{5... | collective-permute-start | bytes 589832 | tf_op jit(solution)/shard_map/ppermute | solution.py:741
  98.8 19.2 %collective-permute-start.21 = (bf16[2,2,2,96,512]{4,3,2,1,0:T(8,128)(2,1)S(1)}, bf16[2,2,2,96,512]{4,3,2,1,0:T(8,128)(2,1)S(1)}, u32[]{:S(2)}, u32[]{:S(2)}) collective-permute-start(bf16[2,2,2,96,512]{4,3,2,1,0:T(8,128)(2,1)S(1)} %pad_maximum_fusion.8), channel_id=1, source_target_pairs={{0,2},{1,3},{2,0},{3,1},{4,6},{5,7},{6,4},{7,5},{8,10},{9,11},{10,... | collective-permute-start | bytes 2359304 | tf_op jit(solution)/shard_map/ppermute | solution.py:746
  99.3 18.9 %collective-permute-start.22 = (bf16[2,2,2,96,512]{4,3,2,1,0:T(8,128)(2,1)S(1)}, bf16[2,2,2,96,512]{4,3,2,1,0:T(8,128)(2,1)S(1)}, u32[]{:S(2)}, u32[]{:S(2)}) collective-permute-start(bf16[2,2,2,96,512]{4,3,2,1,0:T(8,128)(2,1)S(1)} %pad_maximum_fusion.9), channel_id=1, source_target_pairs={{0,4},{4,0},{8,12},{12,8},{16,20},{20,16},{24,28},{28,24},{1,5},{5... | collective-permute-start | bytes 2359304 | tf_op jit(solution)/shard_map/ppermute | solution.py:741
  126.2 17.6 %collective-permute-start.28 = (bf16[2,2,2,96,256]{4,3,2,1,0:T(8,128)(2,1)S(1)}, bf16[2,2,2,96,256]{4,3,2,1,0:T(8,128)(2,1)S(1)}, u32[]{:S(2)}, u32[]{:S(2)}) collective-permute-start(bf16[2,2,2,96,256]{4,3,2,1,0:T(8,128)(2,1)S(1)} %pad_maximum_fusion.19), channel_id=1, source_target_pairs={{0,2},{1,3},{2,0},{3,1},{4,6},{5,7},{6,4},{7,5},{8,10},{9,11},{10,... | collective-permute-start | bytes 1179656 | tf_op jit(solution)/shard_map/ppermute | solution.py:746
  127.7 16.1 %collective-permute-start.29 = (bf16[2,2,2,96,256]{4,3,2,1,0:T(8,128)(2,1)S(1)}, bf16[2,2,2,96,256]{4,3,2,1,0:T(8,128)(2,1)S(1)}, u32[]{:S(2)}, u32[]{:S(2)}) collective-permute-start(bf16[2,2,2,96,256]{4,3,2,1,0:T(8,128)(2,1)S(1)} %pad_maximum_fusion.20), channel_id=1, source_target_pairs={{0,4},{4,0},{8,12},{12,8},{16,20},{20,16},{24,28},{28,24},{1,5},{5... | collective-permute-start | bytes 1179656 | tf_op jit(solution)/shard_map/ppermute | solution.py:741
  181.8 44.2 %collective-permute-start.35 = (bf16[2,2,2,96,768]{4,3,2,1,0:T(8,128)(2,1)}, bf16[2,2,2,96,768]{4,3,2,1,0:T(8,128)(2,1)}, u32[]{:S(2)}, u32[]{:S(2)}) collective-permute-start(bf16[2,2,2,96,768]{4,3,2,1,0:T(8,128)(2,1)} %fusion), channel_id=1, source_target_pairs={{0,4},{4,0},{8,12},{12,8},{16,20},{20,16},{24,28},{28,24},{1,5},{5... | collective-permute-start | bytes 3538952 | tf_op jit(solution)/shard_map/ppermute | solution.py:741
  182.3 21.4 %collective-permute-start.33 = (bf16[2,2,2,2,96,768]{5,4,3,2,1,0:T(8,128)(2,1)S(1)}, bf16[2,2,2,2,96,768]{5,4,3,2,1,0:T(8,128)(2,1)}, u32[]{:S(2)}, u32[]{:S(2)}) collective-permute-start(bf16[2,2,2,2,96,768]{5,4,3,2,1,0:T(8,128)(2,1)S(1)} %get-tuple-element.202), channel_id=1, source_target_pairs={{0,1},{1,0},{2,3},{3,2},{4,5},{5,4},{6,7},{7,6},{8,9},{9,8},{10,11... | collective-permute-start | bytes 7077896 | tf_op jit(solution)/shard_map/ppermute | solution.py:746
  203.8 22.3 %collective-permute-start.34 = (f32[4,768]{1,0:T(4,128)S(1)}, f32[4,768]{1,0:T(4,128)S(1)}, u32[]{:S(2)}, u32[]{:S(2)}) collective-permute-start(f32[4,768]{1,0:T(4,128)S(1)} %pad_maximum_fusion.35), channel_id=1, source_target_pairs={{0,1},{1,0},{2,3},{3,2},{4,5},{5,4},{6,7},{7,6},{8,9},{9,8},{10,11... | collective-permute-start | bytes 36872 | tf_op jit(solution)/shard_map/ppermute | solution.py:829
  206.6 28.0 %collective-permute-start.39 = (bf16[2,2,2,96,768]{4,3,2,1,0:T(8,128)(2,1)S(1)}, bf16[2,2,2,96,768]{4,3,2,1,0:T(8,128)(2,1)S(1)}, u32[]{:S(2)}, u32[]{:S(2)}) collective-permute-start(bf16[2,2,2,96,768]{4,3,2,1,0:T(8,128)(2,1)S(1)} %fusion.1), channel_id=1, source_target_pairs={{0,2},{1,3},{2,0},{3,1},{4,6},{5,7},{6,4},{7,5},{8,10},{9,11},{10,... | collective-permute-start | bytes 3538952 | tf_op jit(solution)/shard_map/ppermute | solution.py:746
  240.6 18.6 %collective-permute-start.42 = (bf16[2,2,2,2,96,384]{5,4,3,2,1,0:T(8,128)(2,1)S(1)}, bf16[2,2,2,2,96,384]{5,4,3,2,1,0:T(8,128)(2,1)S(1)}, u32[]{:S(2)}, u32[]{:S(2)}) collective-permute-start(bf16[2,2,2,2,96,384]{5,4,3,2,1,0:T(8,128)(2,1)S(1)} %get-tuple-element.240), channel_id=1, source_target_pairs={{0,1},{1,0},{2,3},{3,2},{4,5},{5,4},{6,7},{7,6},{8,9},{9,8},{10,11... | collective-permute-start | bytes 3538952 | tf_op jit(solution)/shard_map/ppermute | solution.py:746
  240.6 18.6 %collective-permute-start.43 = (bf16[2,2,2,2,96,384]{5,4,3,2,1,0:T(8,128)(2,1)S(1)}, bf16[2,2,2,2,96,384]{5,4,3,2,1,0:T(8,128)(2,1)S(1)}, u32[]{:S(2)}, u32[]{:S(2)}) collective-permute-start(bf16[2,2,2,2,96,384]{5,4,3,2,1,0:T(8,128)(2,1)S(1)} %get-tuple-element.241), channel_id=1, source_target_pairs={{0,1},{1,0},{2,3},{3,2},{4,5},{5,4},{6,7},{7,6},{8,9},{9,8},{10,11... | collective-permute-start | bytes 3538952 | tf_op jit(solution)/shard_map/ppermute | solution.py:746
  241.1 18.0 %collective-permute-start.41 = (f32[4,768]{1,0:T(4,128)S(1)}, f32[4,768]{1,0:T(4,128)S(1)}, u32[]{:S(2)}, u32[]{:S(2)}) collective-permute-start(f32[4,768]{1,0:T(4,128)S(1)} %add.275), channel_id=1, source_target_pairs={{0,16},{4,20},{8,24},{12,28},{16,0},{20,4},{24,8},{28,12},{1,17},{... | collective-permute-start | bytes 36872 | tf_op jit(solution)/shard_map/ppermute | solution.py:829
  241.5 17.7 %collective-permute-start.44 = (bf16[2,2,96,768]{3,2,1,0:T(8,128)(2,1)}, bf16[2,2,96,768]{3,2,1,0:T(8,128)(2,1)}, u32[]{:S(2)}, u32[]{:S(2)}) collective-permute-start(bf16[2,2,96,768]{3,2,1,0:T(8,128)(2,1)} %fusion.4), channel_id=1, source_target_pairs={{0,2},{1,3},{2,0},{3,1},{4,6},{5,7},{6,4},{7,5},{8,10},{9,11},{10,... | collective-permute-start | bytes 1769480 | tf_op jit(solution)/shard_map/ppermute | solution.py:746
  242.3 16.8 %collective-permute-start.45 = (bf16[2,2,96,768]{3,2,1,0:T(8,128)(2,1)}, bf16[2,2,96,768]{3,2,1,0:T(8,128)(2,1)}, u32[]{:S(2)}, u32[]{:S(2)}) collective-permute-start(bf16[2,2,96,768]{3,2,1,0:T(8,128)(2,1)} %fusion.3), channel_id=1, source_target_pairs={{0,4},{4,0},{8,12},{12,8},{16,20},{20,16},{24,28},{28,24},{1,5},{5... | collective-permute-start | bytes 1769480 | tf_op jit(solution)/shard_map/ppermute | solution.py:741
  263.6 20.5 %collective-permute-start.48 = (bf16[2,2,2,3,32,512]{5,4,3,2,1,0:T(8,128)(2,1)S(1)}, bf16[2,2,2,3,32,512]{5,4,3,2,1,0:T(8,128)(2,1)S(1)}, u32[]{:S(2)}, u32[]{:S(2)}) collective-permute-start(bf16[2,2,2,3,32,512]{5,4,3,2,1,0:T(8,128)(2,1)S(1)} %get-tuple-element.250), channel_id=1, source_target_pairs={{0,2},{1,3},{2,0},{3,1},{4,6},{5,7},{6,4},{7,5},{8,10},{9,11},{10,... | collective-permute-start | bytes 2359304 | tf_op jit(solution)/shard_map/ppermute | solution.py:746
  266.7 13.1 %collective-permute-start.47 = (bf16[2,2,96,768]{3,2,1,0:T(8,128)(2,1)S(1)}, bf16[2,2,96,768]{3,2,1,0:T(8,128)(2,1)S(1)}, u32[]{:S(2)}, u32[]{:S(2)}) collective-permute-start(bf16[2,2,96,768]{3,2,1,0:T(8,128)(2,1)S(1)} %pad_maximum_fusion.14), channel_id=1, source_target_pairs={{0,8},{4,12},{8,0},{12,4},{16,24},{20,28},{24,16},{28,20},{1,9},{5... | collective-permute-start | bytes 1769480 | tf_op jit(solution)/shard_map/ppermute | solution.py:741
  267.9 20.5 %collective-permute-start.49 = (bf16[2,2,2,3,32,512]{5,4,3,2,1,0:T(8,128)(2,1)S(1)}, bf16[2,2,2,3,32,512]{5,4,3,2,1,0:T(8,128)(2,1)S(1)}, u32[]{:S(2)}, u32[]{:S(2)}) collective-permute-start(bf16[2,2,2,3,32,512]{5,4,3,2,1,0:T(8,128)(2,1)S(1)} %get-tuple-element.251), channel_id=1, source_target_pairs={{0,4},{4,0},{8,12},{12,8},{16,20},{20,16},{24,28},{28,24},{1,5},{5... | collective-permute-start | bytes 2359304 | tf_op jit(solution)/shard_map/ppermute | solution.py:741
  273.3 26.7 %collective-permute-start.50 = (bf16[2,2,2,96,384]{4,3,2,1,0:T(8,128)(2,1)S(1)}, bf16[2,2,2,96,384]{4,3,2,1,0:T(8,128)(2,1)S(1)}, u32[]{:S(2)}, u32[]{:S(2)}) collective-permute-start(bf16[2,2,2,96,384]{4,3,2,1,0:T(8,128)(2,1)S(1)} %get-tuple-element.262), channel_id=1, source_target_pairs={{0,2},{1,3},{2,0},{3,1},{4,6},{5,7},{6,4},{7,5},{8,10},{9,11},{10,... | collective-permute-start | bytes 1769480 | tf_op jit(solution)/shard_map/ppermute | solution.py:746
  274.2 26.7 %collective-permute-start.51 = (bf16[2,2,2,96,384]{4,3,2,1,0:T(8,128)(2,1)S(1)}, bf16[2,2,2,96,384]{4,3,2,1,0:T(8,128)(2,1)S(1)}, u32[]{:S(2)}, u32[]{:S(2)}) collective-permute-start(bf16[2,2,2,96,384]{4,3,2,1,0:T(8,128)(2,1)S(1)} %get-tuple-element.263), channel_id=1, source_target_pairs={{0,4},{4,0},{8,12},{12,8},{16,20},{20,16},{24,28},{28,24},{1,5},{5... | collective-permute-start | bytes 1769480 | tf_op jit(solution)/shard_map/ppermute | solution.py:741
  288.5 12.5 %collective-permute-start.54 = (bf16[2,96,768]{2,1,0:T(8,128)(2,1)S(1)}, bf16[2,96,768]{2,1,0:T(8,128)(2,1)S(1)}, u32[]{:S(2)}, u32[]{:S(2)}) collective-permute-start(bf16[2,96,768]{2,1,0:T(8,128)(2,1)S(1)} %pad_maximum_fusion.24), channel_id=1, source_target_pairs={{0,16},{4,20},{8,24},{12,28},{16,0},{20,4},{24,8},{28,12},{1,17},{... | collective-permute-start | bytes 884744 | tf_op jit(solution)/shard_map/ppermute | solution.py:741
  290.3 12.7 %collective-permute-start.53 = (bf16[2,2,3,32,512]{4,3,2,1,0:T(8,128)(2,1)S(1)}, bf16[2,2,3,32,512]{4,3,2,1,0:T(8,128)(2,1)S(1)}, u32[]{:S(2)}, u32[]{:S(2)}) collective-permute-start(bf16[2,2,3,32,512]{4,3,2,1,0:T(8,128)(2,1)S(1)} %fusion.7), channel_id=1, source_target_pairs={{0,2},{1,3},{2,0},{3,1},{4,6},{5,7},{6,4},{7,5},{8,10},{9,11},{10,... | collective-permute-start | bytes 1179656 | tf_op jit(solution)/shard_map/ppermute | solution.py:746
  291.3 14.8 %collective-permute-start.52 = (bf16[2,2,3,32,512]{4,3,2,1,0:T(8,128)(2,1)S(1)}, bf16[2,2,3,32,512]{4,3,2,1,0:T(8,128)(2,1)S(1)}, u32[]{:S(2)}, u32[]{:S(2)}) collective-permute-start(bf16[2,2,3,32,512]{4,3,2,1,0:T(8,128)(2,1)S(1)} %fusion.6), channel_id=1, source_target_pairs={{0,4},{4,0},{8,12},{12,8},{16,20},{20,16},{24,28},{28,24},{1,5},{5... | collective-permute-start | bytes 1179656 | tf_op jit(solution)/shard_map/ppermute | solution.py:741
  309.0 12.8 %collective-permute-start.59 = (bf16[2,2,3,32,512]{4,3,2,1,0:T(8,128)(2,1)S(1)}, bf16[2,2,3,32,512]{4,3,2,1,0:T(8,128)(2,1)S(1)}, u32[]{:S(2)}, u32[]{:S(2)}) collective-permute-start(bf16[2,2,3,32,512]{4,3,2,1,0:T(8,128)(2,1)S(1)} %pad_maximum_fusion.21), channel_id=1, source_target_pairs={{0,8},{4,12},{8,0},{12,4},{16,24},{20,28},{24,16},{28,20},{1,9},{5... | collective-permute-start | bytes 1179656 | tf_op jit(solution)/shard_map/ppermute | solution.py:741
  314.4 11.6 %collective-permute-start.57 = (bf16[2,2,96,384]{3,2,1,0:T(8,128)(2,1)S(1)}, bf16[2,2,96,384]{3,2,1,0:T(8,128)(2,1)S(1)}, u32[]{:S(2)}, u32[]{:S(2)}) collective-permute-start(bf16[2,2,96,384]{3,2,1,0:T(8,128)(2,1)S(1)} %pad_maximum_fusion.25), channel_id=1, source_target_pairs={{0,8},{4,12},{8,0},{12,4},{16,24},{20,28},{24,16},{28,20},{1,9},{5... | collective-permute-start | bytes 884744 | tf_op jit(solution)/shard_map/ppermute | solution.py:741
  (110 other events, 1269.7 us)

commit v3 on v2

--- a/solution.py
+++ b/solution.py
@@ -127,7 +127,7 @@
         assemble(wd, db1, bits, True)
 
 
-def ffn_units(chunk, hid, wu, wd, act_o, gp_o, acc):
+def ffn_units(chunk, hid, wu, wd, act_o, gp_o, acc, finish=None):
     rows = hid.shape[0]
     ats = [pl.ds(r * chunk, chunk) for r in range(rows // chunk)]
     ahead = dot_nn(hid[ats[0], :], wu[...])
@@ -139,6 +139,8 @@
         act_o[0, at, :] = act
         gp_o[0, at, :] = gp.astype(gp_o.dtype)
         acc[at, :] += dot_nt(act, wd[...])
+        if finish is not None:
+            finish(r * chunk, chunk)
 
 
 def ffn_part_kernel(chunk, bits, hid, ua0, ua1, db0, db1, act_o, gp_o, acc, wu, wd):
@@ -159,7 +161,7 @@
     col = pl.BlockSpec((1, rows, n), lambda k, *_: (k, 0, 0))
     return pl.pallas_call(
         functools.partial(ffn_part_kernel, chunk),
-        out_shape=(sds((4, rows, n), BF16), sds((4, rows, n), GP), sds((rows, width), F32)),
+        out_shape=(pltpu.HBM((4, rows, n), BF16), pltpu.HBM((4, rows, n), GP), sds((rows, width), F32)),
         grid_spec=pltpu.PrefetchScalarGridSpec(
             num_scalar_prefetch=1, grid=(4,),
             in_specs=[whole((rows, width)), spec_a((p, n), low_pick), spec_a((p, n), high_pick),
@@ -182,7 +184,9 @@
     def _():
         acc[...] = part[...]
 
-    ffn_units(chunk, hid, wu, wd, act_o, gp_o, acc)
+    @pl.when(k < 3)
+    def _():
+        ffn_units(chunk, hid, wu, wd, act_o, gp_o, acc)
 
     @pl.when(k == 3)
     def _():
@@ -190,25 +194,28 @@
         small = 256
         g = gain[...]
         b = bias[...]
-        dg = jnp.zeros_like(g)
-        db = jnp.zeros_like(g)
-        for r in range(rows // small):
-            at = pl.ds(r * small, small)
-            size = lens[r * small // length]
-            pos = (r * small % length) + lax.broadcasted_iota(jnp.int32, (small, 1), 0)
-            valid = pos < size
-            unit, inverse = norm_stats(acc[at, :])
-            out[at, :] = jnp.where(valid, unit * g + b, 0.0).astype(BF16)
-            dy = jnp.where(valid, dout[at, :].astype(F32), 0.0)
-            dg += jnp.sum(dy * unit, axis=0, keepdims=True)
-            db += jnp.sum(dy, axis=0, keepdims=True)
-            dz = norm_back(dy * g, unit, inverse)
-            acc[at, :] = dz
-            low = dz.astype(BF16)
-            dffn[at, :] = low
-            dffnt[:, at] = low.T
-        dgain[...] = dg
-        dbias[...] = db
+        sums = [jnp.zeros_like(g), jnp.zeros_like(g)]
+
+        def finish(start, count):
+            for at0 in range(start, start + count, small):
+                at = pl.ds(at0, small)
+                size = lens[at0 // length]
+                pos = (at0 % length) + lax.broadcasted_iota(jnp.int32, (small, 1), 0)
+                valid = pos < size
+                unit, inverse = norm_stats(acc[at, :])
+                out[at, :] = jnp.where(valid, unit * g + b, 0.0).astype(BF16)
+                dy = jnp.where(valid, dout[at, :].astype(F32), 0.0)
+                sums[0] = sums[0] + jnp.sum(dy * unit, axis=0, keepdims=True)
+                sums[1] = sums[1] + jnp.sum(dy, axis=0, keepdims=True)
+                dz = norm_back(dy * g, unit, inverse)
+                acc[at, :] = dz
+                low = dz.astype(BF16)
+                dffn[at, :] = low
+                dffnt[:, at] = low.T
+
+        ffn_units(chunk, hid, wu, wd, act_o, gp_o, acc, finish)
+        dgain[...] = sums[0]
+        dbias[...] = sums[1]
 
 
 def ffn_rest(bits, lens, hid, ua0, ua1, db0, db1, part, gain, bias, dout, chunk=512):
@@ -297,41 +304,52 @@
         else:
             acc[...] = jnp.zeros_like(acc)
 
-    ats = [pl.ds(r * chunk, chunk) for r in range(rows // chunk)]
-    ahead = dot_nn(dffn[ats[0], :], wd[...])
-    for r, at in enumerate(ats):
-        dup_s[at, left] = (ahead[:, :np] * gpp[0, at, :].astype(F32)).astype(BF16)
-        dup_s[at, right] = (ahead[:, np:] * gpq[0, at, :].astype(F32)).astype(BF16)
-        if r + 1 < len(ats):
-            ahead = dot_nn(dffn[ats[r + 1], :], wd[...])
-        acc[at, :] += dot_nt(dup_s[at, :], wu[...])
-
-    grad = dot_nn(ht[...], dup_s[...]).astype(BF16)
-    p = gu.shape[-2]
-    for d in range(8):
-        piece(gu, bits, d, False)[...] = grad[d * p : (d + 1) * p]
-
-    if last:
-
-        @pl.when(k == 1)
-        def _():
-            small = 256
-            g = gain[...]
-            dg = jnp.zeros_like(g)
-            db = jnp.zeros_like(g)
-            for r in range(rows // small):
-                at = pl.ds(r * small, small)
+    def run(finish=None):
+        ats = [pl.ds(r * chunk, chunk) for r in range(rows // chunk)]
+        ahead = dot_nn(dffn[ats[0], :], wd[...])
+        for r, at in enumerate(ats):
+            dup_s[at, left] = (ahead[:, :np] * gpp[0, at, :].astype(F32)).astype(BF16)
+            dup_s[at, right] = (ahead[:, np:] * gpq[0, at, :].astype(F32)).astype(BF16)
+            if r + 1 < len(ats):
+                ahead = dot_nn(dffn[ats[r + 1], :], wd[...])
+            acc[at, :] += dot_nt(dup_s[at, :], wu[...])
+            if finish is not None:
+                finish(r * chunk, chunk)
+        grad = dot_nn(ht[...], dup_s[...]).astype(BF16)
+        p = gu.shape[-2]
+        for d in range(8):
+            piece(gu, bits, d, False)[...] = grad[d * p : (d + 1) * p]
+
+    if not last:
+        run()
+        return
+
+    @pl.when(k == 0)
+    def _():
+        run()
+
+    @pl.when(k == 1)
+    def _():
+        small = 256
+        g = gain[...]
+        sums = [jnp.zeros_like(g), jnp.zeros_like(g)]
+
+        def finish(start, count):
+            for at0 in range(start, start + count, small):
+                at = pl.ds(at0, small)
                 dh = acc[at, :]
                 u = unit[at, :]
-                dg += jnp.sum(dh * u, axis=0, keepdims=True)
-                db += jnp.sum(dh, axis=0, keepdims=True)
+                sums[0] = sums[0] + jnp.sum(dh * u, axis=0, keepdims=True)
+                sums[1] = sums[1] + jnp.sum(dh, axis=0, keepdims=True)
                 dz = norm_back(dh * g, u, inverse[at, :])
                 acc[at, :] = dz
                 low = dz.astype(BF16)
                 dattn[at, :] = low
                 dattnt[:, at] = low.T
-            dgain[...] = dg
-            dbias[...] = db
+
+        run(finish)
+        dgain[...] = sums[0]
+        dbias[...] = sums[1]
 
 
 def ffn_backward(last, bits, ht, dffn, uap, uaq, dbp, dbq, gpp, gpq, extra=(), chunk=512):
@@ -951,10 +969,10 @@
     ga_out, gb_out, dqk0, norms, cqk, cvo, yd, yu = after((ga_out, gb_out, dqk0, norms, cqk, cvo, yd, yu), dv0)
     xga = over_x(ga_out)
     norms = total_some(norms, *steps[2:3], *steps[5:])
+    gb_out, yu, yd, norms = after((gb_out, yu, yd, norms), norms)
+    xgb = over_y(gb_out)
     u, d = third_sum(up0, cu, xu, yu), third_sum(down0, cd, xd, yd)
     send_f = jnp.stack([u[1], d[1]]).astype(BF16)
-    send_f, gb_out, norms = after((send_f, gb_out, norms), norms)
-    xgb = over_y(gb_out)
     near_f = over_near(send_f)
     qka0, qka_out, vo0, vo_out = qkv_grads(True, bits, xt, dattnt, dqk0, dv0, m0, (cqk, cvo))
     xqk, xvo = over_x(qka_out), over_y(vo_out)

time: 339 us -> 331 us (0.976)
  local copies, waits for them, and re-layouts: 27.4 us -> 20 us
    unnamed x164 -> x166, local copies, waits for them, and re-layouts: 25.4 us -> 18 us
    ppermute x28, waiting for transfers between devices: 62.5 us -> 69.1 us  [partner_dp(): return lax.ppermute(value, 'dp', [(i, i ^ step) for i in range(size)])]
    ppermute x28, waiting for transfers between devices: 30.1 us -> 24.8 us  [partner_head(): return lax.ppermute(value, 'head', [(i, i ^ 1 << bit) for i in range(size)])]
where the time goes in v3:
time: 331 us; the launch traced here: 328 us
  Pallas kernels  127 us (38%)
  waiting for transfers between devices  95.4 us (29%)
  starting transfers between devices  62.6 us (19%)
  other arithmetic  20.6 us (6%)
  local copies, waits for them, and re-layouts  20 us (6%)
    ppermute x28, waiting for transfers between devices, partner_dp(): return lax.ppermute(value, 'dp', [(i, i ^ step) for i in range(size)])  69.1 us
    ppermute x28, starting transfers between devices, partner_dp(): return lax.ppermute(value, 'dp', [(i, i ^ step) for i in range(size)])  38.9 us
    pallas_call x2, Pallas kernels, attention_backward(): pl.pallas_call(functools.partial(att_bwd_kernel, last), out_shape=out_sha...  29.5 us
    pallas_call x2, Pallas kernels, ffn_backward(): pl.pallas_call(functools.partial(ffn_bwd_kernel, chunk, last), out_shape=...  26.4 us
    ppermute x28, waiting for transfers between devices, partner_head(): return lax.ppermute(value, 'head', [(i, i ^ 1 << bit) for i in range(size)])  24.8 us
    unnamed x166, local copies, waits for them, and re-layouts  18 us
    ppermute x28, starting transfers between devices, partner_head(): return lax.ppermute(value, 'head', [(i, i ^ 1 << bit) for i in range(size)])  18 us
    pallas_call x2, Pallas kernels, attention_forward(): pl.pallas_call(att_fwd_kernel, out_shape=(sds((2, rows, w1), BF16), sds((...  13.1 us
  transfers between devices with their start and end apart: 61, of which 28 were waited for; matrix products, arithmetic and copies ran while one was open for 4% of the time, Pallas kernels for 33%

profile of v3, /device:TPU:0, one launch (start us, length us, event | category | flops | bytes accessed | tf_op | source)
XLA Modules:
  0.0 328.3 jit_solution(9281856883557412952)
XLA Ops:
  2.6 4.1 %collective-permute-start = (bf16[2,96,384]{2,1,0:T(8,128)(2,1)S(1)}, bf16[2,96,384]{2,1,0:T(8,128)(2,1)S(1)}, u32[]{:S(2)}, u32[]{:S(2)}) collective-permute-start(bf16[2,96,384]{2,1,0:T(8,128)(2,1)S(1)} %get-tuple-element.319), channel_id=1, source_target_pairs={{0,16},{4,20},{8,24},{12,28},{16,0},{20,4},{24,8},{28,12},{1,17},{... | collective-permute-start | bytes 442376 | tf_op jit(solution)/shard_map/ppermute | solution.py:759
  8.0 5.8 %collective-permute-done = bf16[2,96,384]{2,1,0:T(8,128)(2,1)S(1)} collective-permute-done((bf16[2,96,384]{2,1,0:T(8,128)(2,1)S(1)}, bf16[2,96,384]{2,1,0:T(8,128)(2,1)S(1)}, u32[]{:S(2)}, u32[]{:S(2)}) %collective-permute-start) | collective-permute-done | bytes 147488 | tf_op jit(solution)/shard_map/ppermute | solution.py:759
  14.6 7.4 %collective-permute-done.1 = bf16[2,2,96,384]{3,2,1,0:T(8,128)(2,1)S(1)} collective-permute-done((bf16[2,2,96,384]{3,2,1,0:T(8,128)(2,1)S(1)}, bf16[2,2,96,384]{3,2,1,0:T(8,128)(2,1)S(1)}, u32[]{:S(2)}, u32[]{:S(2)}) %collective-permute-start.1) | collective-permute-done | bytes 294944 | tf_op jit(solution)/shard_map/ppermute | solution.py:759
  25.0 3.4 %collective-permute-start.4 = (bf16[2,3,32,512]{3,2,1,0:T(8,128)(2,1)S(1)}, bf16[2,3,32,512]{3,2,1,0:T(8,128)(2,1)S(1)}, u32[]{:S(2)}, u32[]{:S(2)}) collective-permute-start(bf16[2,3,32,512]{3,2,1,0:T(8,128)(2,1)S(1)} %pad_maximum_fusion.28), channel_id=1, source_target_pairs={{0,16},{4,20},{8,24},{12,28},{16,0},{20,4},{24,8},{28,12},{1,17},{... | collective-permute-start | bytes 589832 | tf_op jit(solution)/shard_map/ppermute | solution.py:759
  30.7 6.0 %collective-permute-done.4 = bf16[2,3,32,512]{3,2,1,0:T(8,128)(2,1)S(1)} collective-permute-done((bf16[2,3,32,512]{3,2,1,0:T(8,128)(2,1)S(1)}, bf16[2,3,32,512]{3,2,1,0:T(8,128)(2,1)S(1)}, u32[]{:S(2)}, u32[]{:S(2)}) %collective-permute-start.4) | collective-permute-done | bytes 196640 | tf_op jit(solution)/shard_map/ppermute | solution.py:759
  38.9 8.6 %collective-permute-done.5 = bf16[2,2,3,32,512]{4,3,2,1,0:T(8,128)(2,1)} collective-permute-done((bf16[2,2,3,32,512]{4,3,2,1,0:T(8,128)(2,1)S(1)}, bf16[2,2,3,32,512]{4,3,2,1,0:T(8,128)(2,1)}, u32[]{:S(2)}, u32[]{:S(2)}) %collective-permute-start.5) | collective-permute-done | bytes 393248 | tf_op jit(solution)/shard_map/ppermute | solution.py:759
  47.5 3.2 collective-permute-start.12
  56.5 4.8 %shard_map.178 = (bf16[2,1024,384]{2,1,0:T(8,128)(2,1)S(1)}, bf16[2,1024,192]{2,1,0:T(8,128)(2,1)S(1)}, bf16[2,768,384]{2,1,0:T(8,128)(2,1)S(1)}, bf16[2,768,192...) custom-call(s32[3]{0:T(128)S(1)} %pad_add_fusion.bits, ...), custom_call_target="tpu_custom_call" | custom-call | flops 18119393280 | bytes 62914560 | tf_op jit(solution)/shard_map/pallas_call | solution.py:616
  67.2 3.7 %shard_map.179 = (bf16[2,1024,384]{2,1,0:T(8,128)(2,1)S(1)}, bf16[2,1024,192]{2,1,0:T(8,128)(2,1)S(1)}, bf16[2,768,384]{2,1,0:T(8,128)(2,1)S(1)}, bf16[2,768,192...) custom-call(s32[3]{0:T(128)S(1)} %pad_add_fusion.bits, bf16[1024,768]{1,0:T(8,128)(2,1)S(1)} %bitcast.222, ...), custom_call_target="tpu_custom_call" | custom-call | flops 18119393280 | bytes 62914560 | tf_op jit(solution)/shard_map/pallas_call | solution.py:616
  71.9 3.0 collective-permute-done.13
  74.9 9.8 %collective-permute-done.14 = bf16[2,2,2,3,32,512]{5,4,3,2,1,0:T(8,128)(2,1)S(1)} collective-permute-done((bf16[2,2,2,3,32,512]{5,4,3,2,1,0:T(8,128)(2,1)S(1)}, bf16[2,2,2,3,32,512]{5,4,3,2,1,0:T(8,128)(2,1)S(1)}, u32[]{:S(2)}, u32[]{:S(2)}) %collective-permute-start.14) | collective-permute-done | bytes 786464 | tf_op jit(solution)/shard_map/ppermute | solution.py:764
  90.4 6.5 %shard_map.180 = (bf16[2,1024,192]{2,1,0:T(8,128)(2,1)S(1)}, f32[2,1024,3]{2,1,0:T(8,128)S(1)}) custom-call(s32[3]{0:T(128)S(1)} %pad_add_fusion.bits, s32[2]{0:T(128)S(1)} %dynamic-slice_reduce_fusion.lens, bf16[2,1024,384]{2,1,0:T(8,128)(2,1)S(1)} %get-tuple-element.150.qk, bf16[2,1024,192]{2,1,0:T(8,128)(2,1)S(1)} %get-tuple-element.162.v, ...), custom_call_target="tpu_custom_call" | custom-call | flops 32212254720 | bytes 31457280 | tf_op jit(solution)/shard_map/pallas_call | solution.py:443
  99.6 6.5 %shard_map.181 = (bf16[2,1024,192]{2,1,0:T(8,128)(2,1)S(1)}, f32[2,1024,3]{2,1,0:T(8,128)S(1)}) custom-call(s32[3]{0:T(128)S(1)} %pad_add_fusion.bits, s32[2]{0:T(128)S(1)} %dynamic-slice_reduce_fusion.lens, bf16[2,1024,384]{2,1,0:T(8,128)(2,1)S(1)} %get-tuple-element.156.qk, bf16[2,1024,192]{2,1,0:T(8,128)(2,1)S(1)} %get-tuple-element.167.v, ...), custom_call_target="tpu_custom_call" | custom-call | flops 32212254720 | bytes 31457280 | tf_op jit(solution)/shard_map/pallas_call | solution.py:443
  106.2 4.0 %shard_map.182 = (bf16[1024,768]{1,0:T(8,128)(2,1)S(1)}, f32[1024,768]{1,0:T(8,128)S(1)}, f32[1024,1]{1,0:T(8,128)S(1)}, bf16[768,1024]{1,0:T(8,128)(2,1)S(1)}) custom-call(bf16[1024,768]{1,0:T(8,128)(2,1)S(1)} %bitcast.223, bf16[2,1024,192]{2,1,0:T(8,128)(2,1)S(1)} %get-tuple-element.163.m0.mixed, bf16[2,1024,192]{2,1,0:T(8,128)(2,1)S(1)} %get-tuple-element.170.m1.mixed, ...), custom_call_target="tpu_custom_call" | custom-call | flops 12079595520 | bytes 94371840 | tf_op jit(solution)/shard_map/pallas_call | solution.py:649
  110.3 7.2 %collective-permute-done.21 = bf16[2,2,2,96,512]{4,3,2,1,0:T(8,128)(2,1)S(1)} collective-permute-done((bf16[2,2,2,96,512]{4,3,2,1,0:T(8,128)(2,1)S(1)}, bf16[2,2,2,96,512]{4,3,2,1,0:T(8,128)(2,1)S(1)}, u32[]{:S(2)}, u32[]{:S(2)}) %collective-permute-start.21) | collective-permute-done | bytes 786464 | tf_op jit(solution)/shard_map/ppermute | solution.py:764
  120.5 4.9 %collective-permute-done.24 = bf16[2,2,96,256]{3,2,1,0:T(8,128)(2,1)S(1)} collective-permute-done((bf16[2,2,96,256]{3,2,1,0:T(8,128)(2,1)S(1)}, bf16[2,2,96,256]{3,2,1,0:T(8,128)(2,1)S(1)}, u32[]{:S(2)}, u32[]{:S(2)}) %collective-permute-start.24) | collective-permute-done | bytes 196640 | tf_op jit(solution)/shard_map/ppermute | solution.py:759
  128.8 10.9 %shard_map.183 = (bf16[4,1024,512]{2,1,0:T(8,128)(2,1)}, bf16[4,1024,512]{2,1,0:T(8,128)(2,1)}, f32[1024,768]{1,0:T(8,128)S(1)}) custom-call(s32[3]{0:T(128)S(1)} %pad_add_fusion.bits, bf16[1024,768]{1,0:T(8,128)(2,1)S(1)} %get-tuple-element.178.hid, bf16[2,2,2,2,96,512]{5,4,3,2,1,0:T(8,128)(2,1)S(1)} %pad_maximum_fusion.2.ua0.uap, ...), custom_call_target="tpu_custom_call" | custom-call | flops 64424509440 | bytes 125829120 | tf_op jit(solution)/shard_map/pallas_call | solution.py:162
  143.3 10.7 %shard_map.184 = (bf16[4,1024,256]{2,1,0:T(8,128)(2,1)S(1)}, bf16[4,1024,256]{2,1,0:T(8,128)(2,1)S(1)}, bf16[1024,768]{1,0:T(8,128)(2,1)}, f32[1024,768]{1,0:T(8...) custom-call(s32[3]{0:T(128)S(1)} %pad_add_fusion.bits, ...), custom_call_target="tpu_custom_call" | custom-call | flops 32212254720 | bytes 157286400 | tf_op jit(solution)/shard_map/pallas_call | solution.py:228
  155.2 7.0 %shard_map.185 = (bf16[2,2,2,2,96,768]{5,4,3,2,1,0:T(8,128)(2,1)S(1)}, bf16[2,2,2,2,96,768]{5,4,3,2,1,0:T(8,128)(2,1)S(1)}) custom-call(s32[3]{0:T(128)S(1)} %pad_add_fusion.bits, bf16[768,1024]{1,0:T(8,128)(2,1)S(1)} %get-tuple-element.186.dt, bf16[4,1024,512]{2,1,0:T(8,128)(2,1)S(1)} %copy-done.64, bf16[4,1024,256]{2,1,0:T(8,128)(2,1)S(1)} %get-tuple-element.188.actq), custom_call_target="tpu_custom_call" | custom-call | flops 48318382080 | bytes 110100480 | tf_op jit(solution)/shard_map/pallas_call | solution.py:272
  162.4 10.7 %shard_map.186 = (bf16[2,2,2,2,96,768]{5,4,3,2,1,0:T(8,128)(2,1)S(1)}, f32[1024,768]{1,0:T(8,128)S(1)}) custom-call(s32[3]{0:T(128)S(1)} %pad_add_fusion.bits, bf16[768,1024]{1,0:T(8,128)(2,1)S(1)} %get-tuple-element.185.ht, bf16[1024,768]{1,0:T(8,128)(2,1)S(1)} %copy-done.66, bf16[2,2,2,2,96,512]{5,4,3,2,1,0:T(8,128)(2,1)S(1)} %collective-permute-done.26.ua1.uap, ...), custom_call_target="tpu_custom_call" | custom-call | flops 72477573120 | bytes 235929600 | tf_op jit(solution)/shard_map/pallas_call | solution.py:381
  173.2 3.6 %fusion = bf16[2,2,2,96,768]{4,3,2,1,0:T(8,128)(2,1)} fusion(bf16[2,2,2,2,96,768]{5,4,3,2,1,0:T(8,128)(2,1)} %collective-permute-done.32, bf16[2,2,2,2,96,768]{5,4,3,2,1,0:T(8,128)(2,1)S(1)} %get-tuple-element.219), kind=kLoop, calls=%fused_computation.6 | loop fusion | flops 2359296 | bytes 3538944 | tf_op jit(solution)/shard_map/convert_element_type | solution.py:815
  179.0 15.7 %shard_map.187 = (bf16[2,2,2,2,96,768]{5,4,3,2,1,0:T(8,128)(2,1)S(1)}, f32[1024,768]{1,0:T(8,128)}, bf16[1024,768]{1,0:T(8,128)(2,1)S(1)}, bf16[768,1024]{1,0:T(...) custom-call(s32[3]{0:T(128)S(1)} %pad_add_fusion.bits, bf16[768,1024]{1,0:T(8,128)(2,1)S(1)} %get-tuple-element.185.ht, ...), custom_call_target="tpu_custom_call" | custom-call | flops 72477573120 | bytes 235929600 | tf_op jit(solution)/shard_map/pallas_call | solution.py:381
  201.9 14.5 %shard_map.188 = (bf16[2,1024,384]{2,1,0:T(8,128)(2,1)S(1)}, bf16[2,1024,192]{2,1,0:T(8,128)(2,1)S(1)}, bf16[2,2,2,2,3,32,512]{6,5,4,3,2,1,0:T(8,128)(2,1)S(1)}, bf16[2,2,2,2,3,32,512]{6,5,4,3,2,1,0:T(8,128)(2,1)S(1)}) custom-call(s32[3]{0:T(128)S(1)} %pad_add_fusion.bits, s32[2]{0:T(128)S(1)} %copy-done.15, bf16[2,1024,384]{2,1,0:T(8,128)(2,1)S(1)} %copy-done.37, ...), custom_call_target="tpu_custom_call" | custom-call | flops 80530636800 | bytes 58982400 | tf_op jit(solution)/shard_map/pallas_call | solution.py:576
  221.3 5.0 %shard_map.189 = (bf16[2,2,2,2,96,384]{5,4,3,2,1,0:T(8,128)(2,1)S(1)}, bf16[2,2,2,2,96,384]{5,4,3,2,1,0:T(8,128)(2,1)S(1)}) custom-call(s32[3]{0:T(128)S(1)} %pad_add_fusion.bits, bf16[768,1024]{1,0:T(8,128)(2,1)S(1)} %copy-done.32, bf16[768,1024]{1,0:T(8,128)(2,1)S(1)} %copy-done.48, bf16[2,1024,384]{2,1,0:T(8,128)(2,1)S(1)} %copy-done.51, ...), custom_call_target="tpu_custom_call" | custom-call | flops 24159191040 | bytes 62914560 | tf_op jit(solution)/shard_map/pallas_call | solution.py:715
  235.6 15.0 %shard_map.190 = (bf16[2,1024,384]{2,1,0:T(8,128)(2,1)S(1)}, bf16[2,1024,192]{2,1,0:T(8,128)(2,1)S(1)}, bf16[2,2,2,3,32,512]{5,4,3,2,1,0:T(8,128)(2,1)S(1)}, bf1...) custom-call(s32[3]{0:T(128)S(1)} %pad_add_fusion.bits, ...), custom_call_target="tpu_custom_call" | custom-call | flops 80530636800 | bytes 58982400 | tf_op jit(solution)/shard_map/pallas_call | solution.py:576
  260.5 4.9 %shard_map.191 = (bf16[2,2,2,96,384]{4,3,2,1,0:T(8,128)(2,1)S(1)}, bf16[2,2,2,96,384]{4,3,2,1,0:T(8,128)(2,1)S(1)}, bf16[2,2,2,96,384]{4,3,2,1,0:T(8,128)(2,1)S(1)}, bf16[2,2,2,96,384]{4,3,2,1,0:T(8,128)(2,1)S(1)}) custom-call(s32[3]{0:T(128)S(1)} %pad_add_fusion.bits, bf16[768,1024]{1,0:T(8,128)(2,1)S(1)} %copy-done.33, bf16[768,1024]{1,0:T(8,128)(2,1)S(1)} %copy-done.49, ...), custom_call_target="tpu_custom_call" | custom-call | flops 24159191040 | bytes 62914560 | tf_op jit(solution)/shard_map/pallas_call | solution.py:715
  267.5 3.9 %collective-permute-done.47 = bf16[2,2,96,768]{3,2,1,0:T(8,128)(2,1)S(1)} collective-permute-done((bf16[2,2,96,768]{3,2,1,0:T(8,128)(2,1)S(1)}, bf16[2,2,96,768]{3,2,1,0:T(8,128)(2,1)S(1)}, u32[]{:S(2)}, u32[]{:S(2)}) %collective-permute-start.47) | collective-permute-done | bytes 589856 | tf_op jit(solution)/shard_map/ppermute | solution.py:759
  272.7 6.7 %collective-permute-done.49 = bf16[2,2,2,3,32,512]{5,4,3,2,1,0:T(8,128)(2,1)S(1)} collective-permute-done((bf16[2,2,2,3,32,512]{5,4,3,2,1,0:T(8,128)(2,1)S(1)}, bf16[2,2,2,3,32,512]{5,4,3,2,1,0:T(8,128)(2,1)S(1)}, u32[]{:S(2)}, u32[]{:S(2)}) %collective-permute-start.49) | collective-permute-done | bytes 786464 | tf_op jit(solution)/shard_map/ppermute | solution.py:759
  284.0 7.1 %shard_map.192 = f32[1024,768]{1,0:T(8,128)} custom-call(f32[1024,768]{1,0:T(8,128)S(1)} %copy-done.53, bf16[2,1024,384]{2,1,0:T(8,128)(2,1)S(1)} %get-tuple-element.258.dqk.dqk0, bf16[2,1024,384]{2,1,0:T(8,128)(2,1)S(1)} %copy-done.52, bf16[2,1024,192]{2,1,0:T(8,128)(2,1)S(1)} %copy-done.61, bf16[2,1024,192]{2,1,0:T(8,128)(2,1)S(1)} %copy-done.63, ...), custom_call_target="tpu_custom_call" | custom-call | flops 36238786560 | bytes 110100480 | tf_op jit(solution)/shard_map/pallas_call | solution.py:741
  292.0 5.2 %collective-permute-done.52 = bf16[2,2,3,32,512]{4,3,2,1,0:T(8,128)(2,1)S(1)} collective-permute-done((bf16[2,2,3,32,512]{4,3,2,1,0:T(8,128)(2,1)S(1)}, bf16[2,2,3,32,512]{4,3,2,1,0:T(8,128)(2,1)S(1)}, u32[]{:S(2)}, u32[]{:S(2)}) %collective-permute-start.52) | collective-permute-done | bytes 393248 | tf_op jit(solution)/shard_map/ppermute | solution.py:759
  306.8 6.7 %collective-permute-done.59 = bf16[2,2,3,32,512]{4,3,2,1,0:T(8,128)(2,1)S(1)} collective-permute-done((bf16[2,2,3,32,512]{4,3,2,1,0:T(8,128)(2,1)S(1)}, bf16[2,2,3,32,512]{4,3,2,1,0:T(8,128)(2,1)S(1)}, u32[]{:S(2)}, u32[]{:S(2)}) %collective-permute-start.59) | collective-permute-done | bytes 393248 | tf_op jit(solution)/shard_map/ppermute | solution.py:759
  314.8 3.2 collective-permute-done.57
  (351 shorter events, 105.9 us)
Async XLA Ops:
  2.6 11.1 %collective-permute-start = (bf16[2,96,384]{2,1,0:T(8,128)(2,1)S(1)}, bf16[2,96,384]{2,1,0:T(8,128)(2,1)S(1)}, u32[]{:S(2)}, u32[]{:S(2)}) collective-permute-start(bf16[2,96,384]{2,1,0:T(8,128)(2,1)S(1)} %get-tuple-element.319), channel_id=1, source_target_pairs={{0,16},{4,20},{8,24},{12,28},{16,0},{20,4},{24,8},{28,12},{1,17},{... | collective-permute-start | bytes 442376 | tf_op jit(solution)/shard_map/ppermute | solution.py:759
  25.0 11.6 %collective-permute-start.4 = (bf16[2,3,32,512]{3,2,1,0:T(8,128)(2,1)S(1)}, bf16[2,3,32,512]{3,2,1,0:T(8,128)(2,1)S(1)}, u32[]{:S(2)}, u32[]{:S(2)}) collective-permute-start(bf16[2,3,32,512]{3,2,1,0:T(8,128)(2,1)S(1)} %pad_maximum_fusion.28), channel_id=1, source_target_pairs={{0,16},{4,20},{8,24},{12,28},{16,0},{20,4},{24,8},{28,12},{1,17},{... | collective-permute-start | bytes 589832 | tf_op jit(solution)/shard_map/ppermute | solution.py:759
  36.7 15.2 %collective-permute-start.6 = (bf16[2,2,2,96,384]{4,3,2,1,0:T(8,128)(2,1)S(1)}, bf16[2,2,2,96,384]{4,3,2,1,0:T(8,128)(2,1)S(1)}, u32[]{:S(2)}, u32[]{:S(2)}) collective-permute-start(bf16[2,2,2,96,384]{4,3,2,1,0:T(8,128)(2,1)S(1)} %pad_maximum_fusion.12), channel_id=1, source_target_pairs={{0,2},{1,3},{2,0},{3,1},{4,6},{5,7},{6,4},{7,5},{8,10},{9,11},{10,... | collective-permute-start | bytes 1769480 | tf_op jit(solution)/shard_map/ppermute | solution.py:764
  37.3 14.6 %collective-permute-start.7 = (bf16[2,2,2,96,384]{4,3,2,1,0:T(8,128)(2,1)S(1)}, bf16[2,2,2,96,384]{4,3,2,1,0:T(8,128)(2,1)S(1)}, u32[]{:S(2)}, u32[]{:S(2)}) collective-permute-start(bf16[2,2,2,96,384]{4,3,2,1,0:T(8,128)(2,1)S(1)} %pad_maximum_fusion.13), channel_id=1, source_target_pairs={{0,4},{4,0},{8,12},{12,8},{16,20},{20,16},{24,28},{28,24},{1,5},{5... | collective-permute-start | bytes 1769480 | tf_op jit(solution)/shard_map/ppermute | solution.py:759
  47.5 16.8 %collective-permute-start.12 = (bf16[2,96,512]{2,1,0:T(8,128)(2,1)S(1)}, bf16[2,96,512]{2,1,0:T(8,128)(2,1)S(1)}, u32[]{:S(2)}, u32[]{:S(2)}) collective-permute-start(bf16[2,96,512]{2,1,0:T(8,128)(2,1)S(1)} %pad_maximum_fusion.29), channel_id=1, source_target_pairs={{0,16},{4,20},{8,24},{12,28},{16,0},{20,4},{24,8},{28,12},{1,17},{... | collective-permute-start | bytes 589832 | tf_op jit(solution)/shard_map/ppermute | solution.py:759
  51.8 11.3 %collective-permute-start.8 = (bf16[2,2,3,32,512]{4,3,2,1,0:T(8,128)(2,1)S(1)}, bf16[2,2,3,32,512]{4,3,2,1,0:T(8,128)(2,1)S(1)}, u32[]{:S(2)}, u32[]{:S(2)}) collective-permute-start(bf16[2,2,3,32,512]{4,3,2,1,0:T(8,128)(2,1)S(1)} %get-tuple-element.147), channel_id=1, source_target_pairs={{0,4},{4,0},{8,12},{12,8},{16,20},{20,16},{24,28},{28,24},{1,5},{5... | collective-permute-start | bytes 1179656 | tf_op jit(solution)/shard_map/ppermute | solution.py:759
  66.2 18.6 %collective-permute-start.14 = (bf16[2,2,2,3,32,512]{5,4,3,2,1,0:T(8,128)(2,1)S(1)}, bf16[2,2,2,3,32,512]{5,4,3,2,1,0:T(8,128)(2,1)S(1)}, u32[]{:S(2)}, u32[]{:S(2)}) collective-permute-start(bf16[2,2,2,3,32,512]{5,4,3,2,1,0:T(8,128)(2,1)S(1)} %pad_maximum_fusion.6), channel_id=1, source_target_pairs={{0,2},{1,3},{2,0},{3,1},{4,6},{5,7},{6,4},{7,5},{8,10},{9,11},{10,... | collective-permute-start | bytes 2359304 | tf_op jit(solution)/shard_map/ppermute | solution.py:764
  66.7 18.3 %collective-permute-start.15 = (bf16[2,2,2,3,32,512]{5,4,3,2,1,0:T(8,128)(2,1)S(1)}, bf16[2,2,2,3,32,512]{5,4,3,2,1,0:T(8,128)(2,1)S(1)}, u32[]{:S(2)}, u32[]{:S(2)}) collective-permute-start(bf16[2,2,2,3,32,512]{5,4,3,2,1,0:T(8,128)(2,1)S(1)} %pad_maximum_fusion.7), channel_id=1, source_target_pairs={{0,4},{4,0},{8,12},{12,8},{16,20},{20,16},{24,28},{28,24},{1,5},{5... | collective-permute-start | bytes 2359304 | tf_op jit(solution)/shard_map/ppermute | solution.py:759
  85.2 11.8 %collective-permute-start.18 = (bf16[2,96,256]{2,1,0:T(8,128)(2,1)S(1)}, bf16[2,96,256]{2,1,0:T(8,128)(2,1)S(1)}, u32[]{:S(2)}, u32[]{:S(2)}) collective-permute-start(bf16[2,96,256]{2,1,0:T(8,128)(2,1)S(1)} %pad_maximum_fusion.34), channel_id=1, source_target_pairs={{0,16},{4,20},{8,24},{12,28},{16,0},{20,4},{24,8},{28,12},{1,17},{... | collective-permute-start | bytes 294920 | tf_op jit(solution)/shard_map/ppermute | solution.py:759
  97.9 12.3 %collective-permute-start.23 = (bf16[2,2,96,256]{3,2,1,0:T(8,128)(2,1)S(1)}, bf16[2,2,96,256]{3,2,1,0:T(8,128)(2,1)S(1)}, u32[]{:S(2)}, u32[]{:S(2)}) collective-permute-start(bf16[2,2,96,256]{3,2,1,0:T(8,128)(2,1)S(1)} %pad_maximum_fusion.30), channel_id=1, source_target_pairs={{0,8},{4,12},{8,0},{12,4},{16,24},{20,28},{24,16},{28,20},{1,9},{5... | collective-permute-start | bytes 589832 | tf_op jit(solution)/shard_map/ppermute | solution.py:759
  98.4 19.2 %collective-permute-start.21 = (bf16[2,2,2,96,512]{4,3,2,1,0:T(8,128)(2,1)S(1)}, bf16[2,2,2,96,512]{4,3,2,1,0:T(8,128)(2,1)S(1)}, u32[]{:S(2)}, u32[]{:S(2)}) collective-permute-start(bf16[2,2,2,96,512]{4,3,2,1,0:T(8,128)(2,1)S(1)} %pad_maximum_fusion.8), channel_id=1, source_target_pairs={{0,2},{1,3},{2,0},{3,1},{4,6},{5,7},{6,4},{7,5},{8,10},{9,11},{10,... | collective-permute-start | bytes 2359304 | tf_op jit(solution)/shard_map/ppermute | solution.py:764
  99.1 18.7 %collective-permute-start.22 = (bf16[2,2,2,96,512]{4,3,2,1,0:T(8,128)(2,1)S(1)}, bf16[2,2,2,96,512]{4,3,2,1,0:T(8,128)(2,1)S(1)}, u32[]{:S(2)}, u32[]{:S(2)}) collective-permute-start(bf16[2,2,2,96,512]{4,3,2,1,0:T(8,128)(2,1)S(1)} %pad_maximum_fusion.9), channel_id=1, source_target_pairs={{0,4},{4,0},{8,12},{12,8},{16,20},{20,16},{24,28},{28,24},{1,5},{5... | collective-permute-start | bytes 2359304 | tf_op jit(solution)/shard_map/ppermute | solution.py:759
  125.7 14.0 %collective-permute-start.28 = (bf16[2,2,2,96,256]{4,3,2,1,0:T(8,128)(2,1)S(1)}, bf16[2,2,2,96,256]{4,3,2,1,0:T(8,128)(2,1)S(1)}, u32[]{:S(2)}, u32[]{:S(2)}) collective-permute-start(bf16[2,2,2,96,256]{4,3,2,1,0:T(8,128)(2,1)S(1)} %pad_maximum_fusion.19), channel_id=1, source_target_pairs={{0,2},{1,3},{2,0},{3,1},{4,6},{5,7},{6,4},{7,5},{8,10},{9,11},{10,... | collective-permute-start | bytes 1179656 | tf_op jit(solution)/shard_map/ppermute | solution.py:764
  127.3 12.5 %collective-permute-start.29 = (bf16[2,2,2,96,256]{4,3,2,1,0:T(8,128)(2,1)S(1)}, bf16[2,2,2,96,256]{4,3,2,1,0:T(8,128)(2,1)S(1)}, u32[]{:S(2)}, u32[]{:S(2)}) collective-permute-start(bf16[2,2,2,96,256]{4,3,2,1,0:T(8,128)(2,1)S(1)} %pad_maximum_fusion.20), channel_id=1, source_target_pairs={{0,4},{4,0},{8,12},{12,8},{16,20},{20,16},{24,28},{28,24},{1,5},{5... | collective-permute-start | bytes 1179656 | tf_op jit(solution)/shard_map/ppermute | solution.py:759
  176.8 40.7 %collective-permute-start.35 = (bf16[2,2,2,96,768]{4,3,2,1,0:T(8,128)(2,1)}, bf16[2,2,2,96,768]{4,3,2,1,0:T(8,128)(2,1)}, u32[]{:S(2)}, u32[]{:S(2)}) collective-permute-start(bf16[2,2,2,96,768]{4,3,2,1,0:T(8,128)(2,1)} %fusion), channel_id=1, source_target_pairs={{0,4},{4,0},{8,12},{12,8},{16,20},{20,16},{24,28},{28,24},{1,5},{5... | collective-permute-start | bytes 3538952 | tf_op jit(solution)/shard_map/ppermute | solution.py:759
  177.4 18.6 %collective-permute-start.33 = (bf16[2,2,2,2,96,768]{5,4,3,2,1,0:T(8,128)(2,1)S(1)}, bf16[2,2,2,2,96,768]{5,4,3,2,1,0:T(8,128)(2,1)S(1)}, u32[]{:S(2)}, u32[]{:S(2)}) collective-permute-start(bf16[2,2,2,2,96,768]{5,4,3,2,1,0:T(8,128)(2,1)S(1)} %get-tuple-element.203), channel_id=1, source_target_pairs={{0,1},{1,0},{2,3},{3,2},{4,5},{5,4},{6,7},{7,6},{8,9},{9,8},{10,11... | collective-permute-start | bytes 7077896 | tf_op jit(solution)/shard_map/ppermute | solution.py:764
  196.0 21.6 %collective-permute-start.34 = (f32[4,768]{1,0:T(4,128)S(1)}, f32[4,768]{1,0:T(4,128)S(1)}, u32[]{:S(2)}, u32[]{:S(2)}) collective-permute-start(f32[4,768]{1,0:T(4,128)S(1)} %pad_maximum_fusion.35), channel_id=1, source_target_pairs={{0,1},{1,0},{2,3},{3,2},{4,5},{5,4},{6,7},{7,6},{8,9},{9,8},{10,11... | collective-permute-start | bytes 36872 | tf_op jit(solution)/shard_map/ppermute | solution.py:847
  197.0 29.3 %collective-permute-start.39 = (bf16[2,2,2,96,768]{4,3,2,1,0:T(8,128)(2,1)S(1)}, bf16[2,2,2,96,768]{4,3,2,1,0:T(8,128)(2,1)}, u32[]{:S(2)}, u32[]{:S(2)}) collective-permute-start(bf16[2,2,2,96,768]{4,3,2,1,0:T(8,128)(2,1)S(1)} %fusion.1), channel_id=1, source_target_pairs={{0,2},{1,3},{2,0},{3,1},{4,6},{5,7},{6,4},{7,5},{8,10},{9,11},{10,... | collective-permute-start | bytes 3538952 | tf_op jit(solution)/shard_map/ppermute | solution.py:764
  231.8 18.8 %collective-permute-start.42 = (bf16[2,2,2,2,96,384]{5,4,3,2,1,0:T(8,128)(2,1)S(1)}, bf16[2,2,2,2,96,384]{5,4,3,2,1,0:T(8,128)(2,1)S(1)}, u32[]{:S(2)}, u32[]{:S(2)}) collective-permute-start(bf16[2,2,2,2,96,384]{5,4,3,2,1,0:T(8,128)(2,1)S(1)} %get-tuple-element.241), channel_id=1, source_target_pairs={{0,1},{1,0},{2,3},{3,2},{4,5},{5,4},{6,7},{7,6},{8,9},{9,8},{10,11... | collective-permute-start | bytes 3538952 | tf_op jit(solution)/shard_map/ppermute | solution.py:764
  231.8 18.8 %collective-permute-start.43 = (bf16[2,2,2,2,96,384]{5,4,3,2,1,0:T(8,128)(2,1)S(1)}, bf16[2,2,2,2,96,384]{5,4,3,2,1,0:T(8,128)(2,1)S(1)}, u32[]{:S(2)}, u32[]{:S(2)}) collective-permute-start(bf16[2,2,2,2,96,384]{5,4,3,2,1,0:T(8,128)(2,1)S(1)} %get-tuple-element.242), channel_id=1, source_target_pairs={{0,1},{1,0},{2,3},{3,2},{4,5},{5,4},{6,7},{7,6},{8,9},{9,8},{10,11... | collective-permute-start | bytes 3538952 | tf_op jit(solution)/shard_map/ppermute | solution.py:764
  232.5 18.0 %collective-permute-start.41 = (f32[4,768]{1,0:T(4,128)S(1)}, f32[4,768]{1,0:T(4,128)S(1)}, u32[]{:S(2)}, u32[]{:S(2)}) collective-permute-start(f32[4,768]{1,0:T(4,128)S(1)} %add.275), channel_id=1, source_target_pairs={{0,16},{4,20},{8,24},{12,28},{16,0},{20,4},{24,8},{28,12},{1,17},{... | collective-permute-start | bytes 36872 | tf_op jit(solution)/shard_map/ppermute | solution.py:847
  233.8 16.8 %collective-permute-start.44 = (bf16[2,2,96,768]{3,2,1,0:T(8,128)(2,1)}, bf16[2,2,96,768]{3,2,1,0:T(8,128)(2,1)}, u32[]{:S(2)}, u32[]{:S(2)}) collective-permute-start(bf16[2,2,96,768]{3,2,1,0:T(8,128)(2,1)} %fusion.4), channel_id=1, source_target_pairs={{0,2},{1,3},{2,0},{3,1},{4,6},{5,7},{6,4},{7,5},{8,10},{9,11},{10,... | collective-permute-start | bytes 1769480 | tf_op jit(solution)/shard_map/ppermute | solution.py:764
  235.0 15.6 %collective-permute-start.45 = (bf16[2,2,96,768]{3,2,1,0:T(8,128)(2,1)}, bf16[2,2,96,768]{3,2,1,0:T(8,128)(2,1)S(1)}, u32[]{:S(2)}, u32[]{:S(2)}) collective-permute-start(bf16[2,2,96,768]{3,2,1,0:T(8,128)(2,1)} %fusion.3), channel_id=1, source_target_pairs={{0,4},{4,0},{8,12},{12,8},{16,20},{20,16},{24,28},{28,24},{1,5},{5... | collective-permute-start | bytes 1769480 | tf_op jit(solution)/shard_map/ppermute | solution.py:759
  252.2 20.5 %collective-permute-start.48 = (bf16[2,2,2,3,32,512]{5,4,3,2,1,0:T(8,128)(2,1)S(1)}, bf16[2,2,2,3,32,512]{5,4,3,2,1,0:T(8,128)(2,1)S(1)}, u32[]{:S(2)}, u32[]{:S(2)}) collective-permute-start(bf16[2,2,2,3,32,512]{5,4,3,2,1,0:T(8,128)(2,1)S(1)} %get-tuple-element.252), channel_id=1, source_target_pairs={{0,2},{1,3},{2,0},{3,1},{4,6},{5,7},{6,4},{7,5},{8,10},{9,11},{10,... | collective-permute-start | bytes 2359304 | tf_op jit(solution)/shard_map/ppermute | solution.py:764
  258.0 13.4 %collective-permute-start.47 = (bf16[2,2,96,768]{3,2,1,0:T(8,128)(2,1)S(1)}, bf16[2,2,96,768]{3,2,1,0:T(8,128)(2,1)S(1)}, u32[]{:S(2)}, u32[]{:S(2)}) collective-permute-start(bf16[2,2,96,768]{3,2,1,0:T(8,128)(2,1)S(1)} %pad_maximum_fusion.14), channel_id=1, source_target_pairs={{0,8},{4,12},{8,0},{12,4},{16,24},{20,28},{24,16},{28,20},{1,9},{5... | collective-permute-start | bytes 1769480 | tf_op jit(solution)/shard_map/ppermute | solution.py:759
  258.9 20.5 %collective-permute-start.49 = (bf16[2,2,2,3,32,512]{5,4,3,2,1,0:T(8,128)(2,1)S(1)}, bf16[2,2,2,3,32,512]{5,4,3,2,1,0:T(8,128)(2,1)S(1)}, u32[]{:S(2)}, u32[]{:S(2)}) collective-permute-start(bf16[2,2,2,3,32,512]{5,4,3,2,1,0:T(8,128)(2,1)S(1)} %get-tuple-element.253), channel_id=1, source_target_pairs={{0,4},{4,0},{8,12},{12,8},{16,20},{20,16},{24,28},{28,24},{1,5},{5... | collective-permute-start | bytes 2359304 | tf_op jit(solution)/shard_map/ppermute | solution.py:759
  265.4 25.6 %collective-permute-start.50 = (bf16[2,2,2,96,384]{4,3,2,1,0:T(8,128)(2,1)S(1)}, bf16[2,2,2,96,384]{4,3,2,1,0:T(8,128)(2,1)S(1)}, u32[]{:S(2)}, u32[]{:S(2)}) collective-permute-start(bf16[2,2,2,96,384]{4,3,2,1,0:T(8,128)(2,1)S(1)} %get-tuple-element.264), channel_id=1, source_target_pairs={{0,2},{1,3},{2,0},{3,1},{4,6},{5,7},{6,4},{7,5},{8,10},{9,11},{10,... | collective-permute-start | bytes 1769480 | tf_op jit(solution)/shard_map/ppermute | solution.py:764
  266.3 25.7 %collective-permute-start.51 = (bf16[2,2,2,96,384]{4,3,2,1,0:T(8,128)(2,1)S(1)}, bf16[2,2,2,96,384]{4,3,2,1,0:T(8,128)(2,1)S(1)}, u32[]{:S(2)}, u32[]{:S(2)}) collective-permute-start(bf16[2,2,2,96,384]{4,3,2,1,0:T(8,128)(2,1)S(1)} %get-tuple-element.265), channel_id=1, source_target_pairs={{0,4},{4,0},{8,12},{12,8},{16,20},{20,16},{24,28},{28,24},{1,5},{5... | collective-permute-start | bytes 1769480 | tf_op jit(solution)/shard_map/ppermute | solution.py:759
  279.5 12.5 %collective-permute-start.54 = (bf16[2,96,768]{2,1,0:T(8,128)(2,1)S(1)}, bf16[2,96,768]{2,1,0:T(8,128)(2,1)S(1)}, u32[]{:S(2)}, u32[]{:S(2)}) collective-permute-start(bf16[2,96,768]{2,1,0:T(8,128)(2,1)S(1)} %pad_maximum_fusion.24), channel_id=1, source_target_pairs={{0,16},{4,20},{8,24},{12,28},{16,0},{20,4},{24,8},{28,12},{1,17},{... | collective-permute-start | bytes 884744 | tf_op jit(solution)/shard_map/ppermute | solution.py:759
  283.3 13.9 %collective-permute-start.52 = (bf16[2,2,3,32,512]{4,3,2,1,0:T(8,128)(2,1)S(1)}, bf16[2,2,3,32,512]{4,3,2,1,0:T(8,128)(2,1)S(1)}, u32[]{:S(2)}, u32[]{:S(2)}) collective-permute-start(bf16[2,2,3,32,512]{4,3,2,1,0:T(8,128)(2,1)S(1)} %fusion.6), channel_id=1, source_target_pairs={{0,4},{4,0},{8,12},{12,8},{16,20},{20,16},{24,28},{28,24},{1,5},{5... | collective-permute-start | bytes 1179656 | tf_op jit(solution)/shard_map/ppermute | solution.py:759
  301.0 12.5 %collective-permute-start.59 = (bf16[2,2,3,32,512]{4,3,2,1,0:T(8,128)(2,1)S(1)}, bf16[2,2,3,32,512]{4,3,2,1,0:T(8,128)(2,1)S(1)}, u32[]{:S(2)}, u32[]{:S(2)}) collective-permute-start(bf16[2,2,3,32,512]{4,3,2,1,0:T(8,128)(2,1)S(1)} %pad_maximum_fusion.21), channel_id=1, source_target_pairs={{0,8},{4,12},{8,0},{12,4},{16,24},{20,28},{24,16},{28,20},{1,9},{5... | collective-permute-start | bytes 1179656 | tf_op jit(solution)/shard_map/ppermute | solution.py:759
  305.5 12.5 %collective-permute-start.57 = (bf16[2,2,96,384]{3,2,1,0:T(8,128)(2,1)S(1)}, bf16[2,2,96,384]{3,2,1,0:T(8,128)(2,1)S(1)}, u32[]{:S(2)}, u32[]{:S(2)}) collective-permute-start(bf16[2,2,96,384]{3,2,1,0:T(8,128)(2,1)S(1)} %pad_maximum_fusion.25), channel_id=1, source_target_pairs={{0,8},{4,12},{8,0},{12,4},{16,24},{20,28},{24,16},{28,20},{1,9},{5... | collective-permute-start | bytes 884744 | tf_op jit(solution)/shard_map/ppermute | solution.py:759
  (111 other events, 1233.3 us)

commit v4 on v3

--- a/solution.py
+++ b/solution.py
@@ -455,7 +455,7 @@
                 pl.BlockSpec((1, length, heads), lambda k, s, *_: (k, s, 0)),
             ],
         ),
-        compiler_params=params(30, 2),
+        compiler_params=params(22, 2),
         cost_estimate=cost(16 * 2 * rows * length * w1, 16 * rows * w1),
     )(bits, lens, qk, v, ga, gb)
 
@@ -583,7 +583,7 @@
                 pltpu.VMEM((w1, length), BF16), pltpu.VMEM((heads, length, keys), F32),
             ],
         ),
-        compiler_params=params(36, 2),
+        compiler_params=params(30, 2),
         cost_estimate=cost(40 * 2 * rows * length * w1, 30 * rows * w1),
     )(bits, lens, qk, v, ga, gb, lse, dattn, wo, *got)
 
@@ -615,9 +615,9 @@
     head = lambda s: pl.BlockSpec((1,) + s, lambda k, *_: (k, 0, 0))
     return pl.pallas_call(
         functools.partial(qkv_kernel, first),
-        out_shape=[sds((2, rows, w2), BF16), sds((2, rows, w1), BF16), sds((2, width, w2), BF16),
-                   sds((2, width, w1), BF16), sds((2, width, w1), BF16)]
-        + ([sds((width, rows), BF16)] if first else []),
+        out_shape=[sds((2, rows, w2), BF16), sds((2, rows, w1), BF16), pltpu.HBM((2, width, w2), BF16),
+                   pltpu.HBM((2, width, w1), BF16), sds((2, width, w1), BF16)]
+        + ([pltpu.HBM((width, rows), BF16)] if first else []),
         grid_spec=pltpu.PrefetchScalarGridSpec(
             num_scalar_prefetch=1, grid=(2,),
             in_specs=[whole((rows, width)), spec_a((p, w2), pick), spec_b((p, w2), pick)],
@@ -649,7 +649,7 @@
     return pl.pallas_call(
         out_kernel,
         grid=(rows // block,),
-        out_shape=(sds((rows, width), BF16), sds((rows, width), F32), sds((rows, 1), F32), sds((width, rows), BF16)),
+        out_shape=(sds((rows, width), BF16), pltpu.HBM((rows, width), F32), sds((rows, 1), F32), pltpu.HBM((width, rows), BF16)),
         in_specs=[row(width), mix, mix, whole((2, width, w1)), whole((2, width, w1)), whole((1, width)), whole((1, width))],
         out_specs=[row(width), row(width), row(1), pl.BlockSpec((width, block), lambda r: (0, r))],
         compiler_params=params(20),

time: 331 us -> 327 us (0.988)
  local copies, waits for them, and re-layouts: 20 us -> 9.8 us
    unnamed x166 -> x148, local copies, waits for them, and re-layouts: 18 us -> 7.77 us
    ppermute x28, waiting for transfers between devices: 24.8 us -> 30 us  [partner_head(): return lax.ppermute(value, 'head', [(i, i ^ 1 << bit) for i in range(size)])]
  transfers between devices with their start and end apart: 61 -> 61, of which waited for: 28 -> 30; matrix products, arithmetic and copies ran while one was open for 4% -> 5% of each run, Pallas kernels for 33% -> 34%
where the time goes in v4:
time: 327 us; the launch traced here: 325 us
  Pallas kernels  130 us (40%)
  waiting for transfers between devices  98.4 us (30%)
  starting transfers between devices  63.8 us (20%)
  other arithmetic  21 us (6%)
  local copies, waits for them, and re-layouts  9.8 us (3%)
    ppermute x28, waiting for transfers between devices, partner_dp(): return lax.ppermute(value, 'dp', [(i, i ^ step) for i in range(size)])  66.7 us
    ppermute x28, starting transfers between devices, partner_dp(): return lax.ppermute(value, 'dp', [(i, i ^ step) for i in range(size)])  37.9 us
    ppermute x28, waiting for transfers between devices, partner_head(): return lax.ppermute(value, 'head', [(i, i ^ 1 << bit) for i in range(size)])  30 us
    pallas_call x2, Pallas kernels, attention_backward(): pl.pallas_call(functools.partial(att_bwd_kernel, last), out_shape=out_sha...  29.3 us
    pallas_call x2, Pallas kernels, ffn_backward(): pl.pallas_call(functools.partial(ffn_bwd_kernel, chunk, last), out_shape=...  26.3 us
    ppermute x28, starting transfers between devices, partner_head(): return lax.ppermute(value, 'head', [(i, i ^ 1 << bit) for i in range(size)])  20.1 us
    pallas_call x2, Pallas kernels, attention_forward(): pl.pallas_call(att_fwd_kernel, out_shape=(sds((2, rows, w1), BF16), sds((...  13.2 us
    pallas_call x1, Pallas kernels, ffn_part(): pl.pallas_call(functools.partial(ffn_part_kernel, chunk), out_shape=(pltp...  10.9 us
  transfers between devices with their start and end apart: 61, of which 30 were waited for; matrix products, arithmetic and copies ran while one was open for 5% of the time, Pallas kernels for 34%

profile of v4, /device:TPU:0, one launch (start us, length us, event | category | flops | bytes accessed | tf_op | source)
XLA Modules:
  0.0 325.0 jit_solution(14944915004669151576)
XLA Ops:
  2.6 4.1 %collective-permute-start = (bf16[2,96,384]{2,1,0:T(8,128)(2,1)S(1)}, bf16[2,96,384]{2,1,0:T(8,128)(2,1)S(1)}, u32[]{:S(2)}, u32[]{:S(2)}) collective-permute-start(bf16[2,96,384]{2,1,0:T(8,128)(2,1)S(1)} %get-tuple-element.319), channel_id=1, source_target_pairs={{0,16},{4,20},{8,24},{12,28},{16,0},{20,4},{24,8},{28,12},{1,17},{... | collective-permute-start | bytes 442376 | tf_op jit(solution)/shard_map/ppermute | solution.py:759
  8.0 5.8 %collective-permute-done = bf16[2,96,384]{2,1,0:T(8,128)(2,1)S(1)} collective-permute-done((bf16[2,96,384]{2,1,0:T(8,128)(2,1)S(1)}, bf16[2,96,384]{2,1,0:T(8,128)(2,1)S(1)}, u32[]{:S(2)}, u32[]{:S(2)}) %collective-permute-start) | collective-permute-done | bytes 147488 | tf_op jit(solution)/shard_map/ppermute | solution.py:759
  14.6 7.4 %collective-permute-done.1 = bf16[2,2,96,384]{3,2,1,0:T(8,128)(2,1)S(1)} collective-permute-done((bf16[2,2,96,384]{3,2,1,0:T(8,128)(2,1)S(1)}, bf16[2,2,96,384]{3,2,1,0:T(8,128)(2,1)S(1)}, u32[]{:S(2)}, u32[]{:S(2)}) %collective-permute-start.1) | collective-permute-done | bytes 294944 | tf_op jit(solution)/shard_map/ppermute | solution.py:759
  25.0 3.4 %collective-permute-start.4 = (bf16[2,3,32,512]{3,2,1,0:T(8,128)(2,1)S(1)}, bf16[2,3,32,512]{3,2,1,0:T(8,128)(2,1)S(1)}, u32[]{:S(2)}, u32[]{:S(2)}) collective-permute-start(bf16[2,3,32,512]{3,2,1,0:T(8,128)(2,1)S(1)} %pad_maximum_fusion.28), channel_id=1, source_target_pairs={{0,16},{4,20},{8,24},{12,28},{16,0},{20,4},{24,8},{28,12},{1,17},{... | collective-permute-start | bytes 589832 | tf_op jit(solution)/shard_map/ppermute | solution.py:759
  30.7 6.0 %collective-permute-done.4 = bf16[2,3,32,512]{3,2,1,0:T(8,128)(2,1)S(1)} collective-permute-done((bf16[2,3,32,512]{3,2,1,0:T(8,128)(2,1)S(1)}, bf16[2,3,32,512]{3,2,1,0:T(8,128)(2,1)S(1)}, u32[]{:S(2)}, u32[]{:S(2)}) %collective-permute-start.4) | collective-permute-done | bytes 196640 | tf_op jit(solution)/shard_map/ppermute | solution.py:759
  38.9 8.6 %collective-permute-done.5 = bf16[2,2,3,32,512]{4,3,2,1,0:T(8,128)(2,1)} collective-permute-done((bf16[2,2,3,32,512]{4,3,2,1,0:T(8,128)(2,1)S(1)}, bf16[2,2,3,32,512]{4,3,2,1,0:T(8,128)(2,1)}, u32[]{:S(2)}, u32[]{:S(2)}) %collective-permute-start.5) | collective-permute-done | bytes 393248 | tf_op jit(solution)/shard_map/ppermute | solution.py:759
  47.5 3.2 collective-permute-start.12
  56.5 5.7 %shard_map.178 = (bf16[2,1024,384]{2,1,0:T(8,128)(2,1)S(1)}, bf16[2,1024,192]{2,1,0:T(8,128)(2,1)S(1)}, bf16[2,768,384]{2,1,0:T(8,128)(2,1)}, bf16[2,768,192]{2,...) custom-call(s32[3]{0:T(128)S(1)} %pad_add_fusion.bits, bf16[1024,768]{1,0:T(8,128)(2,1)S(1)} %bitcast.221, ...), custom_call_target="tpu_custom_call" | custom-call | flops 18119393280 | bytes 62914560 | tf_op jit(solution)/shard_map/pallas_call | solution.py:616
  66.4 4.6 %shard_map.179 = (bf16[2,1024,384]{2,1,0:T(8,128)(2,1)S(1)}, bf16[2,1024,192]{2,1,0:T(8,128)(2,1)S(1)}, bf16[2,768,384]{2,1,0:T(8,128)(2,1)}, bf16[2,768,192]{2,1,0:T(8,128)(2,1)}, bf16[2,768,192]{2,1,0:T(8,128)(2,1)S(1)}) custom-call(s32[3]{0:T(128)S(1)} %pad_add_fusion.bits, bf16[1024,768]{1,0:T(8,128)(2,1)S(1)} %bitcast.222, ...), custom_call_target="tpu_custom_call" | custom-call | flops 18119393280 | bytes 62914560 | tf_op jit(solution)/shard_map/pallas_call | solution.py:616
  73.0 9.8 %collective-permute-done.14 = bf16[2,2,2,3,32,512]{5,4,3,2,1,0:T(8,128)(2,1)S(1)} collective-permute-done((bf16[2,2,2,3,32,512]{5,4,3,2,1,0:T(8,128)(2,1)S(1)}, bf16[2,2,2,3,32,512]{5,4,3,2,1,0:T(8,128)(2,1)S(1)}, u32[]{:S(2)}, u32[]{:S(2)}) %collective-permute-start.14) | collective-permute-done | bytes 786464 | tf_op jit(solution)/shard_map/ppermute | solution.py:764
  88.4 6.6 %shard_map.180 = (bf16[2,1024,192]{2,1,0:T(8,128)(2,1)S(1)}, f32[2,1024,3]{2,1,0:T(8,128)S(1)}) custom-call(s32[3]{0:T(128)S(1)} %pad_add_fusion.bits, s32[2]{0:T(128)S(1)} %dynamic-slice_reduce_fusion.lens, bf16[2,1024,384]{2,1,0:T(8,128)(2,1)S(1)} %get-tuple-element.150.qk, bf16[2,1024,192]{2,1,0:T(8,128)(2,1)S(1)} %get-tuple-element.162.v, ...), custom_call_target="tpu_custom_call" | custom-call | flops 32212254720 | bytes 31457280 | tf_op jit(solution)/shard_map/pallas_call | solution.py:443
  97.5 6.6 %shard_map.181 = (bf16[2,1024,192]{2,1,0:T(8,128)(2,1)S(1)}, f32[2,1024,3]{2,1,0:T(8,128)S(1)}) custom-call(s32[3]{0:T(128)S(1)} %pad_add_fusion.bits, s32[2]{0:T(128)S(1)} %dynamic-slice_reduce_fusion.lens, bf16[2,1024,384]{2,1,0:T(8,128)(2,1)S(1)} %get-tuple-element.156.qk, bf16[2,1024,192]{2,1,0:T(8,128)(2,1)S(1)} %get-tuple-element.167.v, ...), custom_call_target="tpu_custom_call" | custom-call | flops 32212254720 | bytes 31457280 | tf_op jit(solution)/shard_map/pallas_call | solution.py:443
  105.2 4.9 %shard_map.182 = (bf16[1024,768]{1,0:T(8,128)(2,1)S(1)}, f32[1024,768]{1,0:T(8,128)}, f32[1024,1]{1,0:T(8,128)S(1)}, bf16[768,1024]{1,0:T(8,128)(2,1)}) custom-call(bf16[1024,768]{1,0:T(8,128)(2,1)S(1)} %bitcast.223, bf16[2,1024,192]{2,1,0:T(8,128)(2,1)S(1)} %get-tuple-element.163.m0.mixed, bf16[2,1024,192]{2,1,0:T(8,128)(2,1)S(1)} %get-tuple-element.170.m1.mixed, ...), custom_call_target="tpu_custom_call" | custom-call | flops 12079595520 | bytes 94371840 | tf_op jit(solution)/shard_map/pallas_call | solution.py:649
  110.1 5.5 %collective-permute-done.21 = bf16[2,2,2,96,512]{4,3,2,1,0:T(8,128)(2,1)S(1)} collective-permute-done((bf16[2,2,2,96,512]{4,3,2,1,0:T(8,128)(2,1)S(1)}, bf16[2,2,2,96,512]{4,3,2,1,0:T(8,128)(2,1)S(1)}, u32[]{:S(2)}, u32[]{:S(2)}) %collective-permute-start.21) | collective-permute-done | bytes 786464 | tf_op jit(solution)/shard_map/ppermute | solution.py:764
  118.6 4.9 %collective-permute-done.24 = bf16[2,2,96,256]{3,2,1,0:T(8,128)(2,1)S(1)} collective-permute-done((bf16[2,2,96,256]{3,2,1,0:T(8,128)(2,1)S(1)}, bf16[2,2,96,256]{3,2,1,0:T(8,128)(2,1)S(1)}, u32[]{:S(2)}, u32[]{:S(2)}) %collective-permute-start.24) | collective-permute-done | bytes 196640 | tf_op jit(solution)/shard_map/ppermute | solution.py:759
  126.9 10.9 %shard_map.183 = (bf16[4,1024,512]{2,1,0:T(8,128)(2,1)}, bf16[4,1024,512]{2,1,0:T(8,128)(2,1)}, f32[1024,768]{1,0:T(8,128)S(1)}) custom-call(s32[3]{0:T(128)S(1)} %pad_add_fusion.bits, bf16[1024,768]{1,0:T(8,128)(2,1)S(1)} %get-tuple-element.178.hid, bf16[2,2,2,2,96,512]{5,4,3,2,1,0:T(8,128)(2,1)S(1)} %pad_maximum_fusion.2.ua0.uap, ...), custom_call_target="tpu_custom_call" | custom-call | flops 64424509440 | bytes 125829120 | tf_op jit(solution)/shard_map/pallas_call | solution.py:162
  141.5 10.7 %shard_map.184 = (bf16[4,1024,256]{2,1,0:T(8,128)(2,1)S(1)}, bf16[4,1024,256]{2,1,0:T(8,128)(2,1)S(1)}, bf16[1024,768]{1,0:T(8,128)(2,1)}, f32[1024,768]{1,0:T(8...) custom-call(s32[3]{0:T(128)S(1)} %pad_add_fusion.bits, ...), custom_call_target="tpu_custom_call" | custom-call | flops 32212254720 | bytes 157286400 | tf_op jit(solution)/shard_map/pallas_call | solution.py:228
  153.4 7.0 %shard_map.185 = (bf16[2,2,2,2,96,768]{5,4,3,2,1,0:T(8,128)(2,1)S(1)}, bf16[2,2,2,2,96,768]{5,4,3,2,1,0:T(8,128)(2,1)S(1)}) custom-call(s32[3]{0:T(128)S(1)} %pad_add_fusion.bits, bf16[768,1024]{1,0:T(8,128)(2,1)S(1)} %get-tuple-element.186.dt, bf16[4,1024,512]{2,1,0:T(8,128)(2,1)S(1)} %copy-done.56, bf16[4,1024,256]{2,1,0:T(8,128)(2,1)S(1)} %get-tuple-element.188.actq), custom_call_target="tpu_custom_call" | custom-call | flops 48318382080 | bytes 110100480 | tf_op jit(solution)/shard_map/pallas_call | solution.py:272
  162.9 10.2 %shard_map.186 = (bf16[2,2,2,2,96,768]{5,4,3,2,1,0:T(8,128)(2,1)S(1)}, f32[1024,768]{1,0:T(8,128)S(1)}) custom-call(s32[3]{0:T(128)S(1)} %pad_add_fusion.bits, bf16[768,1024]{1,0:T(8,128)(2,1)S(1)} %copy-done.22, bf16[1024,768]{1,0:T(8,128)(2,1)S(1)} %copy-done.58, bf16[2,2,2,2,96,512]{5,4,3,2,1,0:T(8,128)(2,1)S(1)} %collective-permute-done.26.ua1.uap, ...), custom_call_target="tpu_custom_call" | custom-call | flops 72477573120 | bytes 235929600 | tf_op jit(solution)/shard_map/pallas_call | solution.py:381
  173.2 3.6 %fusion = bf16[2,2,2,96,768]{4,3,2,1,0:T(8,128)(2,1)} fusion(bf16[2,2,2,2,96,768]{5,4,3,2,1,0:T(8,128)(2,1)} %collective-permute-done.32, bf16[2,2,2,2,96,768]{5,4,3,2,1,0:T(8,128)(2,1)S(1)} %get-tuple-element.219), kind=kLoop, calls=%fused_computation.6 | loop fusion | flops 2359296 | bytes 3538944 | tf_op jit(solution)/shard_map/convert_element_type | solution.py:815
  177.4 16.0 %shard_map.187 = (bf16[2,2,2,2,96,768]{5,4,3,2,1,0:T(8,128)(2,1)S(1)}, f32[1024,768]{1,0:T(8,128)}, bf16[1024,768]{1,0:T(8,128)(2,1)S(1)}, bf16[768,1024]{1,0:T(...) custom-call(s32[3]{0:T(128)S(1)} %pad_add_fusion.bits, bf16[768,1024]{1,0:T(8,128)(2,1)S(1)} %copy-done.22, ...), custom_call_target="tpu_custom_call" | custom-call | flops 72477573120 | bytes 235929600 | tf_op jit(solution)/shard_map/pallas_call | solution.py:381
  197.7 14.5 %shard_map.188 = (bf16[2,1024,384]{2,1,0:T(8,128)(2,1)S(1)}, bf16[2,1024,192]{2,1,0:T(8,128)(2,1)S(1)}, bf16[2,2,2,2,3,32,512]{6,5,4,3,2,1,0:T(8,128)(2,1)S(1)}, bf16[2,2,2,2,3,32,512]{6,5,4,3,2,1,0:T(8,128)(2,1)S(1)}) custom-call(s32[3]{0:T(128)S(1)} %pad_add_fusion.bits, s32[2]{0:T(128)S(1)} %copy-done.15, bf16[2,1024,384]{2,1,0:T(8,128)(2,1)S(1)} %copy-done.35, ...), custom_call_target="tpu_custom_call" | custom-call | flops 80530636800 | bytes 58982400 | tf_op jit(solution)/shard_map/pallas_call | solution.py:576
  214.6 5.0 %shard_map.189 = (bf16[2,2,2,2,96,384]{5,4,3,2,1,0:T(8,128)(2,1)S(1)}, bf16[2,2,2,2,96,384]{5,4,3,2,1,0:T(8,128)(2,1)S(1)}) custom-call(s32[3]{0:T(128)S(1)} %pad_add_fusion.bits, bf16[768,1024]{1,0:T(8,128)(2,1)S(1)} %copy-done.31, bf16[768,1024]{1,0:T(8,128)(2,1)S(1)} %copy-done.46, bf16[2,1024,384]{2,1,0:T(8,128)(2,1)S(1)} %get-tuple-element.222.dqk.dqk1, ...), custom_call_target="tpu_custom_call" | custom-call | flops 24159191040 | bytes 62914560 | tf_op jit(solution)/shard_map/pallas_call | solution.py:715
  219.7 5.2 %collective-permute-done.39 = bf16[2,2,2,96,768]{4,3,2,1,0:T(8,128)(2,1)} collective-permute-done((bf16[2,2,2,96,768]{4,3,2,1,0:T(8,128)(2,1)S(1)}, bf16[2,2,2,96,768]{4,3,2,1,0:T(8,128)(2,1)}, u32[]{:S(2)}, u32[]{:S(2)}) %collective-permute-start.39) | collective-permute-done | bytes 1179680 | tf_op jit(solution)/shard_map/ppermute | solution.py:764
  232.5 14.8 %shard_map.190 = (bf16[2,1024,384]{2,1,0:T(8,128)(2,1)S(1)}, bf16[2,1024,192]{2,1,0:T(8,128)(2,1)S(1)}, bf16[2,2,2,3,32,512]{5,4,3,2,1,0:T(8,128)(2,1)S(1)}, bf1...) custom-call(s32[3]{0:T(128)S(1)} %pad_add_fusion.bits, ...), custom_call_target="tpu_custom_call" | custom-call | flops 80530636800 | bytes 58982400 | tf_op jit(solution)/shard_map/pallas_call | solution.py:576
  257.7 4.9 %shard_map.191 = (bf16[2,2,2,96,384]{4,3,2,1,0:T(8,128)(2,1)S(1)}, bf16[2,2,2,96,384]{4,3,2,1,0:T(8,128)(2,1)S(1)}, bf16[2,2,2,96,384]{4,3,2,1,0:T(8,128)(2,1)S(1)}, bf16[2,2,2,96,384]{4,3,2,1,0:T(8,128)(2,1)S(1)}) custom-call(s32[3]{0:T(128)S(1)} %pad_add_fusion.bits, bf16[768,1024]{1,0:T(8,128)(2,1)S(1)} %copy-done.31, bf16[768,1024]{1,0:T(8,128)(2,1)S(1)} %copy-done.46, ...), custom_call_target="tpu_custom_call" | custom-call | flops 24159191040 | bytes 62914560 | tf_op jit(solution)/shard_map/pallas_call | solution.py:715
  269.5 7.1 %collective-permute-done.49 = bf16[2,2,2,3,32,512]{5,4,3,2,1,0:T(8,128)(2,1)S(1)} collective-permute-done((bf16[2,2,2,3,32,512]{5,4,3,2,1,0:T(8,128)(2,1)S(1)}, bf16[2,2,2,3,32,512]{5,4,3,2,1,0:T(8,128)(2,1)S(1)}, u32[]{:S(2)}, u32[]{:S(2)}) %collective-permute-start.49) | collective-permute-done | bytes 786464 | tf_op jit(solution)/shard_map/ppermute | solution.py:759
  281.8 7.1 %shard_map.192 = f32[1024,768]{1,0:T(8,128)} custom-call(f32[1024,768]{1,0:T(8,128)S(1)} %copy-done.49, bf16[2,1024,384]{2,1,0:T(8,128)(2,1)S(1)} %get-tuple-element.258.dqk.dqk0, bf16[2,1024,384]{2,1,0:T(8,128)(2,1)S(1)} %copy-done.48, bf16[2,1024,192]{2,1,0:T(8,128)(2,1)S(1)} %get-tuple-element.245.dv.dv0, bf16[2,1024,192]{2,1,0:T(8,128)(2,1)S(1)} %copy-done.55, ...), custom_call_target="tpu_custom_call" | custom-call | flops 36238786560 | bytes 110100480 | tf_op jit(solution)/shard_map/pallas_call | solution.py:741
  289.3 5.2 %collective-permute-done.52 = bf16[2,2,3,32,512]{4,3,2,1,0:T(8,128)(2,1)S(1)} collective-permute-done((bf16[2,2,3,32,512]{4,3,2,1,0:T(8,128)(2,1)S(1)}, bf16[2,2,3,32,512]{4,3,2,1,0:T(8,128)(2,1)S(1)}, u32[]{:S(2)}, u32[]{:S(2)}) %collective-permute-start.52) | collective-permute-done | bytes 393248 | tf_op jit(solution)/shard_map/ppermute | solution.py:759
  298.6 3.1 collective-permute-done.56
  303.1 7.3 %collective-permute-done.59 = bf16[2,2,3,32,512]{4,3,2,1,0:T(8,128)(2,1)S(1)} collective-permute-done((bf16[2,2,3,32,512]{4,3,2,1,0:T(8,128)(2,1)S(1)}, bf16[2,2,3,32,512]{4,3,2,1,0:T(8,128)(2,1)S(1)}, u32[]{:S(2)}, u32[]{:S(2)}) %collective-permute-start.59) | collective-permute-done | bytes 393248 | tf_op jit(solution)/shard_map/ppermute | solution.py:759
  317.3 4.0 %collective-permute-done.60 = bf16[2,3,32,512]{3,2,1,0:T(8,128)(2,1)S(1)} collective-permute-done((bf16[2,3,32,512]{3,2,1,0:T(8,128)(2,1)S(1)}, bf16[2,3,32,512]{3,2,1,0:T(8,128)(2,1)S(1)}, u32[]{:S(2)}, u32[]{:S(2)}) %collective-permute-start.60) | collective-permute-done | bytes 196640 | tf_op jit(solution)/shard_map/ppermute | solution.py:759
  (333 shorter events, 98.7 us)
Async XLA Ops:
  2.6 11.1 %collective-permute-start = (bf16[2,96,384]{2,1,0:T(8,128)(2,1)S(1)}, bf16[2,96,384]{2,1,0:T(8,128)(2,1)S(1)}, u32[]{:S(2)}, u32[]{:S(2)}) collective-permute-start(bf16[2,96,384]{2,1,0:T(8,128)(2,1)S(1)} %get-tuple-element.319), channel_id=1, source_target_pairs={{0,16},{4,20},{8,24},{12,28},{16,0},{20,4},{24,8},{28,12},{1,17},{... | collective-permute-start | bytes 442376 | tf_op jit(solution)/shard_map/ppermute | solution.py:759
  25.0 11.6 %collective-permute-start.4 = (bf16[2,3,32,512]{3,2,1,0:T(8,128)(2,1)S(1)}, bf16[2,3,32,512]{3,2,1,0:T(8,128)(2,1)S(1)}, u32[]{:S(2)}, u32[]{:S(2)}) collective-permute-start(bf16[2,3,32,512]{3,2,1,0:T(8,128)(2,1)S(1)} %pad_maximum_fusion.28), channel_id=1, source_target_pairs={{0,16},{4,20},{8,24},{12,28},{16,0},{20,4},{24,8},{28,12},{1,17},{... | collective-permute-start | bytes 589832 | tf_op jit(solution)/shard_map/ppermute | solution.py:759
  36.7 15.2 %collective-permute-start.6 = (bf16[2,2,2,96,384]{4,3,2,1,0:T(8,128)(2,1)S(1)}, bf16[2,2,2,96,384]{4,3,2,1,0:T(8,128)(2,1)S(1)}, u32[]{:S(2)}, u32[]{:S(2)}) collective-permute-start(bf16[2,2,2,96,384]{4,3,2,1,0:T(8,128)(2,1)S(1)} %pad_maximum_fusion.12), channel_id=1, source_target_pairs={{0,2},{1,3},{2,0},{3,1},{4,6},{5,7},{6,4},{7,5},{8,10},{9,11},{10,... | collective-permute-start | bytes 1769480 | tf_op jit(solution)/shard_map/ppermute | solution.py:764
  37.3 14.6 %collective-permute-start.7 = (bf16[2,2,2,96,384]{4,3,2,1,0:T(8,128)(2,1)S(1)}, bf16[2,2,2,96,384]{4,3,2,1,0:T(8,128)(2,1)S(1)}, u32[]{:S(2)}, u32[]{:S(2)}) collective-permute-start(bf16[2,2,2,96,384]{4,3,2,1,0:T(8,128)(2,1)S(1)} %pad_maximum_fusion.13), channel_id=1, source_target_pairs={{0,4},{4,0},{8,12},{12,8},{16,20},{20,16},{24,28},{28,24},{1,5},{5... | collective-permute-start | bytes 1769480 | tf_op jit(solution)/shard_map/ppermute | solution.py:759
  47.5 15.3 %collective-permute-start.12 = (bf16[2,96,512]{2,1,0:T(8,128)(2,1)S(1)}, bf16[2,96,512]{2,1,0:T(8,128)(2,1)S(1)}, u32[]{:S(2)}, u32[]{:S(2)}) collective-permute-start(bf16[2,96,512]{2,1,0:T(8,128)(2,1)S(1)} %pad_maximum_fusion.29), channel_id=1, source_target_pairs={{0,16},{4,20},{8,24},{12,28},{16,0},{20,4},{24,8},{28,12},{1,17},{... | collective-permute-start | bytes 589832 | tf_op jit(solution)/shard_map/ppermute | solution.py:759
  64.4 18.5 %collective-permute-start.14 = (bf16[2,2,2,3,32,512]{5,4,3,2,1,0:T(8,128)(2,1)S(1)}, bf16[2,2,2,3,32,512]{5,4,3,2,1,0:T(8,128)(2,1)S(1)}, u32[]{:S(2)}, u32[]{:S(2)}) collective-permute-start(bf16[2,2,2,3,32,512]{5,4,3,2,1,0:T(8,128)(2,1)S(1)} %pad_maximum_fusion.6), channel_id=1, source_target_pairs={{0,2},{1,3},{2,0},{3,1},{4,6},{5,7},{6,4},{7,5},{8,10},{9,11},{10,... | collective-permute-start | bytes 2359304 | tf_op jit(solution)/shard_map/ppermute | solution.py:764
  65.8 17.2 %collective-permute-start.15 = (bf16[2,2,2,3,32,512]{5,4,3,2,1,0:T(8,128)(2,1)S(1)}, bf16[2,2,2,3,32,512]{5,4,3,2,1,0:T(8,128)(2,1)S(1)}, u32[]{:S(2)}, u32[]{:S(2)}) collective-permute-start(bf16[2,2,2,3,32,512]{5,4,3,2,1,0:T(8,128)(2,1)S(1)} %pad_maximum_fusion.7), channel_id=1, source_target_pairs={{0,4},{4,0},{8,12},{12,8},{16,20},{20,16},{24,28},{28,24},{1,5},{5... | collective-permute-start | bytes 2359304 | tf_op jit(solution)/shard_map/ppermute | solution.py:759
  83.2 11.8 %collective-permute-start.18 = (bf16[2,96,256]{2,1,0:T(8,128)(2,1)S(1)}, bf16[2,96,256]{2,1,0:T(8,128)(2,1)S(1)}, u32[]{:S(2)}, u32[]{:S(2)}) collective-permute-start(bf16[2,96,256]{2,1,0:T(8,128)(2,1)S(1)} %pad_maximum_fusion.34), channel_id=1, source_target_pairs={{0,16},{4,20},{8,24},{12,28},{16,0},{20,4},{24,8},{28,12},{1,17},{... | collective-permute-start | bytes 294920 | tf_op jit(solution)/shard_map/ppermute | solution.py:759
  96.0 14.0 %collective-permute-start.23 = (bf16[2,2,96,256]{3,2,1,0:T(8,128)(2,1)S(1)}, bf16[2,2,96,256]{3,2,1,0:T(8,128)(2,1)S(1)}, u32[]{:S(2)}, u32[]{:S(2)}) collective-permute-start(bf16[2,2,96,256]{3,2,1,0:T(8,128)(2,1)S(1)} %pad_maximum_fusion.30), channel_id=1, source_target_pairs={{0,8},{4,12},{8,0},{12,4},{16,24},{20,28},{24,16},{28,20},{1,9},{5... | collective-permute-start | bytes 589832 | tf_op jit(solution)/shard_map/ppermute | solution.py:759
  96.5 19.2 %collective-permute-start.21 = (bf16[2,2,2,96,512]{4,3,2,1,0:T(8,128)(2,1)S(1)}, bf16[2,2,2,96,512]{4,3,2,1,0:T(8,128)(2,1)S(1)}, u32[]{:S(2)}, u32[]{:S(2)}) collective-permute-start(bf16[2,2,2,96,512]{4,3,2,1,0:T(8,128)(2,1)S(1)} %pad_maximum_fusion.8), channel_id=1, source_target_pairs={{0,2},{1,3},{2,0},{3,1},{4,6},{5,7},{6,4},{7,5},{8,10},{9,11},{10,... | collective-permute-start | bytes 2359304 | tf_op jit(solution)/shard_map/ppermute | solution.py:764
  97.0 18.9 %collective-permute-start.22 = (bf16[2,2,2,96,512]{4,3,2,1,0:T(8,128)(2,1)S(1)}, bf16[2,2,2,96,512]{4,3,2,1,0:T(8,128)(2,1)S(1)}, u32[]{:S(2)}, u32[]{:S(2)}) collective-permute-start(bf16[2,2,2,96,512]{4,3,2,1,0:T(8,128)(2,1)S(1)} %pad_maximum_fusion.9), channel_id=1, source_target_pairs={{0,4},{4,0},{8,12},{12,8},{16,20},{20,16},{24,28},{28,24},{1,5},{5... | collective-permute-start | bytes 2359304 | tf_op jit(solution)/shard_map/ppermute | solution.py:759
  123.8 14.0 %collective-permute-start.28 = (bf16[2,2,2,96,256]{4,3,2,1,0:T(8,128)(2,1)S(1)}, bf16[2,2,2,96,256]{4,3,2,1,0:T(8,128)(2,1)S(1)}, u32[]{:S(2)}, u32[]{:S(2)}) collective-permute-start(bf16[2,2,2,96,256]{4,3,2,1,0:T(8,128)(2,1)S(1)} %pad_maximum_fusion.19), channel_id=1, source_target_pairs={{0,2},{1,3},{2,0},{3,1},{4,6},{5,7},{6,4},{7,5},{8,10},{9,11},{10,... | collective-permute-start | bytes 1179656 | tf_op jit(solution)/shard_map/ppermute | solution.py:764
  125.4 12.5 %collective-permute-start.29 = (bf16[2,2,2,96,256]{4,3,2,1,0:T(8,128)(2,1)S(1)}, bf16[2,2,2,96,256]{4,3,2,1,0:T(8,128)(2,1)S(1)}, u32[]{:S(2)}, u32[]{:S(2)}) collective-permute-start(bf16[2,2,2,96,256]{4,3,2,1,0:T(8,128)(2,1)S(1)} %pad_maximum_fusion.20), channel_id=1, source_target_pairs={{0,4},{4,0},{8,12},{12,8},{16,20},{20,16},{24,28},{28,24},{1,5},{5... | collective-permute-start | bytes 1179656 | tf_op jit(solution)/shard_map/ppermute | solution.py:759
  160.5 12.7 %collective-permute-start.32 = (bf16[2,2,2,2,96,768]{5,4,3,2,1,0:T(8,128)(2,1)S(1)}, bf16[2,2,2,2,96,768]{5,4,3,2,1,0:T(8,128)(2,1)}, u32[]{:S(2)}, u32[]{:S(2)}) collective-permute-start(bf16[2,2,2,2,96,768]{5,4,3,2,1,0:T(8,128)(2,1)S(1)} %get-tuple-element.190), channel_id=1, source_target_pairs={{0,1},{1,0},{2,3},{3,2},{4,5},{5,4},{6,7},{7,6},{8,9},{9,8},{10,11... | collective-permute-start | bytes 7077896 | tf_op jit(solution)/shard_map/ppermute | solution.py:764
  176.8 35.4 %collective-permute-start.35 = (bf16[2,2,2,96,768]{4,3,2,1,0:T(8,128)(2,1)}, bf16[2,2,2,96,768]{4,3,2,1,0:T(8,128)(2,1)}, u32[]{:S(2)}, u32[]{:S(2)}) collective-permute-start(bf16[2,2,2,96,768]{4,3,2,1,0:T(8,128)(2,1)} %fusion), channel_id=1, source_target_pairs={{0,4},{4,0},{8,12},{12,8},{16,20},{20,16},{24,28},{28,24},{1,5},{5... | collective-permute-start | bytes 3538952 | tf_op jit(solution)/shard_map/ppermute | solution.py:759
  177.4 16.1 %collective-permute-start.33 = (bf16[2,2,2,2,96,768]{5,4,3,2,1,0:T(8,128)(2,1)S(1)}, bf16[2,2,2,2,96,768]{5,4,3,2,1,0:T(8,128)(2,1)}, u32[]{:S(2)}, u32[]{:S(2)}) collective-permute-start(bf16[2,2,2,2,96,768]{5,4,3,2,1,0:T(8,128)(2,1)S(1)} %get-tuple-element.203), channel_id=1, source_target_pairs={{0,1},{1,0},{2,3},{3,2},{4,5},{5,4},{6,7},{7,6},{8,9},{9,8},{10,11... | collective-permute-start | bytes 7077896 | tf_op jit(solution)/shard_map/ppermute | solution.py:764
  193.5 18.7 %collective-permute-start.34 = (f32[4,768]{1,0:T(4,128)S(1)}, f32[4,768]{1,0:T(4,128)S(1)}, u32[]{:S(2)}, u32[]{:S(2)}) collective-permute-start(f32[4,768]{1,0:T(4,128)S(1)} %pad_maximum_fusion.35), channel_id=1, source_target_pairs={{0,1},{1,0},{2,3},{3,2},{4,5},{5,4},{6,7},{7,6},{8,9},{9,8},{10,11... | collective-permute-start | bytes 36872 | tf_op jit(solution)/shard_map/ppermute | solution.py:847
  197.1 27.8 %collective-permute-start.39 = (bf16[2,2,2,96,768]{4,3,2,1,0:T(8,128)(2,1)S(1)}, bf16[2,2,2,96,768]{4,3,2,1,0:T(8,128)(2,1)}, u32[]{:S(2)}, u32[]{:S(2)}) collective-permute-start(bf16[2,2,2,96,768]{4,3,2,1,0:T(8,128)(2,1)S(1)} %fusion.1), channel_id=1, source_target_pairs={{0,2},{1,3},{2,0},{3,1},{4,6},{5,7},{6,4},{7,5},{8,10},{9,11},{10,... | collective-permute-start | bytes 3538952 | tf_op jit(solution)/shard_map/ppermute | solution.py:764
  228.5 18.9 %collective-permute-start.42 = (bf16[2,2,2,2,96,384]{5,4,3,2,1,0:T(8,128)(2,1)S(1)}, bf16[2,2,2,2,96,384]{5,4,3,2,1,0:T(8,128)(2,1)S(1)}, u32[]{:S(2)}, u32[]{:S(2)}) collective-permute-start(bf16[2,2,2,2,96,384]{5,4,3,2,1,0:T(8,128)(2,1)S(1)} %get-tuple-element.241), channel_id=1, source_target_pairs={{0,1},{1,0},{2,3},{3,2},{4,5},{5,4},{6,7},{7,6},{8,9},{9,8},{10,11... | collective-permute-start | bytes 3538952 | tf_op jit(solution)/shard_map/ppermute | solution.py:764
  228.6 18.8 %collective-permute-start.43 = (bf16[2,2,2,2,96,384]{5,4,3,2,1,0:T(8,128)(2,1)S(1)}, bf16[2,2,2,2,96,384]{5,4,3,2,1,0:T(8,128)(2,1)S(1)}, u32[]{:S(2)}, u32[]{:S(2)}) collective-permute-start(bf16[2,2,2,2,96,384]{5,4,3,2,1,0:T(8,128)(2,1)S(1)} %get-tuple-element.242), channel_id=1, source_target_pairs={{0,1},{1,0},{2,3},{3,2},{4,5},{5,4},{6,7},{7,6},{8,9},{9,8},{10,11... | collective-permute-start | bytes 3538952 | tf_op jit(solution)/shard_map/ppermute | solution.py:764
  230.1 17.2 %collective-permute-start.41 = (f32[4,768]{1,0:T(4,128)S(1)}, f32[4,768]{1,0:T(4,128)S(1)}, u32[]{:S(2)}, u32[]{:S(2)}) collective-permute-start(f32[4,768]{1,0:T(4,128)S(1)} %add.275), channel_id=1, source_target_pairs={{0,16},{4,20},{8,24},{12,28},{16,0},{20,4},{24,8},{28,12},{1,17},{... | collective-permute-start | bytes 36872 | tf_op jit(solution)/shard_map/ppermute | solution.py:847
  231.5 15.9 %collective-permute-start.44 = (bf16[2,2,96,768]{3,2,1,0:T(8,128)(2,1)S(1)}, bf16[2,2,96,768]{3,2,1,0:T(8,128)(2,1)S(1)}, u32[]{:S(2)}, u32[]{:S(2)}) collective-permute-start(bf16[2,2,96,768]{3,2,1,0:T(8,128)(2,1)S(1)} %fusion.4), channel_id=1, source_target_pairs={{0,2},{1,3},{2,0},{3,1},{4,6},{5,7},{6,4},{7,5},{8,10},{9,11},{10,... | collective-permute-start | bytes 1769480 | tf_op jit(solution)/shard_map/ppermute | solution.py:764
  232.0 15.4 %collective-permute-start.45 = (bf16[2,2,96,768]{3,2,1,0:T(8,128)(2,1)S(1)}, bf16[2,2,96,768]{3,2,1,0:T(8,128)(2,1)S(1)}, u32[]{:S(2)}, u32[]{:S(2)}) collective-permute-start(bf16[2,2,96,768]{3,2,1,0:T(8,128)(2,1)S(1)} %fusion.3), channel_id=1, source_target_pairs={{0,4},{4,0},{8,12},{12,8},{16,20},{20,16},{24,28},{28,24},{1,5},{5... | collective-permute-start | bytes 1769480 | tf_op jit(solution)/shard_map/ppermute | solution.py:759
  249.0 20.5 %collective-permute-start.48 = (bf16[2,2,2,3,32,512]{5,4,3,2,1,0:T(8,128)(2,1)S(1)}, bf16[2,2,2,3,32,512]{5,4,3,2,1,0:T(8,128)(2,1)S(1)}, u32[]{:S(2)}, u32[]{:S(2)}) collective-permute-start(bf16[2,2,2,3,32,512]{5,4,3,2,1,0:T(8,128)(2,1)S(1)} %get-tuple-element.252), channel_id=1, source_target_pairs={{0,2},{1,3},{2,0},{3,1},{4,6},{5,7},{6,4},{7,5},{8,10},{9,11},{10,... | collective-permute-start | bytes 2359304 | tf_op jit(solution)/shard_map/ppermute | solution.py:764
  254.4 13.3 %collective-permute-start.47 = (bf16[2,2,96,768]{3,2,1,0:T(8,128)(2,1)S(1)}, bf16[2,2,96,768]{3,2,1,0:T(8,128)(2,1)S(1)}, u32[]{:S(2)}, u32[]{:S(2)}) collective-permute-start(bf16[2,2,96,768]{3,2,1,0:T(8,128)(2,1)S(1)} %pad_maximum_fusion.14), channel_id=1, source_target_pairs={{0,8},{4,12},{8,0},{12,4},{16,24},{20,28},{24,16},{28,20},{1,9},{5... | collective-permute-start | bytes 1769480 | tf_op jit(solution)/shard_map/ppermute | solution.py:759
  256.1 20.5 %collective-permute-start.49 = (bf16[2,2,2,3,32,512]{5,4,3,2,1,0:T(8,128)(2,1)S(1)}, bf16[2,2,2,3,32,512]{5,4,3,2,1,0:T(8,128)(2,1)S(1)}, u32[]{:S(2)}, u32[]{:S(2)}) collective-permute-start(bf16[2,2,2,3,32,512]{5,4,3,2,1,0:T(8,128)(2,1)S(1)} %get-tuple-element.253), channel_id=1, source_target_pairs={{0,4},{4,0},{8,12},{12,8},{16,20},{20,16},{24,28},{28,24},{1,5},{5... | collective-permute-start | bytes 2359304 | tf_op jit(solution)/shard_map/ppermute | solution.py:759
  262.6 26.3 %collective-permute-start.50 = (bf16[2,2,2,96,384]{4,3,2,1,0:T(8,128)(2,1)S(1)}, bf16[2,2,2,96,384]{4,3,2,1,0:T(8,128)(2,1)S(1)}, u32[]{:S(2)}, u32[]{:S(2)}) collective-permute-start(bf16[2,2,2,96,384]{4,3,2,1,0:T(8,128)(2,1)S(1)} %get-tuple-element.264), channel_id=1, source_target_pairs={{0,2},{1,3},{2,0},{3,1},{4,6},{5,7},{6,4},{7,5},{8,10},{9,11},{10,... | collective-permute-start | bytes 1769480 | tf_op jit(solution)/shard_map/ppermute | solution.py:764
  264.2 25.1 %collective-permute-start.51 = (bf16[2,2,2,96,384]{4,3,2,1,0:T(8,128)(2,1)S(1)}, bf16[2,2,2,96,384]{4,3,2,1,0:T(8,128)(2,1)S(1)}, u32[]{:S(2)}, u32[]{:S(2)}) collective-permute-start(bf16[2,2,2,96,384]{4,3,2,1,0:T(8,128)(2,1)S(1)} %get-tuple-element.265), channel_id=1, source_target_pairs={{0,4},{4,0},{8,12},{12,8},{16,20},{20,16},{24,28},{28,24},{1,5},{5... | collective-permute-start | bytes 1769480 | tf_op jit(solution)/shard_map/ppermute | solution.py:759
  276.7 12.5 %collective-permute-start.54 = (bf16[2,96,768]{2,1,0:T(8,128)(2,1)S(1)}, bf16[2,96,768]{2,1,0:T(8,128)(2,1)S(1)}, u32[]{:S(2)}, u32[]{:S(2)}) collective-permute-start(bf16[2,96,768]{2,1,0:T(8,128)(2,1)S(1)} %pad_maximum_fusion.24), channel_id=1, source_target_pairs={{0,16},{4,20},{8,24},{12,28},{16,0},{20,4},{24,8},{28,12},{1,17},{... | collective-permute-start | bytes 884744 | tf_op jit(solution)/shard_map/ppermute | solution.py:759
  281.2 13.2 %collective-permute-start.52 = (bf16[2,2,3,32,512]{4,3,2,1,0:T(8,128)(2,1)S(1)}, bf16[2,2,3,32,512]{4,3,2,1,0:T(8,128)(2,1)S(1)}, u32[]{:S(2)}, u32[]{:S(2)}) collective-permute-start(bf16[2,2,3,32,512]{4,3,2,1,0:T(8,128)(2,1)S(1)} %fusion.6), channel_id=1, source_target_pairs={{0,4},{4,0},{8,12},{12,8},{16,20},{20,16},{24,28},{28,24},{1,5},{5... | collective-permute-start | bytes 1179656 | tf_op jit(solution)/shard_map/ppermute | solution.py:759
  298.1 12.3 %collective-permute-start.59 = (bf16[2,2,3,32,512]{4,3,2,1,0:T(8,128)(2,1)S(1)}, bf16[2,2,3,32,512]{4,3,2,1,0:T(8,128)(2,1)S(1)}, u32[]{:S(2)}, u32[]{:S(2)}) collective-permute-start(bf16[2,2,3,32,512]{4,3,2,1,0:T(8,128)(2,1)S(1)} %pad_maximum_fusion.21), channel_id=1, source_target_pairs={{0,8},{4,12},{8,0},{12,4},{16,24},{20,28},{24,16},{28,20},{1,9},{5... | collective-permute-start | bytes 1179656 | tf_op jit(solution)/shard_map/ppermute | solution.py:759
  302.6 12.3 %collective-permute-start.57 = (bf16[2,2,96,384]{3,2,1,0:T(8,128)(2,1)S(1)}, bf16[2,2,96,384]{3,2,1,0:T(8,128)(2,1)S(1)}, u32[]{:S(2)}, u32[]{:S(2)}) collective-permute-start(bf16[2,2,96,384]{3,2,1,0:T(8,128)(2,1)S(1)} %pad_maximum_fusion.25), channel_id=1, source_target_pairs={{0,8},{4,12},{8,0},{12,4},{16,24},{20,28},{24,16},{28,20},{1,9},{5... | collective-permute-start | bytes 884744 | tf_op jit(solution)/shard_map/ppermute | solution.py:759
  (102 other events, 1288.2 us)

commit v5 on v4

--- a/solution.py
+++ b/solution.py
@@ -720,7 +720,7 @@
             scratch_shapes=[pltpu.VMEM((width, w2), kind), pltpu.VMEM((width, w2), kind)],
         ),
         compiler_params=params(26),
-        cost_estimate=cost(2 * rows * width * 2 * 2 * w2, 8 * rows * width),
+        cost_estimate=cost(1 if last else 8 * rows * width * w2, 1 if last else 8 * rows * width),
     )(bits, xt, dat, dqk, dv, mixed, *got)
 
 

time: 327 us -> 325 us (level)
  waiting for transfers between devices: 98.4 us -> 91.1 us
  local copies, waits for them, and re-layouts: 9.8 us -> 16.4 us
    unnamed x148 -> x146, local copies, waits for them, and re-layouts: 7.77 us -> 14.3 us
    ppermute x28, waiting for transfers between devices: 30 us -> 25.5 us  [partner_head(): return lax.ppermute(value, 'head', [(i, i ^ 1 << bit) for i in range(size)])]
  transfers between devices with their start and end apart: 61 -> 61, of which waited for: 30 -> 31; matrix products, arithmetic and copies ran while one was open for 5% -> 4% of each run, Pallas kernels for 34% -> 35%
where the time goes in v5:
time: 325 us; the launch traced here: 322 us
  Pallas kernels  129 us (40%)
  waiting for transfers between devices  91.1 us (28%)
  starting transfers between devices  64.4 us (20%)
  other arithmetic  18.9 us (6%)
  local copies, waits for them, and re-layouts  16.4 us (5%)
    ppermute x28, waiting for transfers between devices, partner_dp(): return lax.ppermute(value, 'dp', [(i, i ^ step) for i in range(size)])  64 us
    ppermute x28, starting transfers between devices, partner_dp(): return lax.ppermute(value, 'dp', [(i, i ^ step) for i in range(size)])  39.9 us
    pallas_call x2, Pallas kernels, attention_backward(): pl.pallas_call(functools.partial(att_bwd_kernel, last), out_shape=out_sha...  29.2 us
    pallas_call x2, Pallas kernels, ffn_backward(): pl.pallas_call(functools.partial(ffn_bwd_kernel, chunk, last), out_shape=...  26 us
    ppermute x28, waiting for transfers between devices, partner_head(): return lax.ppermute(value, 'head', [(i, i ^ 1 << bit) for i in range(size)])  25.5 us
    ppermute x28, starting transfers between devices, partner_head(): return lax.ppermute(value, 'head', [(i, i ^ 1 << bit) for i in range(size)])  18.7 us
    unnamed x146, local copies, waits for them, and re-layouts  14.3 us
    pallas_call x2, Pallas kernels, attention_forward(): pl.pallas_call(att_fwd_kernel, out_shape=(sds((2, rows, w1), BF16), sds((...  13.3 us
  transfers between devices with their start and end apart: 61, of which 31 were waited for; matrix products, arithmetic and copies ran while one was open for 4% of the time, Pallas kernels for 35%

profile of v5, /device:TPU:0, one launch (start us, length us, event | category | flops | bytes accessed | tf_op | source)
XLA Modules:
  0.0 322.4 jit_solution(10739493537772059356)
XLA Ops:
  2.6 4.1 %collective-permute-start = (bf16[2,96,384]{2,1,0:T(8,128)(2,1)S(1)}, bf16[2,96,384]{2,1,0:T(8,128)(2,1)S(1)}, u32[]{:S(2)}, u32[]{:S(2)}) collective-permute-start(bf16[2,96,384]{2,1,0:T(8,128)(2,1)S(1)} %get-tuple-element.319), channel_id=1, source_target_pairs={{0,16},{4,20},{8,24},{12,28},{16,0},{20,4},{24,8},{28,12},{1,17},{... | collective-permute-start | bytes 442376 | tf_op jit(solution)/shard_map/ppermute | solution.py:759
  8.0 5.8 %collective-permute-done = bf16[2,96,384]{2,1,0:T(8,128)(2,1)S(1)} collective-permute-done((bf16[2,96,384]{2,1,0:T(8,128)(2,1)S(1)}, bf16[2,96,384]{2,1,0:T(8,128)(2,1)S(1)}, u32[]{:S(2)}, u32[]{:S(2)}) %collective-permute-start) | collective-permute-done | bytes 147488 | tf_op jit(solution)/shard_map/ppermute | solution.py:759
  14.6 7.4 %collective-permute-done.1 = bf16[2,2,96,384]{3,2,1,0:T(8,128)(2,1)S(1)} collective-permute-done((bf16[2,2,96,384]{3,2,1,0:T(8,128)(2,1)S(1)}, bf16[2,2,96,384]{3,2,1,0:T(8,128)(2,1)S(1)}, u32[]{:S(2)}, u32[]{:S(2)}) %collective-permute-start.1) | collective-permute-done | bytes 294944 | tf_op jit(solution)/shard_map/ppermute | solution.py:759
  25.0 3.4 %collective-permute-start.4 = (bf16[2,3,32,512]{3,2,1,0:T(8,128)(2,1)S(1)}, bf16[2,3,32,512]{3,2,1,0:T(8,128)(2,1)S(1)}, u32[]{:S(2)}, u32[]{:S(2)}) collective-permute-start(bf16[2,3,32,512]{3,2,1,0:T(8,128)(2,1)S(1)} %pad_maximum_fusion.28), channel_id=1, source_target_pairs={{0,16},{4,20},{8,24},{12,28},{16,0},{20,4},{24,8},{28,12},{1,17},{... | collective-permute-start | bytes 589832 | tf_op jit(solution)/shard_map/ppermute | solution.py:759
  30.7 6.0 %collective-permute-done.4 = bf16[2,3,32,512]{3,2,1,0:T(8,128)(2,1)S(1)} collective-permute-done((bf16[2,3,32,512]{3,2,1,0:T(8,128)(2,1)S(1)}, bf16[2,3,32,512]{3,2,1,0:T(8,128)(2,1)S(1)}, u32[]{:S(2)}, u32[]{:S(2)}) %collective-permute-start.4) | collective-permute-done | bytes 196640 | tf_op jit(solution)/shard_map/ppermute | solution.py:759
  38.9 8.6 %collective-permute-done.5 = bf16[2,2,3,32,512]{4,3,2,1,0:T(8,128)(2,1)} collective-permute-done((bf16[2,2,3,32,512]{4,3,2,1,0:T(8,128)(2,1)S(1)}, bf16[2,2,3,32,512]{4,3,2,1,0:T(8,128)(2,1)}, u32[]{:S(2)}, u32[]{:S(2)}) %collective-permute-start.5) | collective-permute-done | bytes 393248 | tf_op jit(solution)/shard_map/ppermute | solution.py:759
  47.5 3.2 collective-permute-start.12
  56.5 5.7 %shard_map.178 = (bf16[2,1024,384]{2,1,0:T(8,128)(2,1)S(1)}, bf16[2,1024,192]{2,1,0:T(8,128)(2,1)S(1)}, bf16[2,768,384]{2,1,0:T(8,128)(2,1)}, bf16[2,768,192]{2,...) custom-call(s32[3]{0:T(128)S(1)} %pad_add_fusion.bits, bf16[1024,768]{1,0:T(8,128)(2,1)S(1)} %bitcast.221, ...), custom_call_target="tpu_custom_call" | custom-call | flops 18119393280 | bytes 62914560 | tf_op jit(solution)/shard_map/pallas_call | solution.py:616
  66.4 4.6 %shard_map.179 = (bf16[2,1024,384]{2,1,0:T(8,128)(2,1)S(1)}, bf16[2,1024,192]{2,1,0:T(8,128)(2,1)S(1)}, bf16[2,768,384]{2,1,0:T(8,128)(2,1)}, bf16[2,768,192]{2,1,0:T(8,128)(2,1)}, bf16[2,768,192]{2,1,0:T(8,128)(2,1)S(1)}) custom-call(s32[3]{0:T(128)S(1)} %pad_add_fusion.bits, bf16[1024,768]{1,0:T(8,128)(2,1)S(1)} %bitcast.222, ...), custom_call_target="tpu_custom_call" | custom-call | flops 18119393280 | bytes 62914560 | tf_op jit(solution)/shard_map/pallas_call | solution.py:616
  73.0 9.8 %collective-permute-done.14 = bf16[2,2,2,3,32,512]{5,4,3,2,1,0:T(8,128)(2,1)S(1)} collective-permute-done((bf16[2,2,2,3,32,512]{5,4,3,2,1,0:T(8,128)(2,1)S(1)}, bf16[2,2,2,3,32,512]{5,4,3,2,1,0:T(8,128)(2,1)S(1)}, u32[]{:S(2)}, u32[]{:S(2)}) %collective-permute-start.14) | collective-permute-done | bytes 786464 | tf_op jit(solution)/shard_map/ppermute | solution.py:764
  88.5 6.6 %shard_map.180 = (bf16[2,1024,192]{2,1,0:T(8,128)(2,1)S(1)}, f32[2,1024,3]{2,1,0:T(8,128)S(1)}) custom-call(s32[3]{0:T(128)S(1)} %pad_add_fusion.bits, s32[2]{0:T(128)S(1)} %dynamic-slice_reduce_fusion.lens, bf16[2,1024,384]{2,1,0:T(8,128)(2,1)S(1)} %get-tuple-element.150.qk, bf16[2,1024,192]{2,1,0:T(8,128)(2,1)S(1)} %get-tuple-element.162.v, ...), custom_call_target="tpu_custom_call" | custom-call | flops 32212254720 | bytes 31457280 | tf_op jit(solution)/shard_map/pallas_call | solution.py:443
  97.6 6.6 %shard_map.181 = (bf16[2,1024,192]{2,1,0:T(8,128)(2,1)S(1)}, f32[2,1024,3]{2,1,0:T(8,128)S(1)}) custom-call(s32[3]{0:T(128)S(1)} %pad_add_fusion.bits, s32[2]{0:T(128)S(1)} %dynamic-slice_reduce_fusion.lens, bf16[2,1024,384]{2,1,0:T(8,128)(2,1)S(1)} %get-tuple-element.156.qk, bf16[2,1024,192]{2,1,0:T(8,128)(2,1)S(1)} %get-tuple-element.167.v, ...), custom_call_target="tpu_custom_call" | custom-call | flops 32212254720 | bytes 31457280 | tf_op jit(solution)/shard_map/pallas_call | solution.py:443
  105.3 4.9 %shard_map.182 = (bf16[1024,768]{1,0:T(8,128)(2,1)S(1)}, f32[1024,768]{1,0:T(8,128)}, f32[1024,1]{1,0:T(8,128)S(1)}, bf16[768,1024]{1,0:T(8,128)(2,1)}) custom-call(bf16[1024,768]{1,0:T(8,128)(2,1)S(1)} %bitcast.223, bf16[2,1024,192]{2,1,0:T(8,128)(2,1)S(1)} %get-tuple-element.163.m0.mixed, bf16[2,1024,192]{2,1,0:T(8,128)(2,1)S(1)} %get-tuple-element.170.m1.mixed, ...), custom_call_target="tpu_custom_call" | custom-call | flops 12079595520 | bytes 94371840 | tf_op jit(solution)/shard_map/pallas_call | solution.py:649
  110.2 5.5 %collective-permute-done.21 = bf16[2,2,2,96,512]{4,3,2,1,0:T(8,128)(2,1)S(1)} collective-permute-done((bf16[2,2,2,96,512]{4,3,2,1,0:T(8,128)(2,1)S(1)}, bf16[2,2,2,96,512]{4,3,2,1,0:T(8,128)(2,1)S(1)}, u32[]{:S(2)}, u32[]{:S(2)}) %collective-permute-start.21) | collective-permute-done | bytes 786464 | tf_op jit(solution)/shard_map/ppermute | solution.py:764
  118.7 4.9 %collective-permute-done.24 = bf16[2,2,96,256]{3,2,1,0:T(8,128)(2,1)S(1)} collective-permute-done((bf16[2,2,96,256]{3,2,1,0:T(8,128)(2,1)S(1)}, bf16[2,2,96,256]{3,2,1,0:T(8,128)(2,1)S(1)}, u32[]{:S(2)}, u32[]{:S(2)}) %collective-permute-start.24) | collective-permute-done | bytes 196640 | tf_op jit(solution)/shard_map/ppermute | solution.py:759
  127.0 11.0 %shard_map.183 = (bf16[4,1024,512]{2,1,0:T(8,128)(2,1)}, bf16[4,1024,512]{2,1,0:T(8,128)(2,1)}, f32[1024,768]{1,0:T(8,128)S(1)}) custom-call(s32[3]{0:T(128)S(1)} %pad_add_fusion.bits, bf16[1024,768]{1,0:T(8,128)(2,1)S(1)} %get-tuple-element.178.hid, bf16[2,2,2,2,96,512]{5,4,3,2,1,0:T(8,128)(2,1)S(1)} %pad_maximum_fusion.2.ua0.uap, ...), custom_call_target="tpu_custom_call" | custom-call | flops 64424509440 | bytes 125829120 | tf_op jit(solution)/shard_map/pallas_call | solution.py:162
  141.7 10.7 %shard_map.184 = (bf16[4,1024,256]{2,1,0:T(8,128)(2,1)S(1)}, bf16[4,1024,256]{2,1,0:T(8,128)(2,1)S(1)}, bf16[1024,768]{1,0:T(8,128)(2,1)}, f32[1024,768]{1,0:T(8...) custom-call(s32[3]{0:T(128)S(1)} %pad_add_fusion.bits, ...), custom_call_target="tpu_custom_call" | custom-call | flops 32212254720 | bytes 157286400 | tf_op jit(solution)/shard_map/pallas_call | solution.py:228
  153.5 7.0 %shard_map.185 = (bf16[2,2,2,2,96,768]{5,4,3,2,1,0:T(8,128)(2,1)S(1)}, bf16[2,2,2,2,96,768]{5,4,3,2,1,0:T(8,128)(2,1)S(1)}) custom-call(s32[3]{0:T(128)S(1)} %pad_add_fusion.bits, bf16[768,1024]{1,0:T(8,128)(2,1)S(1)} %get-tuple-element.186.dt, bf16[4,1024,512]{2,1,0:T(8,128)(2,1)S(1)} %copy-done.54, bf16[4,1024,256]{2,1,0:T(8,128)(2,1)S(1)} %get-tuple-element.188.actq), custom_call_target="tpu_custom_call" | custom-call | flops 48318382080 | bytes 110100480 | tf_op jit(solution)/shard_map/pallas_call | solution.py:272
  163.0 10.2 %shard_map.186 = (bf16[2,2,2,2,96,768]{5,4,3,2,1,0:T(8,128)(2,1)S(1)}, f32[1024,768]{1,0:T(8,128)S(1)}) custom-call(s32[3]{0:T(128)S(1)} %pad_add_fusion.bits, bf16[768,1024]{1,0:T(8,128)(2,1)S(1)} %copy-done.25, bf16[1024,768]{1,0:T(8,128)(2,1)S(1)} %copy-done.56, bf16[2,2,2,2,96,512]{5,4,3,2,1,0:T(8,128)(2,1)S(1)} %collective-permute-done.26.ua1.uap, ...), custom_call_target="tpu_custom_call" | custom-call | flops 72477573120 | bytes 235929600 | tf_op jit(solution)/shard_map/pallas_call | solution.py:381
  173.3 3.6 %fusion = bf16[2,2,2,96,768]{4,3,2,1,0:T(8,128)(2,1)} fusion(bf16[2,2,2,2,96,768]{5,4,3,2,1,0:T(8,128)(2,1)} %collective-permute-done.32, bf16[2,2,2,2,96,768]{5,4,3,2,1,0:T(8,128)(2,1)S(1)} %get-tuple-element.219), kind=kLoop, calls=%fused_computation.6 | loop fusion | flops 2359296 | bytes 3538944 | tf_op jit(solution)/shard_map/convert_element_type | solution.py:815
  177.5 15.8 %shard_map.187 = (bf16[2,2,2,2,96,768]{5,4,3,2,1,0:T(8,128)(2,1)S(1)}, f32[1024,768]{1,0:T(8,128)}, bf16[1024,768]{1,0:T(8,128)(2,1)S(1)}, bf16[768,1024]{1,0:T(...) custom-call(s32[3]{0:T(128)S(1)} %pad_add_fusion.bits, bf16[768,1024]{1,0:T(8,128)(2,1)S(1)} %copy-done.25, ...), custom_call_target="tpu_custom_call" | custom-call | flops 72477573120 | bytes 235929600 | tf_op jit(solution)/shard_map/pallas_call | solution.py:381
  199.3 14.4 %shard_map.188 = (bf16[2,1024,384]{2,1,0:T(8,128)(2,1)S(1)}, bf16[2,1024,192]{2,1,0:T(8,128)(2,1)S(1)}, bf16[2,2,2,2,3,32,512]{6,5,4,3,2,1,0:T(8,128)(2,1)S(1)}, bf16[2,2,2,2,3,32,512]{6,5,4,3,2,1,0:T(8,128)(2,1)S(1)}) custom-call(s32[3]{0:T(128)S(1)} %pad_add_fusion.bits, s32[2]{0:T(128)S(1)} %copy-done.18, bf16[2,1024,384]{2,1,0:T(8,128)(2,1)S(1)} %copy-done.35, ...), custom_call_target="tpu_custom_call" | custom-call | flops 80530636800 | bytes 58982400 | tf_op jit(solution)/shard_map/pallas_call | solution.py:576
  216.0 5.0 %shard_map.189 = (bf16[2,2,2,2,96,384]{5,4,3,2,1,0:T(8,128)(2,1)S(1)}, bf16[2,2,2,2,96,384]{5,4,3,2,1,0:T(8,128)(2,1)S(1)}) custom-call(s32[3]{0:T(128)S(1)} %pad_add_fusion.bits, bf16[768,1024]{1,0:T(8,128)(2,1)S(1)} %copy-done.4, bf16[768,1024]{1,0:T(8,128)(2,1)S(1)} %get-tuple-element.212.dat, bf16[2,1024,384]{2,1,0:T(8,128)(2,1)S(1)} %get-tuple-element.222.dqk.dqk1, ...), custom_call_target="tpu_custom_call" | custom-call | flops 24159191040 | bytes 62914560 | tf_op jit(solution)/shard_map/pallas_call | solution.py:715
  232.2 14.8 %shard_map.190 = (bf16[2,1024,384]{2,1,0:T(8,128)(2,1)S(1)}, bf16[2,1024,192]{2,1,0:T(8,128)(2,1)S(1)}, bf16[2,2,2,3,32,512]{5,4,3,2,1,0:T(8,128)(2,1)S(1)}, bf1...) custom-call(s32[3]{0:T(128)S(1)} %pad_add_fusion.bits, ...), custom_call_target="tpu_custom_call" | custom-call | flops 80530636800 | bytes 58982400 | tf_op jit(solution)/shard_map/pallas_call | solution.py:576
  257.2 4.9 %shard_map.191 = (bf16[2,2,2,96,384]{4,3,2,1,0:T(8,128)(2,1)S(1)}, bf16[2,2,2,96,384]{4,3,2,1,0:T(8,128)(2,1)S(1)}, bf16[2,2,2,96,384]{4,3,2,1,0:T(8,128)(2,1)S(1)}, bf16[2,2,2,96,384]{4,3,2,1,0:T(8,128)(2,1)S(1)}) custom-call(s32[3]{0:T(128)S(1)} %pad_add_fusion.bits, bf16[768,1024]{1,0:T(8,128)(2,1)S(1)} %copy-done.4, ...), custom_call_target="tpu_custom_call" | custom-call | flops 10 | bytes 10 | tf_op jit(solution)/shard_map/pallas_call | solution.py:715
  264.1 4.4 %collective-permute-done.47 = bf16[2,2,96,768]{3,2,1,0:T(8,128)(2,1)S(1)} collective-permute-done((bf16[2,2,96,768]{3,2,1,0:T(8,128)(2,1)S(1)}, bf16[2,2,96,768]{3,2,1,0:T(8,128)(2,1)S(1)}, u32[]{:S(2)}, u32[]{:S(2)}) %collective-permute-start.47) | collective-permute-done | bytes 589856 | tf_op jit(solution)/shard_map/ppermute | solution.py:759
  269.1 3.8 %collective-permute-done.49 = bf16[2,2,2,3,32,512]{5,4,3,2,1,0:T(8,128)(2,1)S(1)} collective-permute-done((bf16[2,2,2,3,32,512]{5,4,3,2,1,0:T(8,128)(2,1)S(1)}, bf16[2,2,2,3,32,512]{5,4,3,2,1,0:T(8,128)(2,1)S(1)}, u32[]{:S(2)}, u32[]{:S(2)}) %collective-permute-start.49) | collective-permute-done | bytes 786464 | tf_op jit(solution)/shard_map/ppermute | solution.py:759
  277.4 7.0 %shard_map.192 = f32[1024,768]{1,0:T(8,128)} custom-call(f32[1024,768]{1,0:T(8,128)S(1)} %copy-done.47, bf16[2,1024,384]{2,1,0:T(8,128)(2,1)S(1)} %get-tuple-element.258.dqk.dqk0, bf16[2,1024,384]{2,1,0:T(8,128)(2,1)S(1)} %copy-done.46, bf16[2,1024,192]{2,1,0:T(8,128)(2,1)S(1)} %get-tuple-element.245.dv.dv0, bf16[2,1024,192]{2,1,0:T(8,128)(2,1)S(1)} %copy-done.53, ...), custom_call_target="tpu_custom_call" | custom-call | flops 36238786560 | bytes 110100480 | tf_op jit(solution)/shard_map/pallas_call | solution.py:741
  288.0 3.0 collective-permute-done.52
  300.9 6.5 %collective-permute-done.59 = bf16[2,2,3,32,512]{4,3,2,1,0:T(8,128)(2,1)S(1)} collective-permute-done((bf16[2,2,3,32,512]{4,3,2,1,0:T(8,128)(2,1)S(1)}, bf16[2,2,3,32,512]{4,3,2,1,0:T(8,128)(2,1)S(1)}, u32[]{:S(2)}, u32[]{:S(2)}) %collective-permute-start.59) | collective-permute-done | bytes 393248 | tf_op jit(solution)/shard_map/ppermute | solution.py:759
  308.7 3.5 %collective-permute-done.57 = bf16[2,2,96,384]{3,2,1,0:T(8,128)(2,1)S(1)} collective-permute-done((bf16[2,2,96,384]{3,2,1,0:T(8,128)(2,1)S(1)}, bf16[2,2,96,384]{3,2,1,0:T(8,128)(2,1)S(1)}, u32[]{:S(2)}, u32[]{:S(2)}) %collective-permute-start.57) | collective-permute-done | bytes 294944 | tf_op jit(solution)/shard_map/ppermute | solution.py:759
  314.1 3.0 collective-permute-done.60
  (331 shorter events, 104.3 us)
Async XLA Ops:
  25.0 11.6 %collective-permute-start.4 = (bf16[2,3,32,512]{3,2,1,0:T(8,128)(2,1)S(1)}, bf16[2,3,32,512]{3,2,1,0:T(8,128)(2,1)S(1)}, u32[]{:S(2)}, u32[]{:S(2)}) collective-permute-start(bf16[2,3,32,512]{3,2,1,0:T(8,128)(2,1)S(1)} %pad_maximum_fusion.28), channel_id=1, source_target_pairs={{0,16},{4,20},{8,24},{12,28},{16,0},{20,4},{24,8},{28,12},{1,17},{... | collective-permute-start | bytes 589832 | tf_op jit(solution)/shard_map/ppermute | solution.py:759
  36.7 15.2 %collective-permute-start.6 = (bf16[2,2,2,96,384]{4,3,2,1,0:T(8,128)(2,1)S(1)}, bf16[2,2,2,96,384]{4,3,2,1,0:T(8,128)(2,1)S(1)}, u32[]{:S(2)}, u32[]{:S(2)}) collective-permute-start(bf16[2,2,2,96,384]{4,3,2,1,0:T(8,128)(2,1)S(1)} %pad_maximum_fusion.12), channel_id=1, source_target_pairs={{0,2},{1,3},{2,0},{3,1},{4,6},{5,7},{6,4},{7,5},{8,10},{9,11},{10,... | collective-permute-start | bytes 1769480 | tf_op jit(solution)/shard_map/ppermute | solution.py:764
  37.3 14.6 %collective-permute-start.7 = (bf16[2,2,2,96,384]{4,3,2,1,0:T(8,128)(2,1)S(1)}, bf16[2,2,2,96,384]{4,3,2,1,0:T(8,128)(2,1)S(1)}, u32[]{:S(2)}, u32[]{:S(2)}) collective-permute-start(bf16[2,2,2,96,384]{4,3,2,1,0:T(8,128)(2,1)S(1)} %pad_maximum_fusion.13), channel_id=1, source_target_pairs={{0,4},{4,0},{8,12},{12,8},{16,20},{20,16},{24,28},{28,24},{1,5},{5... | collective-permute-start | bytes 1769480 | tf_op jit(solution)/shard_map/ppermute | solution.py:759
  47.5 15.3 %collective-permute-start.12 = (bf16[2,96,512]{2,1,0:T(8,128)(2,1)S(1)}, bf16[2,96,512]{2,1,0:T(8,128)(2,1)S(1)}, u32[]{:S(2)}, u32[]{:S(2)}) collective-permute-start(bf16[2,96,512]{2,1,0:T(8,128)(2,1)S(1)} %pad_maximum_fusion.29), channel_id=1, source_target_pairs={{0,16},{4,20},{8,24},{12,28},{16,0},{20,4},{24,8},{28,12},{1,17},{... | collective-permute-start | bytes 589832 | tf_op jit(solution)/shard_map/ppermute | solution.py:759
  64.4 18.5 %collective-permute-start.14 = (bf16[2,2,2,3,32,512]{5,4,3,2,1,0:T(8,128)(2,1)S(1)}, bf16[2,2,2,3,32,512]{5,4,3,2,1,0:T(8,128)(2,1)S(1)}, u32[]{:S(2)}, u32[]{:S(2)}) collective-permute-start(bf16[2,2,2,3,32,512]{5,4,3,2,1,0:T(8,128)(2,1)S(1)} %pad_maximum_fusion.6), channel_id=1, source_target_pairs={{0,2},{1,3},{2,0},{3,1},{4,6},{5,7},{6,4},{7,5},{8,10},{9,11},{10,... | collective-permute-start | bytes 2359304 | tf_op jit(solution)/shard_map/ppermute | solution.py:764
  65.8 17.3 %collective-permute-start.15 = (bf16[2,2,2,3,32,512]{5,4,3,2,1,0:T(8,128)(2,1)S(1)}, bf16[2,2,2,3,32,512]{5,4,3,2,1,0:T(8,128)(2,1)S(1)}, u32[]{:S(2)}, u32[]{:S(2)}) collective-permute-start(bf16[2,2,2,3,32,512]{5,4,3,2,1,0:T(8,128)(2,1)S(1)} %pad_maximum_fusion.7), channel_id=1, source_target_pairs={{0,4},{4,0},{8,12},{12,8},{16,20},{20,16},{24,28},{28,24},{1,5},{5... | collective-permute-start | bytes 2359304 | tf_op jit(solution)/shard_map/ppermute | solution.py:759
  83.3 11.9 %collective-permute-start.18 = (bf16[2,96,256]{2,1,0:T(8,128)(2,1)S(1)}, bf16[2,96,256]{2,1,0:T(8,128)(2,1)S(1)}, u32[]{:S(2)}, u32[]{:S(2)}) collective-permute-start(bf16[2,96,256]{2,1,0:T(8,128)(2,1)S(1)} %pad_maximum_fusion.34), channel_id=1, source_target_pairs={{0,16},{4,20},{8,24},{12,28},{16,0},{20,4},{24,8},{28,12},{1,17},{... | collective-permute-start | bytes 294920 | tf_op jit(solution)/shard_map/ppermute | solution.py:759
  96.1 14.1 %collective-permute-start.23 = (bf16[2,2,96,256]{3,2,1,0:T(8,128)(2,1)S(1)}, bf16[2,2,96,256]{3,2,1,0:T(8,128)(2,1)S(1)}, u32[]{:S(2)}, u32[]{:S(2)}) collective-permute-start(bf16[2,2,96,256]{3,2,1,0:T(8,128)(2,1)S(1)} %pad_maximum_fusion.30), channel_id=1, source_target_pairs={{0,8},{4,12},{8,0},{12,4},{16,24},{20,28},{24,16},{28,20},{1,9},{5... | collective-permute-start | bytes 589832 | tf_op jit(solution)/shard_map/ppermute | solution.py:759
  96.5 19.2 %collective-permute-start.21 = (bf16[2,2,2,96,512]{4,3,2,1,0:T(8,128)(2,1)S(1)}, bf16[2,2,2,96,512]{4,3,2,1,0:T(8,128)(2,1)S(1)}, u32[]{:S(2)}, u32[]{:S(2)}) collective-permute-start(bf16[2,2,2,96,512]{4,3,2,1,0:T(8,128)(2,1)S(1)} %pad_maximum_fusion.8), channel_id=1, source_target_pairs={{0,2},{1,3},{2,0},{3,1},{4,6},{5,7},{6,4},{7,5},{8,10},{9,11},{10,... | collective-permute-start | bytes 2359304 | tf_op jit(solution)/shard_map/ppermute | solution.py:764
  97.1 18.9 %collective-permute-start.22 = (bf16[2,2,2,96,512]{4,3,2,1,0:T(8,128)(2,1)S(1)}, bf16[2,2,2,96,512]{4,3,2,1,0:T(8,128)(2,1)S(1)}, u32[]{:S(2)}, u32[]{:S(2)}) collective-permute-start(bf16[2,2,2,96,512]{4,3,2,1,0:T(8,128)(2,1)S(1)} %pad_maximum_fusion.9), channel_id=1, source_target_pairs={{0,4},{4,0},{8,12},{12,8},{16,20},{20,16},{24,28},{28,24},{1,5},{5... | collective-permute-start | bytes 2359304 | tf_op jit(solution)/shard_map/ppermute | solution.py:759
  123.9 14.1 %collective-permute-start.28 = (bf16[2,2,2,96,256]{4,3,2,1,0:T(8,128)(2,1)S(1)}, bf16[2,2,2,96,256]{4,3,2,1,0:T(8,128)(2,1)S(1)}, u32[]{:S(2)}, u32[]{:S(2)}) collective-permute-start(bf16[2,2,2,96,256]{4,3,2,1,0:T(8,128)(2,1)S(1)} %pad_maximum_fusion.19), channel_id=1, source_target_pairs={{0,2},{1,3},{2,0},{3,1},{4,6},{5,7},{6,4},{7,5},{8,10},{9,11},{10,... | collective-permute-start | bytes 1179656 | tf_op jit(solution)/shard_map/ppermute | solution.py:764
  125.4 12.6 %collective-permute-start.29 = (bf16[2,2,2,96,256]{4,3,2,1,0:T(8,128)(2,1)S(1)}, bf16[2,2,2,96,256]{4,3,2,1,0:T(8,128)(2,1)S(1)}, u32[]{:S(2)}, u32[]{:S(2)}) collective-permute-start(bf16[2,2,2,96,256]{4,3,2,1,0:T(8,128)(2,1)S(1)} %pad_maximum_fusion.20), channel_id=1, source_target_pairs={{0,4},{4,0},{8,12},{12,8},{16,20},{20,16},{24,28},{28,24},{1,5},{5... | collective-permute-start | bytes 1179656 | tf_op jit(solution)/shard_map/ppermute | solution.py:759
  160.6 12.7 %collective-permute-start.32 = (bf16[2,2,2,2,96,768]{5,4,3,2,1,0:T(8,128)(2,1)S(1)}, bf16[2,2,2,2,96,768]{5,4,3,2,1,0:T(8,128)(2,1)}, u32[]{:S(2)}, u32[]{:S(2)}) collective-permute-start(bf16[2,2,2,2,96,768]{5,4,3,2,1,0:T(8,128)(2,1)S(1)} %get-tuple-element.190), channel_id=1, source_target_pairs={{0,1},{1,0},{2,3},{3,2},{4,5},{5,4},{6,7},{7,6},{8,9},{9,8},{10,11... | collective-permute-start | bytes 7077896 | tf_op jit(solution)/shard_map/ppermute | solution.py:764
  177.0 36.8 %collective-permute-start.35 = (bf16[2,2,2,96,768]{4,3,2,1,0:T(8,128)(2,1)}, bf16[2,2,2,96,768]{4,3,2,1,0:T(8,128)(2,1)}, u32[]{:S(2)}, u32[]{:S(2)}) collective-permute-start(bf16[2,2,2,96,768]{4,3,2,1,0:T(8,128)(2,1)} %fusion), channel_id=1, source_target_pairs={{0,4},{4,0},{8,12},{12,8},{16,20},{20,16},{24,28},{28,24},{1,5},{5... | collective-permute-start | bytes 3538952 | tf_op jit(solution)/shard_map/ppermute | solution.py:759
  177.5 15.9 %collective-permute-start.33 = (bf16[2,2,2,2,96,768]{5,4,3,2,1,0:T(8,128)(2,1)S(1)}, bf16[2,2,2,2,96,768]{5,4,3,2,1,0:T(8,128)(2,1)S(1)}, u32[]{:S(2)}, u32[]{:S(2)}) collective-permute-start(bf16[2,2,2,2,96,768]{5,4,3,2,1,0:T(8,128)(2,1)S(1)} %get-tuple-element.203), channel_id=1, source_target_pairs={{0,1},{1,0},{2,3},{3,2},{4,5},{5,4},{6,7},{7,6},{8,9},{9,8},{10,11... | collective-permute-start | bytes 7077896 | tf_op jit(solution)/shard_map/ppermute | solution.py:764
  193.4 20.3 %collective-permute-start.34 = (f32[4,768]{1,0:T(4,128)S(1)}, f32[4,768]{1,0:T(4,128)S(1)}, u32[]{:S(2)}, u32[]{:S(2)}) collective-permute-start(f32[4,768]{1,0:T(4,128)S(1)} %pad_maximum_fusion.35), channel_id=1, source_target_pairs={{0,1},{1,0},{2,3},{3,2},{4,5},{5,4},{6,7},{7,6},{8,9},{9,8},{10,11... | collective-permute-start | bytes 36872 | tf_op jit(solution)/shard_map/ppermute | solution.py:847
  194.4 28.4 %collective-permute-start.39 = (bf16[2,2,2,96,768]{4,3,2,1,0:T(8,128)(2,1)S(1)}, bf16[2,2,2,96,768]{4,3,2,1,0:T(8,128)(2,1)S(1)}, u32[]{:S(2)}, u32[]{:S(2)}) collective-permute-start(bf16[2,2,2,96,768]{4,3,2,1,0:T(8,128)(2,1)S(1)} %fusion.1), channel_id=1, source_target_pairs={{0,2},{1,3},{2,0},{3,1},{4,6},{5,7},{6,4},{7,5},{8,10},{9,11},{10,... | collective-permute-start | bytes 3538952 | tf_op jit(solution)/shard_map/ppermute | solution.py:764
  227.1 19.9 %collective-permute-start.42 = (bf16[2,2,2,2,96,384]{5,4,3,2,1,0:T(8,128)(2,1)S(1)}, bf16[2,2,2,2,96,384]{5,4,3,2,1,0:T(8,128)(2,1)S(1)}, u32[]{:S(2)}, u32[]{:S(2)}) collective-permute-start(bf16[2,2,2,2,96,384]{5,4,3,2,1,0:T(8,128)(2,1)S(1)} %get-tuple-element.241), channel_id=1, source_target_pairs={{0,1},{1,0},{2,3},{3,2},{4,5},{5,4},{6,7},{7,6},{8,9},{9,8},{10,11... | collective-permute-start | bytes 3538952 | tf_op jit(solution)/shard_map/ppermute | solution.py:764
  227.1 19.9 %collective-permute-start.43 = (bf16[2,2,2,2,96,384]{5,4,3,2,1,0:T(8,128)(2,1)S(1)}, bf16[2,2,2,2,96,384]{5,4,3,2,1,0:T(8,128)(2,1)S(1)}, u32[]{:S(2)}, u32[]{:S(2)}) collective-permute-start(bf16[2,2,2,2,96,384]{5,4,3,2,1,0:T(8,128)(2,1)S(1)} %get-tuple-element.242), channel_id=1, source_target_pairs={{0,1},{1,0},{2,3},{3,2},{4,5},{5,4},{6,7},{7,6},{8,9},{9,8},{10,11... | collective-permute-start | bytes 3538952 | tf_op jit(solution)/shard_map/ppermute | solution.py:764
  227.9 19.1 %collective-permute-start.41 = (f32[4,768]{1,0:T(4,128)S(1)}, f32[4,768]{1,0:T(4,128)S(1)}, u32[]{:S(2)}, u32[]{:S(2)}) collective-permute-start(f32[4,768]{1,0:T(4,128)S(1)} %add.275), channel_id=1, source_target_pairs={{0,16},{4,20},{8,24},{12,28},{16,0},{20,4},{24,8},{28,12},{1,17},{... | collective-permute-start | bytes 36872 | tf_op jit(solution)/shard_map/ppermute | solution.py:847
  229.2 17.7 %collective-permute-start.44 = (bf16[2,2,96,768]{3,2,1,0:T(8,128)(2,1)}, bf16[2,2,96,768]{3,2,1,0:T(8,128)(2,1)S(1)}, u32[]{:S(2)}, u32[]{:S(2)}) collective-permute-start(bf16[2,2,96,768]{3,2,1,0:T(8,128)(2,1)} %fusion.4), channel_id=1, source_target_pairs={{0,2},{1,3},{2,0},{3,1},{4,6},{5,7},{6,4},{7,5},{8,10},{9,11},{10,... | collective-permute-start | bytes 1769480 | tf_op jit(solution)/shard_map/ppermute | solution.py:764
  230.4 16.6 %collective-permute-start.45 = (bf16[2,2,96,768]{3,2,1,0:T(8,128)(2,1)S(1)}, bf16[2,2,96,768]{3,2,1,0:T(8,128)(2,1)S(1)}, u32[]{:S(2)}, u32[]{:S(2)}) collective-permute-start(bf16[2,2,96,768]{3,2,1,0:T(8,128)(2,1)S(1)} %fusion.3), channel_id=1, source_target_pairs={{0,4},{4,0},{8,12},{12,8},{16,20},{20,16},{24,28},{28,24},{1,5},{5... | collective-permute-start | bytes 1769480 | tf_op jit(solution)/shard_map/ppermute | solution.py:759
  248.6 20.5 %collective-permute-start.48 = (bf16[2,2,2,3,32,512]{5,4,3,2,1,0:T(8,128)(2,1)S(1)}, bf16[2,2,2,3,32,512]{5,4,3,2,1,0:T(8,128)(2,1)S(1)}, u32[]{:S(2)}, u32[]{:S(2)}) collective-permute-start(bf16[2,2,2,3,32,512]{5,4,3,2,1,0:T(8,128)(2,1)S(1)} %get-tuple-element.252), channel_id=1, source_target_pairs={{0,2},{1,3},{2,0},{3,1},{4,6},{5,7},{6,4},{7,5},{8,10},{9,11},{10,... | collective-permute-start | bytes 2359304 | tf_op jit(solution)/shard_map/ppermute | solution.py:764
  252.3 20.5 %collective-permute-start.49 = (bf16[2,2,2,3,32,512]{5,4,3,2,1,0:T(8,128)(2,1)S(1)}, bf16[2,2,2,3,32,512]{5,4,3,2,1,0:T(8,128)(2,1)S(1)}, u32[]{:S(2)}, u32[]{:S(2)}) collective-permute-start(bf16[2,2,2,3,32,512]{5,4,3,2,1,0:T(8,128)(2,1)S(1)} %get-tuple-element.253), channel_id=1, source_target_pairs={{0,4},{4,0},{8,12},{12,8},{16,20},{20,16},{24,28},{28,24},{1,5},{5... | collective-permute-start | bytes 2359304 | tf_op jit(solution)/shard_map/ppermute | solution.py:759
  255.4 13.0 %collective-permute-start.47 = (bf16[2,2,96,768]{3,2,1,0:T(8,128)(2,1)S(1)}, bf16[2,2,96,768]{3,2,1,0:T(8,128)(2,1)S(1)}, u32[]{:S(2)}, u32[]{:S(2)}) collective-permute-start(bf16[2,2,96,768]{3,2,1,0:T(8,128)(2,1)S(1)} %pad_maximum_fusion.14), channel_id=1, source_target_pairs={{0,8},{4,12},{8,0},{12,4},{16,24},{20,28},{24,16},{28,20},{1,9},{5... | collective-permute-start | bytes 1769480 | tf_op jit(solution)/shard_map/ppermute | solution.py:759
  262.1 22.4 %collective-permute-start.50 = (bf16[2,2,2,96,384]{4,3,2,1,0:T(8,128)(2,1)S(1)}, bf16[2,2,2,96,384]{4,3,2,1,0:T(8,128)(2,1)S(1)}, u32[]{:S(2)}, u32[]{:S(2)}) collective-permute-start(bf16[2,2,2,96,384]{4,3,2,1,0:T(8,128)(2,1)S(1)} %get-tuple-element.264), channel_id=1, source_target_pairs={{0,2},{1,3},{2,0},{3,1},{4,6},{5,7},{6,4},{7,5},{8,10},{9,11},{10,... | collective-permute-start | bytes 1769480 | tf_op jit(solution)/shard_map/ppermute | solution.py:764
  263.0 22.5 %collective-permute-start.51 = (bf16[2,2,2,96,384]{4,3,2,1,0:T(8,128)(2,1)S(1)}, bf16[2,2,2,96,384]{4,3,2,1,0:T(8,128)(2,1)S(1)}, u32[]{:S(2)}, u32[]{:S(2)}) collective-permute-start(bf16[2,2,2,96,384]{4,3,2,1,0:T(8,128)(2,1)S(1)} %get-tuple-element.265), channel_id=1, source_target_pairs={{0,4},{4,0},{8,12},{12,8},{16,20},{20,16},{24,28},{28,24},{1,5},{5... | collective-permute-start | bytes 1769480 | tf_op jit(solution)/shard_map/ppermute | solution.py:759
  273.0 12.5 %collective-permute-start.54 = (bf16[2,96,768]{2,1,0:T(8,128)(2,1)S(1)}, bf16[2,96,768]{2,1,0:T(8,128)(2,1)S(1)}, u32[]{:S(2)}, u32[]{:S(2)}) collective-permute-start(bf16[2,96,768]{2,1,0:T(8,128)(2,1)S(1)} %pad_maximum_fusion.24), channel_id=1, source_target_pairs={{0,16},{4,20},{8,24},{12,28},{16,0},{20,4},{24,8},{28,12},{1,17},{... | collective-permute-start | bytes 884744 | tf_op jit(solution)/shard_map/ppermute | solution.py:759
  275.8 12.2 %collective-permute-start.53 = (bf16[2,2,3,32,512]{4,3,2,1,0:T(8,128)(2,1)S(1)}, bf16[2,2,3,32,512]{4,3,2,1,0:T(8,128)(2,1)S(1)}, u32[]{:S(2)}, u32[]{:S(2)}) collective-permute-start(bf16[2,2,3,32,512]{4,3,2,1,0:T(8,128)(2,1)S(1)} %fusion.7), channel_id=1, source_target_pairs={{0,2},{1,3},{2,0},{3,1},{4,6},{5,7},{6,4},{7,5},{8,10},{9,11},{10,... | collective-permute-start | bytes 1179656 | tf_op jit(solution)/shard_map/ppermute | solution.py:764
  276.8 14.2 %collective-permute-start.52 = (bf16[2,2,3,32,512]{4,3,2,1,0:T(8,128)(2,1)S(1)}, bf16[2,2,3,32,512]{4,3,2,1,0:T(8,128)(2,1)S(1)}, u32[]{:S(2)}, u32[]{:S(2)}) collective-permute-start(bf16[2,2,3,32,512]{4,3,2,1,0:T(8,128)(2,1)S(1)} %fusion.6), channel_id=1, source_target_pairs={{0,4},{4,0},{8,12},{12,8},{16,20},{20,16},{24,28},{28,24},{1,5},{5... | collective-permute-start | bytes 1179656 | tf_op jit(solution)/shard_map/ppermute | solution.py:759
  294.7 12.7 %collective-permute-start.59 = (bf16[2,2,3,32,512]{4,3,2,1,0:T(8,128)(2,1)S(1)}, bf16[2,2,3,32,512]{4,3,2,1,0:T(8,128)(2,1)S(1)}, u32[]{:S(2)}, u32[]{:S(2)}) collective-permute-start(bf16[2,2,3,32,512]{4,3,2,1,0:T(8,128)(2,1)S(1)} %pad_maximum_fusion.21), channel_id=1, source_target_pairs={{0,8},{4,12},{8,0},{12,4},{16,24},{20,28},{24,16},{28,20},{1,9},{5... | collective-permute-start | bytes 1179656 | tf_op jit(solution)/shard_map/ppermute | solution.py:759
  299.2 13.0 %collective-permute-start.57 = (bf16[2,2,96,384]{3,2,1,0:T(8,128)(2,1)S(1)}, bf16[2,2,96,384]{3,2,1,0:T(8,128)(2,1)S(1)}, u32[]{:S(2)}, u32[]{:S(2)}) collective-permute-start(bf16[2,2,96,384]{3,2,1,0:T(8,128)(2,1)S(1)} %pad_maximum_fusion.25), channel_id=1, source_target_pairs={{0,8},{4,12},{8,0},{12,4},{16,24},{20,28},{24,16},{28,20},{1,9},{5... | collective-permute-start | bytes 884744 | tf_op jit(solution)/shard_map/ppermute | solution.py:759
  (101 other events, 1158.9 us)

commit v6 on v5

--- a/solution.py
+++ b/solution.py
@@ -746,7 +746,7 @@
         + [whole((2, width, w2))] * 2 + [whole((2, width, w1))] * 2,
         out_specs=row,
         compiler_params=params(24),
-        cost_estimate=cost(2 * rows * width * 4 * (w1 + w2), 14 * rows * width),
+        cost_estimate=cost(1, 1),
     )(dfirst, dqk0, dqk1, dv0, dv1, wqk0, wqk1, wv0, wv1)
 
 

time: 325 us -> 324 us (level)
  local copies, waits for them, and re-layouts: 16.4 us -> 11 us
    unnamed x146 -> x140, local copies, waits for them, and re-layouts: 14.3 us -> 8.99 us
where the time goes in v6:
time: 324 us; the launch traced here: 322 us
  Pallas kernels  131 us (40%)
  waiting for transfers between devices  92.4 us (29%)
  starting transfers between devices  65.9 us (20%)
  other arithmetic  19.2 us (6%)
  local copies, waits for them, and re-layouts  11 us (3%)
    ppermute x28, waiting for transfers between devices, partner_dp(): return lax.ppermute(value, 'dp', [(i, i ^ step) for i in range(size)])  64 us
    ppermute x28, starting transfers between devices, partner_dp(): return lax.ppermute(value, 'dp', [(i, i ^ step) for i in range(size)])  40.1 us
    pallas_call x2, Pallas kernels, attention_backward(): pl.pallas_call(functools.partial(att_bwd_kernel, last), out_shape=out_sha...  29.5 us
    ppermute x28, waiting for transfers between devices, partner_head(): return lax.ppermute(value, 'head', [(i, i ^ 1 << bit) for i in range(size)])  26.7 us
    pallas_call x2, Pallas kernels, ffn_backward(): pl.pallas_call(functools.partial(ffn_bwd_kernel, chunk, last), out_shape=...  26.6 us
    ppermute x28, starting transfers between devices, partner_head(): return lax.ppermute(value, 'head', [(i, i ^ 1 << bit) for i in range(size)])  20.1 us
    pallas_call x2, Pallas kernels, attention_forward(): pl.pallas_call(att_fwd_kernel, out_shape=(sds((2, rows, w1), BF16), sds((...  13.3 us
    pallas_call x1, Pallas kernels, ffn_part(): pl.pallas_call(functools.partial(ffn_part_kernel, chunk), out_shape=(pltp...  11 us
  transfers between devices with their start and end apart: 61, of which 31 were waited for; matrix products, arithmetic and copies ran while one was open for 4% of the time, Pallas kernels for 35%

profile of v6, /device:TPU:0, one launch (start us, length us, event | category | flops | bytes accessed | tf_op | source)
XLA Modules:
  0.0 321.7 jit_solution(965303876583786909)
XLA Ops:
  2.6 4.1 %collective-permute-start = (bf16[2,96,384]{2,1,0:T(8,128)(2,1)S(1)}, bf16[2,96,384]{2,1,0:T(8,128)(2,1)S(1)}, u32[]{:S(2)}, u32[]{:S(2)}) collective-permute-start(bf16[2,96,384]{2,1,0:T(8,128)(2,1)S(1)} %get-tuple-element.319), channel_id=1, source_target_pairs={{0,16},{4,20},{8,24},{12,28},{16,0},{20,4},{24,8},{28,12},{1,17},{... | collective-permute-start | bytes 442376 | tf_op jit(solution)/shard_map/ppermute | solution.py:759
  8.0 5.8 %collective-permute-done = bf16[2,96,384]{2,1,0:T(8,128)(2,1)S(1)} collective-permute-done((bf16[2,96,384]{2,1,0:T(8,128)(2,1)S(1)}, bf16[2,96,384]{2,1,0:T(8,128)(2,1)S(1)}, u32[]{:S(2)}, u32[]{:S(2)}) %collective-permute-start) | collective-permute-done | bytes 147488 | tf_op jit(solution)/shard_map/ppermute | solution.py:759
  14.6 7.4 %collective-permute-done.1 = bf16[2,2,96,384]{3,2,1,0:T(8,128)(2,1)S(1)} collective-permute-done((bf16[2,2,96,384]{3,2,1,0:T(8,128)(2,1)S(1)}, bf16[2,2,96,384]{3,2,1,0:T(8,128)(2,1)S(1)}, u32[]{:S(2)}, u32[]{:S(2)}) %collective-permute-start.1) | collective-permute-done | bytes 294944 | tf_op jit(solution)/shard_map/ppermute | solution.py:759
  25.0 3.4 %collective-permute-start.4 = (bf16[2,3,32,512]{3,2,1,0:T(8,128)(2,1)S(1)}, bf16[2,3,32,512]{3,2,1,0:T(8,128)(2,1)S(1)}, u32[]{:S(2)}, u32[]{:S(2)}) collective-permute-start(bf16[2,3,32,512]{3,2,1,0:T(8,128)(2,1)S(1)} %pad_maximum_fusion.28), channel_id=1, source_target_pairs={{0,16},{4,20},{8,24},{12,28},{16,0},{20,4},{24,8},{28,12},{1,17},{... | collective-permute-start | bytes 589832 | tf_op jit(solution)/shard_map/ppermute | solution.py:759
  30.7 6.0 %collective-permute-done.4 = bf16[2,3,32,512]{3,2,1,0:T(8,128)(2,1)S(1)} collective-permute-done((bf16[2,3,32,512]{3,2,1,0:T(8,128)(2,1)S(1)}, bf16[2,3,32,512]{3,2,1,0:T(8,128)(2,1)S(1)}, u32[]{:S(2)}, u32[]{:S(2)}) %collective-permute-start.4) | collective-permute-done | bytes 196640 | tf_op jit(solution)/shard_map/ppermute | solution.py:759
  38.9 8.6 %collective-permute-done.5 = bf16[2,2,3,32,512]{4,3,2,1,0:T(8,128)(2,1)} collective-permute-done((bf16[2,2,3,32,512]{4,3,2,1,0:T(8,128)(2,1)S(1)}, bf16[2,2,3,32,512]{4,3,2,1,0:T(8,128)(2,1)}, u32[]{:S(2)}, u32[]{:S(2)}) %collective-permute-start.5) | collective-permute-done | bytes 393248 | tf_op jit(solution)/shard_map/ppermute | solution.py:759
  47.5 3.2 collective-permute-start.12
  56.5 5.7 %shard_map.178 = (bf16[2,1024,384]{2,1,0:T(8,128)(2,1)S(1)}, bf16[2,1024,192]{2,1,0:T(8,128)(2,1)S(1)}, bf16[2,768,384]{2,1,0:T(8,128)(2,1)}, bf16[2,768,192]{2,...) custom-call(s32[3]{0:T(128)S(1)} %pad_add_fusion.bits, bf16[1024,768]{1,0:T(8,128)(2,1)S(1)} %bitcast.221, ...), custom_call_target="tpu_custom_call" | custom-call | flops 18119393280 | bytes 62914560 | tf_op jit(solution)/shard_map/pallas_call | solution.py:616
  66.4 4.5 %shard_map.179 = (bf16[2,1024,384]{2,1,0:T(8,128)(2,1)S(1)}, bf16[2,1024,192]{2,1,0:T(8,128)(2,1)S(1)}, bf16[2,768,384]{2,1,0:T(8,128)(2,1)}, bf16[2,768,192]{2,1,0:T(8,128)(2,1)}, bf16[2,768,192]{2,1,0:T(8,128)(2,1)S(1)}) custom-call(s32[3]{0:T(128)S(1)} %pad_add_fusion.bits, bf16[1024,768]{1,0:T(8,128)(2,1)S(1)} %bitcast.222, ...), custom_call_target="tpu_custom_call" | custom-call | flops 18119393280 | bytes 62914560 | tf_op jit(solution)/shard_map/pallas_call | solution.py:616
  73.0 9.8 %collective-permute-done.14 = bf16[2,2,2,3,32,512]{5,4,3,2,1,0:T(8,128)(2,1)S(1)} collective-permute-done((bf16[2,2,2,3,32,512]{5,4,3,2,1,0:T(8,128)(2,1)S(1)}, bf16[2,2,2,3,32,512]{5,4,3,2,1,0:T(8,128)(2,1)S(1)}, u32[]{:S(2)}, u32[]{:S(2)}) %collective-permute-start.14) | collective-permute-done | bytes 786464 | tf_op jit(solution)/shard_map/ppermute | solution.py:764
  88.5 6.6 %shard_map.180 = (bf16[2,1024,192]{2,1,0:T(8,128)(2,1)S(1)}, f32[2,1024,3]{2,1,0:T(8,128)S(1)}) custom-call(s32[3]{0:T(128)S(1)} %pad_add_fusion.bits, s32[2]{0:T(128)S(1)} %dynamic-slice_reduce_fusion.lens, bf16[2,1024,384]{2,1,0:T(8,128)(2,1)S(1)} %get-tuple-element.150.qk, bf16[2,1024,192]{2,1,0:T(8,128)(2,1)S(1)} %get-tuple-element.162.v, ...), custom_call_target="tpu_custom_call" | custom-call | flops 32212254720 | bytes 31457280 | tf_op jit(solution)/shard_map/pallas_call | solution.py:443
  97.6 6.6 %shard_map.181 = (bf16[2,1024,192]{2,1,0:T(8,128)(2,1)S(1)}, f32[2,1024,3]{2,1,0:T(8,128)S(1)}) custom-call(s32[3]{0:T(128)S(1)} %pad_add_fusion.bits, s32[2]{0:T(128)S(1)} %dynamic-slice_reduce_fusion.lens, bf16[2,1024,384]{2,1,0:T(8,128)(2,1)S(1)} %get-tuple-element.156.qk, bf16[2,1024,192]{2,1,0:T(8,128)(2,1)S(1)} %get-tuple-element.167.v, ...), custom_call_target="tpu_custom_call" | custom-call | flops 32212254720 | bytes 31457280 | tf_op jit(solution)/shard_map/pallas_call | solution.py:443
  105.3 4.9 %shard_map.182 = (bf16[1024,768]{1,0:T(8,128)(2,1)S(1)}, f32[1024,768]{1,0:T(8,128)}, f32[1024,1]{1,0:T(8,128)S(1)}, bf16[768,1024]{1,0:T(8,128)(2,1)}) custom-call(bf16[1024,768]{1,0:T(8,128)(2,1)S(1)} %bitcast.223, bf16[2,1024,192]{2,1,0:T(8,128)(2,1)S(1)} %get-tuple-element.163.m0.mixed, bf16[2,1024,192]{2,1,0:T(8,128)(2,1)S(1)} %get-tuple-element.170.m1.mixed, ...), custom_call_target="tpu_custom_call" | custom-call | flops 12079595520 | bytes 94371840 | tf_op jit(solution)/shard_map/pallas_call | solution.py:649
  110.3 5.5 %collective-permute-done.21 = bf16[2,2,2,96,512]{4,3,2,1,0:T(8,128)(2,1)S(1)} collective-permute-done((bf16[2,2,2,96,512]{4,3,2,1,0:T(8,128)(2,1)S(1)}, bf16[2,2,2,96,512]{4,3,2,1,0:T(8,128)(2,1)S(1)}, u32[]{:S(2)}, u32[]{:S(2)}) %collective-permute-start.21) | collective-permute-done | bytes 786464 | tf_op jit(solution)/shard_map/ppermute | solution.py:764
  118.8 4.9 %collective-permute-done.24 = bf16[2,2,96,256]{3,2,1,0:T(8,128)(2,1)S(1)} collective-permute-done((bf16[2,2,96,256]{3,2,1,0:T(8,128)(2,1)S(1)}, bf16[2,2,96,256]{3,2,1,0:T(8,128)(2,1)S(1)}, u32[]{:S(2)}, u32[]{:S(2)}) %collective-permute-start.24) | collective-permute-done | bytes 196640 | tf_op jit(solution)/shard_map/ppermute | solution.py:759
  127.0 11.0 %shard_map.183 = (bf16[4,1024,512]{2,1,0:T(8,128)(2,1)}, bf16[4,1024,512]{2,1,0:T(8,128)(2,1)}, f32[1024,768]{1,0:T(8,128)S(1)}) custom-call(s32[3]{0:T(128)S(1)} %pad_add_fusion.bits, bf16[1024,768]{1,0:T(8,128)(2,1)S(1)} %get-tuple-element.178.hid, bf16[2,2,2,2,96,512]{5,4,3,2,1,0:T(8,128)(2,1)S(1)} %pad_maximum_fusion.2.ua0.uap, ...), custom_call_target="tpu_custom_call" | custom-call | flops 64424509440 | bytes 125829120 | tf_op jit(solution)/shard_map/pallas_call | solution.py:162
  141.7 10.7 %shard_map.184 = (bf16[4,1024,256]{2,1,0:T(8,128)(2,1)S(1)}, bf16[4,1024,256]{2,1,0:T(8,128)(2,1)S(1)}, bf16[1024,768]{1,0:T(8,128)(2,1)}, f32[1024,768]{1,0:T(8...) custom-call(s32[3]{0:T(128)S(1)} %pad_add_fusion.bits, ...), custom_call_target="tpu_custom_call" | custom-call | flops 32212254720 | bytes 157286400 | tf_op jit(solution)/shard_map/pallas_call | solution.py:228
  153.5 7.0 %shard_map.185 = (bf16[2,2,2,2,96,768]{5,4,3,2,1,0:T(8,128)(2,1)S(1)}, bf16[2,2,2,2,96,768]{5,4,3,2,1,0:T(8,128)(2,1)S(1)}) custom-call(s32[3]{0:T(128)S(1)} %pad_add_fusion.bits, bf16[768,1024]{1,0:T(8,128)(2,1)S(1)} %get-tuple-element.186.dt, bf16[4,1024,512]{2,1,0:T(8,128)(2,1)S(1)} %copy-done.51, bf16[4,1024,256]{2,1,0:T(8,128)(2,1)S(1)} %get-tuple-element.188.actq), custom_call_target="tpu_custom_call" | custom-call | flops 48318382080 | bytes 110100480 | tf_op jit(solution)/shard_map/pallas_call | solution.py:272
  163.0 10.5 %shard_map.186 = (bf16[2,2,2,2,96,768]{5,4,3,2,1,0:T(8,128)(2,1)S(1)}, f32[1024,768]{1,0:T(8,128)S(1)}) custom-call(s32[3]{0:T(128)S(1)} %pad_add_fusion.bits, bf16[768,1024]{1,0:T(8,128)(2,1)S(1)} %copy-done.30, bf16[1024,768]{1,0:T(8,128)(2,1)S(1)} %copy-done.53, bf16[2,2,2,2,96,512]{5,4,3,2,1,0:T(8,128)(2,1)S(1)} %collective-permute-done.26.ua1.uap, ...), custom_call_target="tpu_custom_call" | custom-call | flops 72477573120 | bytes 235929600 | tf_op jit(solution)/shard_map/pallas_call | solution.py:381
  173.6 3.6 %fusion = bf16[2,2,2,96,768]{4,3,2,1,0:T(8,128)(2,1)} fusion(bf16[2,2,2,2,96,768]{5,4,3,2,1,0:T(8,128)(2,1)} %collective-permute-done.32, bf16[2,2,2,2,96,768]{5,4,3,2,1,0:T(8,128)(2,1)S(1)} %get-tuple-element.219), kind=kLoop, calls=%fused_computation.6 | loop fusion | flops 2359296 | bytes 3538944 | tf_op jit(solution)/shard_map/convert_element_type | solution.py:815
  177.9 16.1 %shard_map.187 = (bf16[2,2,2,2,96,768]{5,4,3,2,1,0:T(8,128)(2,1)S(1)}, f32[1024,768]{1,0:T(8,128)}, bf16[1024,768]{1,0:T(8,128)(2,1)S(1)}, bf16[768,1024]{1,0:T(...) custom-call(s32[3]{0:T(128)S(1)} %pad_add_fusion.bits, bf16[768,1024]{1,0:T(8,128)(2,1)S(1)} %copy-done.30, ...), custom_call_target="tpu_custom_call" | custom-call | flops 72477573120 | bytes 235929600 | tf_op jit(solution)/shard_map/pallas_call | solution.py:381
  197.7 14.5 %shard_map.188 = (bf16[2,1024,384]{2,1,0:T(8,128)(2,1)S(1)}, bf16[2,1024,192]{2,1,0:T(8,128)(2,1)S(1)}, bf16[2,2,2,2,3,32,512]{6,5,4,3,2,1,0:T(8,128)(2,1)S(1)}, bf16[2,2,2,2,3,32,512]{6,5,4,3,2,1,0:T(8,128)(2,1)S(1)}) custom-call(s32[3]{0:T(128)S(1)} %pad_add_fusion.bits, s32[2]{0:T(128)S(1)} %copy-done.23, bf16[2,1024,384]{2,1,0:T(8,128)(2,1)S(1)} %copy-done.40, ...), custom_call_target="tpu_custom_call" | custom-call | flops 80530636800 | bytes 58982400 | tf_op jit(solution)/shard_map/pallas_call | solution.py:576
  214.5 5.7 %shard_map.189 = (bf16[2,2,2,2,96,384]{5,4,3,2,1,0:T(8,128)(2,1)}, bf16[2,2,2,2,96,384]{5,4,3,2,1,0:T(8,128)(2,1)S(1)}) custom-call(s32[3]{0:T(128)S(1)} %pad_add_fusion.bits, bf16[768,1024]{1,0:T(8,128)(2,1)S(1)} %copy-done.5, bf16[768,1024]{1,0:T(8,128)(2,1)S(1)} %get-tuple-element.212.dat, bf16[2,1024,384]{2,1,0:T(8,128)(2,1)S(1)} %get-tuple-element.222.dqk.dqk1, ...), custom_call_target="tpu_custom_call" | custom-call | flops 24159191040 | bytes 62914560 | tf_op jit(solution)/shard_map/pallas_call | solution.py:715
  220.2 3.8 %collective-permute-done.39 = bf16[2,2,2,96,768]{4,3,2,1,0:T(8,128)(2,1)} collective-permute-done((bf16[2,2,2,96,768]{4,3,2,1,0:T(8,128)(2,1)}, bf16[2,2,2,96,768]{4,3,2,1,0:T(8,128)(2,1)}, u32[]{:S(2)}, u32[]{:S(2)}) %collective-permute-start.39) | collective-permute-done | bytes 1179680 | tf_op jit(solution)/shard_map/ppermute | solution.py:764
  231.6 15.0 %shard_map.190 = (bf16[2,1024,384]{2,1,0:T(8,128)(2,1)S(1)}, bf16[2,1024,192]{2,1,0:T(8,128)(2,1)S(1)}, bf16[2,2,2,3,32,512]{5,4,3,2,1,0:T(8,128)(2,1)S(1)}, bf1...) custom-call(s32[3]{0:T(128)S(1)} %pad_add_fusion.bits, ...), custom_call_target="tpu_custom_call" | custom-call | flops 80530636800 | bytes 58982400 | tf_op jit(solution)/shard_map/pallas_call | solution.py:576
  256.9 4.9 %shard_map.191 = (bf16[2,2,2,96,384]{4,3,2,1,0:T(8,128)(2,1)S(1)}, bf16[2,2,2,96,384]{4,3,2,1,0:T(8,128)(2,1)S(1)}, bf16[2,2,2,96,384]{4,3,2,1,0:T(8,128)(2,1)S(1)}, bf16[2,2,2,96,384]{4,3,2,1,0:T(8,128)(2,1)S(1)}) custom-call(s32[3]{0:T(128)S(1)} %pad_add_fusion.bits, bf16[768,1024]{1,0:T(8,128)(2,1)S(1)} %copy-done.5, ...), custom_call_target="tpu_custom_call" | custom-call | flops 10 | bytes 10 | tf_op jit(solution)/shard_map/pallas_call | solution.py:715
  263.9 4.3 %collective-permute-done.47 = bf16[2,2,96,768]{3,2,1,0:T(8,128)(2,1)S(1)} collective-permute-done((bf16[2,2,96,768]{3,2,1,0:T(8,128)(2,1)S(1)}, bf16[2,2,96,768]{3,2,1,0:T(8,128)(2,1)S(1)}, u32[]{:S(2)}, u32[]{:S(2)}) %collective-permute-start.47) | collective-permute-done | bytes 589856 | tf_op jit(solution)/shard_map/ppermute | solution.py:759
  268.7 3.8 %collective-permute-done.49 = bf16[2,2,2,3,32,512]{5,4,3,2,1,0:T(8,128)(2,1)S(1)} collective-permute-done((bf16[2,2,2,3,32,512]{5,4,3,2,1,0:T(8,128)(2,1)S(1)}, bf16[2,2,2,3,32,512]{5,4,3,2,1,0:T(8,128)(2,1)S(1)}, u32[]{:S(2)}, u32[]{:S(2)}) %collective-permute-start.49) | collective-permute-done | bytes 786464 | tf_op jit(solution)/shard_map/ppermute | solution.py:759
  278.3 7.1 %shard_map.192 = f32[1024,768]{1,0:T(8,128)} custom-call(f32[1024,768]{1,0:T(8,128)S(1)} %copy-done.2, bf16[2,1024,384]{2,1,0:T(8,128)(2,1)S(1)} %get-tuple-element.258.dqk.dqk0, bf16[2,1024,384]{2,1,0:T(8,128)(2,1)S(1)} %get-tuple-element.222.dqk.dqk1, bf16[2,1024,192]{2,1,0:T(8,128)(2,1)S(1)} %get-tuple-element.245.dv.dv0, ...), custom_call_target="tpu_custom_call" | custom-call | flops 10 | bytes 10 | tf_op jit(solution)/shard_map/pallas_call | solution.py:741
  287.6 3.0 collective-permute-done.52
  300.5 6.3 %collective-permute-done.59 = bf16[2,2,3,32,512]{4,3,2,1,0:T(8,128)(2,1)S(1)} collective-permute-done((bf16[2,2,3,32,512]{4,3,2,1,0:T(8,128)(2,1)S(1)}, bf16[2,2,3,32,512]{4,3,2,1,0:T(8,128)(2,1)S(1)}, u32[]{:S(2)}, u32[]{:S(2)}) %collective-permute-start.59) | collective-permute-done | bytes 393248 | tf_op jit(solution)/shard_map/ppermute | solution.py:759
  308.1 3.6 %collective-permute-done.57 = bf16[2,2,96,384]{3,2,1,0:T(8,128)(2,1)S(1)} collective-permute-done((bf16[2,2,96,384]{3,2,1,0:T(8,128)(2,1)S(1)}, bf16[2,2,96,384]{3,2,1,0:T(8,128)(2,1)S(1)}, u32[]{:S(2)}, u32[]{:S(2)}) %collective-permute-start.57) | collective-permute-done | bytes 294944 | tf_op jit(solution)/shard_map/ppermute | solution.py:759
  (325 shorter events, 101.4 us)
Async XLA Ops:
  2.6 11.1 %collective-permute-start = (bf16[2,96,384]{2,1,0:T(8,128)(2,1)S(1)}, bf16[2,96,384]{2,1,0:T(8,128)(2,1)S(1)}, u32[]{:S(2)}, u32[]{:S(2)}) collective-permute-start(bf16[2,96,384]{2,1,0:T(8,128)(2,1)S(1)} %get-tuple-element.319), channel_id=1, source_target_pairs={{0,16},{4,20},{8,24},{12,28},{16,0},{20,4},{24,8},{28,12},{1,17},{... | collective-permute-start | bytes 442376 | tf_op jit(solution)/shard_map/ppermute | solution.py:759
  25.0 11.6 %collective-permute-start.4 = (bf16[2,3,32,512]{3,2,1,0:T(8,128)(2,1)S(1)}, bf16[2,3,32,512]{3,2,1,0:T(8,128)(2,1)S(1)}, u32[]{:S(2)}, u32[]{:S(2)}) collective-permute-start(bf16[2,3,32,512]{3,2,1,0:T(8,128)(2,1)S(1)} %pad_maximum_fusion.28), channel_id=1, source_target_pairs={{0,16},{4,20},{8,24},{12,28},{16,0},{20,4},{24,8},{28,12},{1,17},{... | collective-permute-start | bytes 589832 | tf_op jit(solution)/shard_map/ppermute | solution.py:759
  36.7 15.2 %collective-permute-start.6 = (bf16[2,2,2,96,384]{4,3,2,1,0:T(8,128)(2,1)S(1)}, bf16[2,2,2,96,384]{4,3,2,1,0:T(8,128)(2,1)S(1)}, u32[]{:S(2)}, u32[]{:S(2)}) collective-permute-start(bf16[2,2,2,96,384]{4,3,2,1,0:T(8,128)(2,1)S(1)} %pad_maximum_fusion.12), channel_id=1, source_target_pairs={{0,2},{1,3},{2,0},{3,1},{4,6},{5,7},{6,4},{7,5},{8,10},{9,11},{10,... | collective-permute-start | bytes 1769480 | tf_op jit(solution)/shard_map/ppermute | solution.py:764
  37.3 14.6 %collective-permute-start.7 = (bf16[2,2,2,96,384]{4,3,2,1,0:T(8,128)(2,1)S(1)}, bf16[2,2,2,96,384]{4,3,2,1,0:T(8,128)(2,1)S(1)}, u32[]{:S(2)}, u32[]{:S(2)}) collective-permute-start(bf16[2,2,2,96,384]{4,3,2,1,0:T(8,128)(2,1)S(1)} %pad_maximum_fusion.13), channel_id=1, source_target_pairs={{0,4},{4,0},{8,12},{12,8},{16,20},{20,16},{24,28},{28,24},{1,5},{5... | collective-permute-start | bytes 1769480 | tf_op jit(solution)/shard_map/ppermute | solution.py:759
  47.5 15.3 %collective-permute-start.12 = (bf16[2,96,512]{2,1,0:T(8,128)(2,1)S(1)}, bf16[2,96,512]{2,1,0:T(8,128)(2,1)S(1)}, u32[]{:S(2)}, u32[]{:S(2)}) collective-permute-start(bf16[2,96,512]{2,1,0:T(8,128)(2,1)S(1)} %pad_maximum_fusion.29), channel_id=1, source_target_pairs={{0,16},{4,20},{8,24},{12,28},{16,0},{20,4},{24,8},{28,12},{1,17},{... | collective-permute-start | bytes 589832 | tf_op jit(solution)/shard_map/ppermute | solution.py:759
  64.4 18.5 %collective-permute-start.14 = (bf16[2,2,2,3,32,512]{5,4,3,2,1,0:T(8,128)(2,1)S(1)}, bf16[2,2,2,3,32,512]{5,4,3,2,1,0:T(8,128)(2,1)S(1)}, u32[]{:S(2)}, u32[]{:S(2)}) collective-permute-start(bf16[2,2,2,3,32,512]{5,4,3,2,1,0:T(8,128)(2,1)S(1)} %pad_maximum_fusion.6), channel_id=1, source_target_pairs={{0,2},{1,3},{2,0},{3,1},{4,6},{5,7},{6,4},{7,5},{8,10},{9,11},{10,... | collective-permute-start | bytes 2359304 | tf_op jit(solution)/shard_map/ppermute | solution.py:764
  65.8 17.3 %collective-permute-start.15 = (bf16[2,2,2,3,32,512]{5,4,3,2,1,0:T(8,128)(2,1)S(1)}, bf16[2,2,2,3,32,512]{5,4,3,2,1,0:T(8,128)(2,1)S(1)}, u32[]{:S(2)}, u32[]{:S(2)}) collective-permute-start(bf16[2,2,2,3,32,512]{5,4,3,2,1,0:T(8,128)(2,1)S(1)} %pad_maximum_fusion.7), channel_id=1, source_target_pairs={{0,4},{4,0},{8,12},{12,8},{16,20},{20,16},{24,28},{28,24},{1,5},{5... | collective-permute-start | bytes 2359304 | tf_op jit(solution)/shard_map/ppermute | solution.py:759
  83.3 11.9 %collective-permute-start.18 = (bf16[2,96,256]{2,1,0:T(8,128)(2,1)S(1)}, bf16[2,96,256]{2,1,0:T(8,128)(2,1)S(1)}, u32[]{:S(2)}, u32[]{:S(2)}) collective-permute-start(bf16[2,96,256]{2,1,0:T(8,128)(2,1)S(1)} %pad_maximum_fusion.34), channel_id=1, source_target_pairs={{0,16},{4,20},{8,24},{12,28},{16,0},{20,4},{24,8},{28,12},{1,17},{... | collective-permute-start | bytes 294920 | tf_op jit(solution)/shard_map/ppermute | solution.py:759
  96.2 14.1 %collective-permute-start.23 = (bf16[2,2,96,256]{3,2,1,0:T(8,128)(2,1)S(1)}, bf16[2,2,96,256]{3,2,1,0:T(8,128)(2,1)S(1)}, u32[]{:S(2)}, u32[]{:S(2)}) collective-permute-start(bf16[2,2,96,256]{3,2,1,0:T(8,128)(2,1)S(1)} %pad_maximum_fusion.30), channel_id=1, source_target_pairs={{0,8},{4,12},{8,0},{12,4},{16,24},{20,28},{24,16},{28,20},{1,9},{5... | collective-permute-start | bytes 589832 | tf_op jit(solution)/shard_map/ppermute | solution.py:759
  96.6 19.2 %collective-permute-start.21 = (bf16[2,2,2,96,512]{4,3,2,1,0:T(8,128)(2,1)S(1)}, bf16[2,2,2,96,512]{4,3,2,1,0:T(8,128)(2,1)S(1)}, u32[]{:S(2)}, u32[]{:S(2)}) collective-permute-start(bf16[2,2,2,96,512]{4,3,2,1,0:T(8,128)(2,1)S(1)} %pad_maximum_fusion.8), channel_id=1, source_target_pairs={{0,2},{1,3},{2,0},{3,1},{4,6},{5,7},{6,4},{7,5},{8,10},{9,11},{10,... | collective-permute-start | bytes 2359304 | tf_op jit(solution)/shard_map/ppermute | solution.py:764
  97.1 18.9 %collective-permute-start.22 = (bf16[2,2,2,96,512]{4,3,2,1,0:T(8,128)(2,1)S(1)}, bf16[2,2,2,96,512]{4,3,2,1,0:T(8,128)(2,1)S(1)}, u32[]{:S(2)}, u32[]{:S(2)}) collective-permute-start(bf16[2,2,2,96,512]{4,3,2,1,0:T(8,128)(2,1)S(1)} %pad_maximum_fusion.9), channel_id=1, source_target_pairs={{0,4},{4,0},{8,12},{12,8},{16,20},{20,16},{24,28},{28,24},{1,5},{5... | collective-permute-start | bytes 2359304 | tf_op jit(solution)/shard_map/ppermute | solution.py:759
  123.9 14.1 %collective-permute-start.28 = (bf16[2,2,2,96,256]{4,3,2,1,0:T(8,128)(2,1)S(1)}, bf16[2,2,2,96,256]{4,3,2,1,0:T(8,128)(2,1)S(1)}, u32[]{:S(2)}, u32[]{:S(2)}) collective-permute-start(bf16[2,2,2,96,256]{4,3,2,1,0:T(8,128)(2,1)S(1)} %pad_maximum_fusion.19), channel_id=1, source_target_pairs={{0,2},{1,3},{2,0},{3,1},{4,6},{5,7},{6,4},{7,5},{8,10},{9,11},{10,... | collective-permute-start | bytes 1179656 | tf_op jit(solution)/shard_map/ppermute | solution.py:764
  125.5 12.6 %collective-permute-start.29 = (bf16[2,2,2,96,256]{4,3,2,1,0:T(8,128)(2,1)S(1)}, bf16[2,2,2,96,256]{4,3,2,1,0:T(8,128)(2,1)S(1)}, u32[]{:S(2)}, u32[]{:S(2)}) collective-permute-start(bf16[2,2,2,96,256]{4,3,2,1,0:T(8,128)(2,1)S(1)} %pad_maximum_fusion.20), channel_id=1, source_target_pairs={{0,4},{4,0},{8,12},{12,8},{16,20},{20,16},{24,28},{28,24},{1,5},{5... | collective-permute-start | bytes 1179656 | tf_op jit(solution)/shard_map/ppermute | solution.py:759
  160.6 13.0 %collective-permute-start.32 = (bf16[2,2,2,2,96,768]{5,4,3,2,1,0:T(8,128)(2,1)S(1)}, bf16[2,2,2,2,96,768]{5,4,3,2,1,0:T(8,128)(2,1)}, u32[]{:S(2)}, u32[]{:S(2)}) collective-permute-start(bf16[2,2,2,2,96,768]{5,4,3,2,1,0:T(8,128)(2,1)S(1)} %get-tuple-element.190), channel_id=1, source_target_pairs={{0,1},{1,0},{2,3},{3,2},{4,5},{5,4},{6,7},{7,6},{8,9},{9,8},{10,11... | collective-permute-start | bytes 7077896 | tf_op jit(solution)/shard_map/ppermute | solution.py:764
  177.3 35.0 %collective-permute-start.35 = (bf16[2,2,2,96,768]{4,3,2,1,0:T(8,128)(2,1)}, bf16[2,2,2,96,768]{4,3,2,1,0:T(8,128)(2,1)}, u32[]{:S(2)}, u32[]{:S(2)}) collective-permute-start(bf16[2,2,2,96,768]{4,3,2,1,0:T(8,128)(2,1)} %fusion), channel_id=1, source_target_pairs={{0,4},{4,0},{8,12},{12,8},{16,20},{20,16},{24,28},{28,24},{1,5},{5... | collective-permute-start | bytes 3538952 | tf_op jit(solution)/shard_map/ppermute | solution.py:759
  177.8 16.2 %collective-permute-start.33 = (bf16[2,2,2,2,96,768]{5,4,3,2,1,0:T(8,128)(2,1)S(1)}, bf16[2,2,2,2,96,768]{5,4,3,2,1,0:T(8,128)(2,1)S(1)}, u32[]{:S(2)}, u32[]{:S(2)}) collective-permute-start(bf16[2,2,2,2,96,768]{5,4,3,2,1,0:T(8,128)(2,1)S(1)} %get-tuple-element.203), channel_id=1, source_target_pairs={{0,1},{1,0},{2,3},{3,2},{4,5},{5,4},{6,7},{7,6},{8,9},{9,8},{10,11... | collective-permute-start | bytes 7077896 | tf_op jit(solution)/shard_map/ppermute | solution.py:764
  194.0 18.2 %collective-permute-start.34 = (f32[4,768]{1,0:T(4,128)S(1)}, f32[4,768]{1,0:T(4,128)S(1)}, u32[]{:S(2)}, u32[]{:S(2)}) collective-permute-start(f32[4,768]{1,0:T(4,128)S(1)} %pad_maximum_fusion.35), channel_id=1, source_target_pairs={{0,1},{1,0},{2,3},{3,2},{4,5},{5,4},{6,7},{7,6},{8,9},{9,8},{10,11... | collective-permute-start | bytes 36872 | tf_op jit(solution)/shard_map/ppermute | solution.py:847
  195.9 28.2 %collective-permute-start.39 = (bf16[2,2,2,96,768]{4,3,2,1,0:T(8,128)(2,1)}, bf16[2,2,2,96,768]{4,3,2,1,0:T(8,128)(2,1)}, u32[]{:S(2)}, u32[]{:S(2)}) collective-permute-start(bf16[2,2,2,96,768]{4,3,2,1,0:T(8,128)(2,1)} %fusion.1), channel_id=1, source_target_pairs={{0,2},{1,3},{2,0},{3,1},{4,6},{5,7},{6,4},{7,5},{8,10},{9,11},{10,... | collective-permute-start | bytes 3538952 | tf_op jit(solution)/shard_map/ppermute | solution.py:764
  227.5 19.0 %collective-permute-start.42 = (bf16[2,2,2,2,96,384]{5,4,3,2,1,0:T(8,128)(2,1)}, bf16[2,2,2,2,96,384]{5,4,3,2,1,0:T(8,128)(2,1)S(1)}, u32[]{:S(2)}, u32[]{:S(2)}) collective-permute-start(bf16[2,2,2,2,96,384]{5,4,3,2,1,0:T(8,128)(2,1)} %get-tuple-element.241), channel_id=1, source_target_pairs={{0,1},{1,0},{2,3},{3,2},{4,5},{5,4},{6,7},{7,6},{8,9},{9,8},{10,11... | collective-permute-start | bytes 3538952 | tf_op jit(solution)/shard_map/ppermute | solution.py:764
  227.6 19.0 %collective-permute-start.43 = (bf16[2,2,2,2,96,384]{5,4,3,2,1,0:T(8,128)(2,1)S(1)}, bf16[2,2,2,2,96,384]{5,4,3,2,1,0:T(8,128)(2,1)S(1)}, u32[]{:S(2)}, u32[]{:S(2)}) collective-permute-start(bf16[2,2,2,2,96,384]{5,4,3,2,1,0:T(8,128)(2,1)S(1)} %get-tuple-element.242), channel_id=1, source_target_pairs={{0,1},{1,0},{2,3},{3,2},{4,5},{5,4},{6,7},{7,6},{8,9},{9,8},{10,11... | collective-permute-start | bytes 3538952 | tf_op jit(solution)/shard_map/ppermute | solution.py:764
  229.1 17.4 %collective-permute-start.41 = (f32[4,768]{1,0:T(4,128)S(1)}, f32[4,768]{1,0:T(4,128)S(1)}, u32[]{:S(2)}, u32[]{:S(2)}) collective-permute-start(f32[4,768]{1,0:T(4,128)S(1)} %add.275), channel_id=1, source_target_pairs={{0,16},{4,20},{8,24},{12,28},{16,0},{20,4},{24,8},{28,12},{1,17},{... | collective-permute-start | bytes 36872 | tf_op jit(solution)/shard_map/ppermute | solution.py:847
  230.5 16.1 %collective-permute-start.44 = (bf16[2,2,96,768]{3,2,1,0:T(8,128)(2,1)S(1)}, bf16[2,2,96,768]{3,2,1,0:T(8,128)(2,1)S(1)}, u32[]{:S(2)}, u32[]{:S(2)}) collective-permute-start(bf16[2,2,96,768]{3,2,1,0:T(8,128)(2,1)S(1)} %fusion.4), channel_id=1, source_target_pairs={{0,2},{1,3},{2,0},{3,1},{4,6},{5,7},{6,4},{7,5},{8,10},{9,11},{10,... | collective-permute-start | bytes 1769480 | tf_op jit(solution)/shard_map/ppermute | solution.py:764
  231.0 15.6 %collective-permute-start.45 = (bf16[2,2,96,768]{3,2,1,0:T(8,128)(2,1)S(1)}, bf16[2,2,96,768]{3,2,1,0:T(8,128)(2,1)S(1)}, u32[]{:S(2)}, u32[]{:S(2)}) collective-permute-start(bf16[2,2,96,768]{3,2,1,0:T(8,128)(2,1)S(1)} %fusion.3), channel_id=1, source_target_pairs={{0,4},{4,0},{8,12},{12,8},{16,20},{20,16},{24,28},{28,24},{1,5},{5... | collective-permute-start | bytes 1769480 | tf_op jit(solution)/shard_map/ppermute | solution.py:759
  248.2 20.5 %collective-permute-start.48 = (bf16[2,2,2,3,32,512]{5,4,3,2,1,0:T(8,128)(2,1)S(1)}, bf16[2,2,2,3,32,512]{5,4,3,2,1,0:T(8,128)(2,1)S(1)}, u32[]{:S(2)}, u32[]{:S(2)}) collective-permute-start(bf16[2,2,2,3,32,512]{5,4,3,2,1,0:T(8,128)(2,1)S(1)} %get-tuple-element.252), channel_id=1, source_target_pairs={{0,2},{1,3},{2,0},{3,1},{4,6},{5,7},{6,4},{7,5},{8,10},{9,11},{10,... | collective-permute-start | bytes 2359304 | tf_op jit(solution)/shard_map/ppermute | solution.py:764
  251.9 20.5 %collective-permute-start.49 = (bf16[2,2,2,3,32,512]{5,4,3,2,1,0:T(8,128)(2,1)S(1)}, bf16[2,2,2,3,32,512]{5,4,3,2,1,0:T(8,128)(2,1)S(1)}, u32[]{:S(2)}, u32[]{:S(2)}) collective-permute-start(bf16[2,2,2,3,32,512]{5,4,3,2,1,0:T(8,128)(2,1)S(1)} %get-tuple-element.253), channel_id=1, source_target_pairs={{0,4},{4,0},{8,12},{12,8},{16,20},{20,16},{24,28},{28,24},{1,5},{5... | collective-permute-start | bytes 2359304 | tf_op jit(solution)/shard_map/ppermute | solution.py:759
  255.2 13.0 %collective-permute-start.47 = (bf16[2,2,96,768]{3,2,1,0:T(8,128)(2,1)S(1)}, bf16[2,2,96,768]{3,2,1,0:T(8,128)(2,1)S(1)}, u32[]{:S(2)}, u32[]{:S(2)}) collective-permute-start(bf16[2,2,96,768]{3,2,1,0:T(8,128)(2,1)S(1)} %pad_maximum_fusion.14), channel_id=1, source_target_pairs={{0,8},{4,12},{8,0},{12,4},{16,24},{20,28},{24,16},{28,20},{1,9},{5... | collective-permute-start | bytes 1769480 | tf_op jit(solution)/shard_map/ppermute | solution.py:759
  261.8 23.6 %collective-permute-start.50 = (bf16[2,2,2,96,384]{4,3,2,1,0:T(8,128)(2,1)S(1)}, bf16[2,2,2,96,384]{4,3,2,1,0:T(8,128)(2,1)S(1)}, u32[]{:S(2)}, u32[]{:S(2)}) collective-permute-start(bf16[2,2,2,96,384]{4,3,2,1,0:T(8,128)(2,1)S(1)} %get-tuple-element.264), channel_id=1, source_target_pairs={{0,2},{1,3},{2,0},{3,1},{4,6},{5,7},{6,4},{7,5},{8,10},{9,11},{10,... | collective-permute-start | bytes 1769480 | tf_op jit(solution)/shard_map/ppermute | solution.py:764
  263.4 22.0 %collective-permute-start.51 = (bf16[2,2,2,96,384]{4,3,2,1,0:T(8,128)(2,1)S(1)}, bf16[2,2,2,96,384]{4,3,2,1,0:T(8,128)(2,1)S(1)}, u32[]{:S(2)}, u32[]{:S(2)}) collective-permute-start(bf16[2,2,2,96,384]{4,3,2,1,0:T(8,128)(2,1)S(1)} %get-tuple-element.265), channel_id=1, source_target_pairs={{0,4},{4,0},{8,12},{12,8},{16,20},{20,16},{24,28},{28,24},{1,5},{5... | collective-permute-start | bytes 1769480 | tf_op jit(solution)/shard_map/ppermute | solution.py:759
  272.6 15.0 %collective-permute-start.53 = (bf16[2,2,3,32,512]{4,3,2,1,0:T(8,128)(2,1)S(1)}, bf16[2,2,3,32,512]{4,3,2,1,0:T(8,128)(2,1)S(1)}, u32[]{:S(2)}, u32[]{:S(2)}) collective-permute-start(bf16[2,2,3,32,512]{4,3,2,1,0:T(8,128)(2,1)S(1)} %fusion.7), channel_id=1, source_target_pairs={{0,2},{1,3},{2,0},{3,1},{4,6},{5,7},{6,4},{7,5},{8,10},{9,11},{10,... | collective-permute-start | bytes 1179656 | tf_op jit(solution)/shard_map/ppermute | solution.py:764
  274.3 16.3 %collective-permute-start.52 = (bf16[2,2,3,32,512]{4,3,2,1,0:T(8,128)(2,1)S(1)}, bf16[2,2,3,32,512]{4,3,2,1,0:T(8,128)(2,1)S(1)}, u32[]{:S(2)}, u32[]{:S(2)}) collective-permute-start(bf16[2,2,3,32,512]{4,3,2,1,0:T(8,128)(2,1)S(1)} %fusion.6), channel_id=1, source_target_pairs={{0,4},{4,0},{8,12},{12,8},{16,20},{20,16},{24,28},{28,24},{1,5},{5... | collective-permute-start | bytes 1179656 | tf_op jit(solution)/shard_map/ppermute | solution.py:759
  294.3 12.5 %collective-permute-start.59 = (bf16[2,2,3,32,512]{4,3,2,1,0:T(8,128)(2,1)S(1)}, bf16[2,2,3,32,512]{4,3,2,1,0:T(8,128)(2,1)S(1)}, u32[]{:S(2)}, u32[]{:S(2)}) collective-permute-start(bf16[2,2,3,32,512]{4,3,2,1,0:T(8,128)(2,1)S(1)} %pad_maximum_fusion.21), channel_id=1, source_target_pairs={{0,8},{4,12},{8,0},{12,4},{16,24},{20,28},{24,16},{28,20},{1,9},{5... | collective-permute-start | bytes 1179656 | tf_op jit(solution)/shard_map/ppermute | solution.py:759
  298.8 12.9 %collective-permute-start.57 = (bf16[2,2,96,384]{3,2,1,0:T(8,128)(2,1)S(1)}, bf16[2,2,96,384]{3,2,1,0:T(8,128)(2,1)S(1)}, u32[]{:S(2)}, u32[]{:S(2)}) collective-permute-start(bf16[2,2,96,384]{3,2,1,0:T(8,128)(2,1)S(1)} %pad_maximum_fusion.25), channel_id=1, source_target_pairs={{0,8},{4,12},{8,0},{12,4},{16,24},{20,28},{24,16},{28,20},{1,9},{5... | collective-permute-start | bytes 884744 | tf_op jit(solution)/shard_map/ppermute | solution.py:759
  (98 other events, 1241.9 us)
